TPU v7x, 32 devices: a whole 2x2x4 slice. The times are simulated.
32 devices in a mesh: dp: 4 (over x, core), seq: 8 (over z, y).
Axes of the slice: x: 2, y: 2, z: 4, core: 2. Of those that a mesh axis runs over, the one named last changes fastest.
Arguments:
- tokens: bfloat16 [8, 1024, 1024], P('dp', 'seq'), may hold values from -6 to 6
- attn_gain: bfloat16 [1024], P(('dp', 'seq')), may hold values from 0.25 to 1.75
- w_query: bfloat16 [1024, 2048], P(('dp', 'seq')), may hold values from -0.1875 to 0.1875
- key_projection: bfloat16 [1024, 1024], P(('dp', 'seq')), may hold values from -0.1875 to 0.1875
- value_projection: bfloat16 [1024, 1024], P(('dp', 'seq')), may hold values from -0.1875 to 0.1875
- query_head_gain: bfloat16 [128], replicated, may hold values from 1.3984375 to 2.59375
- key_gain: bfloat16 [128], replicated, may hold values from 0.25 to 1.75
- w_out: bfloat16 [2048, 1024], P(('dp', 'seq')), may hold values from -0.75 to 0.75
- mlp_gain: bfloat16 [1024], P(('dp', 'seq')), may hold values from 0.25 to 1.75
- w_gate: bfloat16 [1024, 3072], P(('dp', 'seq')), may hold values from -0.1875 to 0.1875
- w_up: bfloat16 [1024, 3072], P(('dp', 'seq')), may hold values from -0.1875 to 0.1875
- w_down: bfloat16 [3072, 1024], P(('dp', 'seq')), may hold values from -0.21875 to 0.21875
- cotangent: bfloat16 [8, 1024, 1024], P('dp', 'seq'), may hold values from -6 to 6
- span_order: int32 [8, 16], P('dp'), may hold values from 0 to 15, each once within a row
Outputs:
- output: bfloat16 [8, 1024, 1024], P('dp', 'seq')
- input_grad: bfloat16 [8, 1024, 1024], P('dp', 'seq')
- grad_attn_gain: float32 [1024], P(('dp', 'seq'))
- grad_query: float32 [1024, 2048], P(('dp', 'seq'))
- grad_key: float32 [1024, 1024], P(('dp', 'seq'))
- grad_value: float32 [1024, 1024], P(('dp', 'seq'))
- grad_query_gain: float32 [128], replicated
- grad_key_gain: float32 [128], replicated
- grad_out: float32 [2048, 1024], P(('dp', 'seq'))
- grad_mlp_gain: float32 [1024], P(('dp', 'seq'))
- grad_gate: float32 [1024, 3072], P(('dp', 'seq'))
- grad_up: float32 [1024, 3072], P(('dp', 'seq'))
- grad_down: float32 [3072, 1024], P(('dp', 'seq'))
Inputs may be any that keep to these rules, and one draw needn't show every extreme that they name: Each row is a permutation of the numbers 0 to 15: stored block b of sequence s holds its tokens span_order[s, b] * 64 to span_order[s, b] * 64 + 63.
All inputs are finite; a program needn't handle non-finite values.
Results may differ from a plain program's by a relative error of at most 0.02.
Values may be sent and summed in bfloat16 or wider, within the bound.
A program may use at most 192 MiB of HBM per device.

v0:
```python
import jax
import jax.numpy as jnp
from jax import lax
from jax.sharding import PartitionSpec as P

QUERY_HEADS = 16
KEY_VALUE_HEADS = 8
HEAD_SIZE = 128
BLK = 64
MB = 2


EPS = 1e-06
BASE = 1000000.0
NEGATIVE_FILL = -1e30


def from_behind(block, axis, distance):
    devices = range(lax.axis_size(axis))
    route = [((i - distance) % len(devices), i) for i in devices]
    return lax.ppermute(block, axis, route)


def row_norm_apply(v, gain):
    return v * lax.rsqrt(jnp.mean(v * v, axis=-1, keepdims=True) + EPS) * gain


def apply_rotary(v, cosine_table, sine_table):
    half = v.shape[-1] // 2
    first = v[..., :half]
    second = v[..., half:]
    return jnp.concatenate(
        [first * cosine_table - second * sine_table, second * cosine_table + first * sine_table],
        axis=-1,
    )


def matrix_multiply(left, right):
    return jnp.dot(left, right, preferred_element_type=jnp.float32)


def row_product(left, right):
    return lax.dot_general(
        left, right, (((0,), (0,)), ((), ())), preferred_element_type=jnp.float32
    )


def product_backward(left, right):
    return lax.dot_general(
        left, right, (((1,), (1,)), ((), ())), preferred_element_type=jnp.float32
    )


def block_positions(order, start, count):
    places = start + lax.iota(jnp.int32, count)
    which = places // BLK
    hits = (which[:, None] == lax.iota(jnp.int32, order.shape[1])[None, :]).astype(jnp.int32)
    spans = jnp.sum(hits[None, :, :] * order[:, None, :], axis=-1)
    return spans * BLK + places % BLK


def pack_shares(members, count):
    return jnp.concatenate([m.reshape(count, -1) for m in members], axis=1).reshape(-1)


def unpack_shares(flat, members, count):
    pieces = []
    offset = 0
    for m in members:
        length = m.size // count
        share_shape = (m.shape[0] // count,) + tuple(m.shape[1:])
        pieces.append(flat[offset : offset + length].reshape(share_shape))
        offset = offset + length
    return pieces


def shards(
    tokens,
    attn_gain,
    w_query,
    key_projection,
    value_projection,
    query_head_gain,
    key_gain,
    w_out,
    mlp_gain,
    w_gate,
    w_up,
    w_down,
    cotangent,
    span_order,
):
    seq_count = lax.axis_size("seq")
    seq_place = lax.axis_index("seq")
    all_count = lax.axis_size(("dp", "seq"))
    local_length = tokens.shape[1]
    width = tokens.shape[2]
    sequence_permutation = tokens.shape[0] // MB
    query_group = QUERY_HEADS // KEY_VALUE_HEADS
    scale = HEAD_SIZE ** (-0.5)
    freqs = BASE ** (-(lax.iota(jnp.float32, HEAD_SIZE // 2) * 2.0) / HEAD_SIZE)
    query_norm_gain = query_head_gain.astype(jnp.float32)
    kgain = key_gain.astype(jnp.float32)
    sums = None
    outputs = []
    input_grads = []
    for batch in range(MB):
        rows_x = tokens[batch * sequence_permutation : (batch + 1) * sequence_permutation]
        rows_cot = cotangent[batch * sequence_permutation : (batch + 1) * sequence_permutation]
        order = span_order[batch * sequence_permutation : (batch + 1) * sequence_permutation]
        gain_a, wq, key_weight, value_weight, output_weight = (
            lax.all_gather(attn_gain, ("dp", "seq"), axis=0, tiled=True),
            lax.all_gather(w_query, ("dp", "seq"), axis=0, tiled=True),
            lax.all_gather(key_projection, ("dp", "seq"), axis=0, tiled=True),
            lax.all_gather(value_projection, ("dp", "seq"), axis=0, tiled=True),
            lax.all_gather(w_out, ("dp", "seq"), axis=0, tiled=True),
        )
        gain_m, wg, wu, wd = (
            lax.all_gather(mlp_gain, ("dp", "seq"), axis=0, tiled=True),
            lax.all_gather(w_gate, ("dp", "seq"), axis=0, tiled=True),
            lax.all_gather(w_up, ("dp", "seq"), axis=0, tiled=True),
            lax.all_gather(w_down, ("dp", "seq"), axis=0, tiled=True),
        )
        own_pos = block_positions(order, seq_place * local_length, local_length)
        angles = own_pos.astype(jnp.float32)[..., None] * freqs
        cosine_table = jnp.cos(angles)[:, :, None, :]
        sine_table = jnp.sin(angles)[:, :, None, :]

        def query_per_head(raw, gain):
            return apply_rotary(row_norm_apply(raw, gain), cosine_table, sine_table)

        flat_x = rows_x.reshape(-1, width).astype(jnp.float32)
        first_operand = row_norm_apply(flat_x, gain_a.astype(jnp.float32)).astype(jnp.bfloat16)
        query_unrotated = matrix_multiply(first_operand, wq).reshape(
            sequence_permutation, local_length, QUERY_HEADS, HEAD_SIZE
        )
        key_unrotated = matrix_multiply(first_operand, key_weight).reshape(
            sequence_permutation, local_length, KEY_VALUE_HEADS, HEAD_SIZE
        )
        value_reduced = (
            matrix_multiply(first_operand, value_weight)
            .astype(jnp.bfloat16)
            .reshape(sequence_permutation, local_length, KEY_VALUE_HEADS, HEAD_SIZE)
        )
        q_low = (
            query_per_head(query_unrotated, query_norm_gain)
            .astype(jnp.bfloat16)
            .reshape(sequence_permutation, local_length, KEY_VALUE_HEADS, query_group, HEAD_SIZE)
        )
        k_low = query_per_head(key_unrotated, kgain).astype(jnp.bfloat16)
        initial_maximum = jnp.full(
            (sequence_permutation, KEY_VALUE_HEADS, query_group, local_length),
            NEGATIVE_FILL,
            jnp.float32,
        )
        top = initial_maximum
        piece_k = lax.all_gather(k_low, "seq", axis=1, tiled=True)
        piece_v = lax.all_gather(value_reduced, "seq", axis=1, tiled=True)
        key_pos = block_positions(order, jnp.int32(0), piece_k.shape[1])
        visible = key_pos[:, None, None, None, :] <= own_pos[:, None, None, :, None]
        scores = (
            jnp.einsum("sqgrd,skgd->sgrqk", q_low, piece_k, preferred_element_type=jnp.float32)
            * scale
        )
        scores = jnp.where(visible, scores, NEGATIVE_FILL)
        new_top = jnp.maximum(top, jnp.max(scores, axis=-1))
        weights = jnp.exp(scores - new_top[..., None])
        new_total = jnp.sum(weights, axis=-1)
        taken = jnp.einsum(
            "sgrqk,skgd->sqgrd",
            weights.astype(jnp.bfloat16),
            piece_v,
            preferred_element_type=jnp.float32,
        )
        top = new_top
        log_total = top + jnp.log(new_total)
        attn = taken / jnp.transpose(new_total, (0, 3, 1, 2))[..., None]
        o_low = attn.astype(jnp.bfloat16).reshape(
            sequence_permutation * local_length, QUERY_HEADS * HEAD_SIZE
        )
        hidden = flat_x + matrix_multiply(o_low, output_weight)
        gain_second = gain_m.astype(jnp.float32)
        a_second = row_norm_apply(hidden, gain_second).astype(jnp.bfloat16)
        gate = matrix_multiply(a_second, wg)
        up_part = matrix_multiply(a_second, wu)
        mixed = (gate * jax.nn.sigmoid(gate) * up_part).astype(jnp.bfloat16)
        result = hidden + matrix_multiply(mixed, wd)
        outputs.append(
            result.astype(jnp.bfloat16).reshape(sequence_permutation, local_length, width)
        )
        gain_a, wq, key_weight, value_weight, output_weight = (
            lax.all_gather(attn_gain, ("dp", "seq"), axis=0, tiled=True),
            lax.all_gather(w_query, ("dp", "seq"), axis=0, tiled=True),
            lax.all_gather(key_projection, ("dp", "seq"), axis=0, tiled=True),
            lax.all_gather(value_projection, ("dp", "seq"), axis=0, tiled=True),
            lax.all_gather(w_out, ("dp", "seq"), axis=0, tiled=True),
        )
        gain_m, wg, wu, wd = (
            lax.all_gather(mlp_gain, ("dp", "seq"), axis=0, tiled=True),
            lax.all_gather(w_gate, ("dp", "seq"), axis=0, tiled=True),
            lax.all_gather(w_up, ("dp", "seq"), axis=0, tiled=True),
            lax.all_gather(w_down, ("dp", "seq"), axis=0, tiled=True),
        )
        flat_cot = rows_cot.reshape(-1, width)
        grad_down = row_product(mixed, flat_cot)
        d_mixed = product_backward(flat_cot, wd)

        def mix(gate_in, up_in):
            return gate_in * jax.nn.sigmoid(gate_in) * up_in

        _, mix_back = jax.vjp(mix, gate, up_part)
        d_gate, d_up = mix_back(d_mixed)
        gate_low = d_gate.astype(jnp.bfloat16)
        up_low = d_up.astype(jnp.bfloat16)
        grad_gate = row_product(a_second, gate_low)
        grad_up = row_product(a_second, up_low)
        d_second = product_backward(gate_low, wg) + product_backward(up_low, wu)
        _, second_back = jax.vjp(row_norm_apply, hidden, gain_second)
        d_hidden_norm, grad_mlp_gain = second_back(d_second)
        d_hidden = flat_cot.astype(jnp.float32) + d_hidden_norm
        grad_output_reduced = d_hidden.astype(jnp.bfloat16)
        grad_out = row_product(o_low, grad_output_reduced)
        do_low = (
            product_backward(grad_output_reduced, output_weight)
            .astype(jnp.bfloat16)
            .reshape(sequence_permutation, local_length, KEY_VALUE_HEADS, query_group, HEAD_SIZE)
        )
        delta = jnp.transpose(jnp.sum(do_low.astype(jnp.float32) * attn, axis=-1), (0, 2, 3, 1))

        def back_terms(held_k, held_v, visible):
            scores = (
                jnp.einsum("sqgrd,skgd->sgrqk", q_low, held_k, preferred_element_type=jnp.float32)
                * scale
            )
            scores = jnp.where(visible, scores, NEGATIVE_FILL)
            probs = jnp.exp(scores - log_total[..., None])
            d_probs = jnp.einsum(
                "sqgrd,skgd->sgrqk", do_low, held_v, preferred_element_type=jnp.float32
            )
            score_low = (probs * (d_probs - delta[..., None])).astype(jnp.bfloat16)
            probs_low = probs.astype(jnp.bfloat16)
            term_q = scale * jnp.einsum(
                "sgrqk,skgd->sqgrd", score_low, held_k, preferred_element_type=jnp.float32
            )
            term_k = scale * jnp.einsum(
                "sgrqk,sqgrd->skgd", score_low, q_low, preferred_element_type=jnp.float32
            )
            term_v = jnp.einsum(
                "sgrqk,sqgrd->skgd", probs_low, do_low, preferred_element_type=jnp.float32
            )
            return (term_k, term_v, term_q)

        def cycle_step(turn, state):
            held_k, held_v, acc_k, acc_v, acc_q = state
            owner = (seq_place - turn) % seq_count
            key_pos = block_positions(order, owner * local_length, local_length)
            visible = key_pos[:, None, None, None, :] <= own_pos[:, None, None, :, None]
            term_k, term_v, term_q = back_terms(held_k, held_v, visible)
            acc_k, acc_v, acc_q = (acc_k + term_k, acc_v + term_v, acc_q + term_q)
            held_k, held_v = from_behind((held_k, held_v), "seq", 1)
            acc_k, acc_v = (
                from_behind(acc_k.astype(jnp.bfloat16), "seq", 1).astype(acc_k.dtype),
                from_behind(acc_v.astype(jnp.bfloat16), "seq", 1).astype(acc_v.dtype),
            )
            return (held_k, held_v, acc_k, acc_v, acc_q)

        def two_steps(pair, state):
            return cycle_step(2 * pair + 1, cycle_step(2 * pair, state))

        blank_key_value = jnp.zeros(
            (sequence_permutation, local_length, KEY_VALUE_HEADS, HEAD_SIZE), jnp.float32
        )
        blank_query = jnp.zeros(
            (sequence_permutation, local_length, KEY_VALUE_HEADS, query_group, HEAD_SIZE),
            jnp.float32,
        )
        state = lax.fori_loop(
            0,
            seq_count // 2,
            two_steps,
            (k_low, value_reduced, blank_key_value, blank_key_value, blank_query),
        )
        _, _, d_keys, grad_value_rows, d_queries = state
        _, query_back = jax.vjp(query_per_head, query_unrotated, query_norm_gain)
        d_q_raw, grad_qgain = query_back(
            d_queries.reshape(sequence_permutation, local_length, QUERY_HEADS, HEAD_SIZE)
        )
        _, key_back = jax.vjp(query_per_head, key_unrotated, kgain)
        grad_key_unrotated, grad_kgain = key_back(d_keys)
        dq_low = d_q_raw.astype(jnp.bfloat16).reshape(
            sequence_permutation * local_length, QUERY_HEADS * HEAD_SIZE
        )
        grad_key_reduced = grad_key_unrotated.astype(jnp.bfloat16).reshape(
            sequence_permutation * local_length, KEY_VALUE_HEADS * HEAD_SIZE
        )
        grad_value_reduced = grad_value_rows.astype(jnp.bfloat16).reshape(
            sequence_permutation * local_length, KEY_VALUE_HEADS * HEAD_SIZE
        )
        grad_query = row_product(first_operand, dq_low)
        grad_key = row_product(first_operand, grad_key_reduced)
        grad_value = row_product(first_operand, grad_value_reduced)
        d_first = (
            product_backward(dq_low, wq)
            + product_backward(grad_key_reduced, key_weight)
            + product_backward(grad_value_reduced, value_weight)
        )
        _, first_back = jax.vjp(row_norm_apply, flat_x, gain_a.astype(jnp.float32))
        d_x_norm, grad_attn_gain = first_back(d_first)
        input_grads.append(
            (d_hidden + d_x_norm)
            .astype(jnp.bfloat16)
            .reshape(sequence_permutation, local_length, width)
        )
        fresh = (
            grad_attn_gain,
            grad_query,
            grad_key,
            grad_value,
            grad_out,
            grad_mlp_gain,
            grad_gate,
            grad_up,
            grad_down,
            grad_qgain,
            grad_kgain,
        )
        if sums is None:
            sums = fresh
        else:
            sums = tuple((a + b for a, b in zip(sums, fresh)))
    attn_members = (sums[0], sums[1], sums[2], sums[3], sums[4])
    mlp_members = (sums[5], sums[6], sums[7], sums[8])
    attn_flat = lax.psum_scatter(
        pack_shares(attn_members, all_count), ("dp", "seq"), scatter_dimension=0, tiled=True
    )
    mlp_flat = lax.psum_scatter(
        pack_shares(mlp_members, all_count), ("dp", "seq"), scatter_dimension=0, tiled=True
    )
    attn_shares = unpack_shares(attn_flat, attn_members, all_count)
    mlp_shares = unpack_shares(mlp_flat, mlp_members, all_count)
    head_sums = lax.psum((sums[9], sums[10]), ("dp", "seq"))
    return (
        jnp.concatenate(outputs, axis=0),
        jnp.concatenate(input_grads, axis=0),
        attn_shares[0],
        attn_shares[1],
        attn_shares[2],
        attn_shares[3],
        head_sums[0],
        head_sums[1],
        attn_shares[4],
        mlp_shares[0],
        mlp_shares[1],
        mlp_shares[2],
        mlp_shares[3],
    )


def solution(mesh):
    return jax.shard_map(
        shards,
        mesh=mesh,
        in_specs=(
            P("dp", "seq", None),
            P(("dp", "seq")),
            P(("dp", "seq"), None),
            P(("dp", "seq"), None),
            P(("dp", "seq"), None),
            P(),
            P(),
            P(("dp", "seq"), None),
            P(("dp", "seq")),
            P(("dp", "seq"), None),
            P(("dp", "seq"), None),
            P(("dp", "seq"), None),
            P("dp", "seq", None),
            P("dp", None),
        ),
        out_specs=(
            P("dp", "seq", None),
            P("dp", "seq", None),
            P(("dp", "seq")),
            P(("dp", "seq"), None),
            P(("dp", "seq"), None),
            P(("dp", "seq"), None),
            P(),
            P(),
            P(("dp", "seq"), None),
            P(("dp", "seq")),
            P(("dp", "seq"), None),
            P(("dp", "seq"), None),
            P(("dp", "seq"), None),
        ),
        check_vma=False,
    )
```

profile of v0, /device:TPU:27, one launch (start us, length us, event | category | flops | bytes accessed | tf_op | source)
XLA Modules:
  0.0 2449.6 jit_solution(8134314648129835)
XLA Ops:
  11.1 38.6 %all-reduce.14 = (bf16[1024]{0:T(1024)(128)(2,1)S(1)}, bf16[1024]{0:T(1024)(128)(2,1)}) all-reduce(bf16[1024]{0:T(1024)(128)(2,1)S(1)} %dynamic-update-slice, bf16[1024]{0:T(1024)(128)(2,1)S(1)} %dynamic-update-slice.1), channel_id=1, replica_groups=mesh['dp'=4,'seq'=8] {'dp','seq'}, use_global_device_ids=true, to_apply=%add.8 | all-reduce | flops 2048 | bytes 8192
  55.1 12.7 all-gather.16.cloned.1.call-done
  75.3 50.9 %all-gather.12.cloned.1.call-done = bf16[1024,1024]{1,0:T(8,128)(2,1)} async-done(((bf16[32,1024]{1,0:T(8,128)(2,1)}), bf16[1024,1024]{1,0:T(8,128)(2,1)}) %all-gather.12.cloned.1.call-update) | async-done | bytes 2097168 | tf_op jit(solution)/shard_map/all_gather | solution.py:115
  144.3 45.4 %all-gather.20.cloned.1.call-done = bf16[1024,2048]{1,0:T(8,128)(2,1)} async-done(((bf16[32,2048]{1,0:T(8,128)(2,1)}), bf16[1024,2048]{1,0:T(8,128)(2,1)}) %all-gather.20.cloned.1.call-update) | async-done | bytes 4194320 | tf_op jit(solution)/shard_map/all_gather | solution.py:113
  203.4 36.5 %all-gather.18.cloned.1.call-done = bf16[1,1024,8,128]{3,1,2,0:T(8,128)(2,1)} async-done(((bf16[1,128,8,128]{3,1,2,0:T(8,128)(2,1)}), bf16[1,1024,8,128]{3,1,2,0:T(8,128)(2,1)}) %all-gather.18.cloned.1.call-update) | async-done | bytes 2097168 | tf_op jit(solution)/shard_map/all_gather | solution.py:157
  248.3 43.5 %all-gather.14.cloned.1.call-done = bf16[1,1024,8,128]{1,3,2,0:T(8,128)(2,1)} async-done(((bf16[1,128,8,128]{1,3,2,0:T(8,128)(2,1)}), bf16[1,1024,8,128]{1,3,2,0:T(8,128)(2,1)}) %all-gather.14.cloned.1.call-update) | async-done | bytes 2097168 | tf_op jit(solution)/shard_map/all_gather | solution.py:158
  299.1 56.4 %all-gather.22.cloned.1.call-done = bf16[2048,1024]{1,0:T(8,128)(2,1)} async-done(((bf16[64,1024]{1,0:T(8,128)(2,1)}), bf16[2048,1024]{1,0:T(8,128)(2,1)}) %all-gather.22.cloned.1.call-update) | async-done | bytes 4194320 | tf_op jit(solution)/shard_map/all_gather | solution.py:116
  358.7 47.1 %all-gather.32.cloned.1.call-done = bf16[1,1024,8,128]{3,1,2,0:T(8,128)(2,1)} async-done(((bf16[1,128,8,128]{3,1,2,0:T(8,128)(2,1)}), bf16[1,1024,8,128]{3,1,2,0:T(8,128)(2,1)}) %all-gather.32.cloned.1.call-update) | async-done | bytes 2097168 | tf_op jit(solution)/shard_map/all_gather | solution.py:157
  414.2 43.7 %all-gather.30.cloned.1.call-done = bf16[1,1024,8,128]{1,3,2,0:T(8,128)(2,1)} async-done(((bf16[1,128,8,128]{1,3,2,0:T(8,128)(2,1)}), bf16[1,1024,8,128]{1,3,2,0:T(8,128)(2,1)}) %all-gather.30.cloned.1.call-update) | async-done | bytes 2097168 | tf_op jit(solution)/shard_map/all_gather | solution.py:158
  468.1 61.0 %all-gather.24.cloned.1.call-done = bf16[1024,3072]{1,0:T(8,128)(2,1)} async-done(((bf16[32,3072]{1,0:T(8,128)(2,1)}), bf16[1024,3072]{1,0:T(8,128)(2,1)}) %all-gather.24.cloned.1.call-update) | async-done | bytes 6291472 | tf_op jit(solution)/shard_map/all_gather | solution.py:120
  534.0 65.9 %all-gather.26.cloned.1.call-done = bf16[1024,3072]{1,0:T(8,128)(2,1)} async-done(((bf16[32,3072]{1,0:T(8,128)(2,1)}), bf16[1024,3072]{1,0:T(8,128)(2,1)}) %all-gather.26.cloned.1.call-update) | async-done | bytes 6291472 | tf_op jit(solution)/shard_map/all_gather | solution.py:121
  604.8 66.0 %all-gather.28.cloned.1.call-done = bf16[3072,1024]{1,0:T(8,128)(2,1)} async-done(((bf16[96,1024]{1,0:T(8,128)(2,1)}), bf16[3072,1024]{1,0:T(8,128)(2,1)}) %all-gather.28.cloned.1.call-update) | async-done | bytes 6291472 | tf_op jit(solution)/shard_map/all_gather | solution.py:122
  716.1 186.4 %while.51 = (s32[]{:T(128)}, bf16[1,128,8,128]{3,1,2,0:T(8,128)(2,1)S(1)}, bf16[1,128,8,128]{3,1,2,0:T(8,128)(2,1)}, f32[1,128,8,128]{3,1,2,0:T(8,128)}, f32[1,1...) while((s32[]{:T(128)}, ...), condition=%wide.region_30.31_spmd.clone, body=%wide.region_27.30_spmd.clone.sunk | while | flops 678219008 | bytes 34184580 | solution.py:277
  916.3 175.6 %while.50 = (s32[]{:T(128)}, bf16[1,128,8,128]{3,1,2,0:T(8,128)(2,1)S(1)}, bf16[1,128,8,128]{3,1,2,0:T(8,128)(2,1)S(1)}, f32[1,128,8,128]{3,1,2,0:T(8,128)}, f32...) while((s32[]{:T(128)}, ...), condition=%wide.region_21.22_spmd.clone, body=%wide.region_18.21_spmd.clone.sunk | while | flops 678219008 | bytes 34184580 | solution.py:277
  1133.0 8.1 convolution_add_fusion.4
  1168.5 8.0 convolution_add_fusion.3
  1185.3 26.0 %dynamic-update-slice.7 = f32[32,196640]{1,0:T(8,128)} dynamic-update-slice(f32[32,196640]{1,0:T(8,128)} %dynamic-update-slice.6, f32[32,65536]{1,0:T(8,128)} %reshape.2647, s32[]{} %constant.514, s32[]{} %constant.515) | dynamic-update-slice | bytes 16777220
  1211.3 14.9 dynamic-update-slice.8
  1226.1 14.8 dynamic-update-slice.9
  1241.0 25.7 %dynamic-update-slice.10 = f32[32,196640]{1,0:T(8,128)} dynamic-update-slice(f32[32,196640]{1,0:T(8,128)} %dynamic-update-slice.9, f32[32,65536]{1,0:T(8,128)} %reshape.2650, s32[]{} %constant.514, s32[]{} %constant.519) | dynamic-update-slice | bytes 16777220 | tf_op jit(solution)/shard_map/concatenate | solution.py:63
  1266.8 26.6 %reshape.2651 = f32[6292480]{0:T(1024)} reshape(f32[32,196640]{1,0:T(8,128)} %dynamic-update-slice.10) | data formatting | bytes 50339840 | tf_op jit(solution)/shard_map/reshape | solution.py:63
  1293.5 11.0 convolution_add_fusion.2
  1304.4 10.1 reshape.2656
  1314.6 11.0 convolution_add_fusion.1
  1325.6 10.1 reshape.2657
  1343.9 9.9 reshape.2658
  1355.1 37.1 %dynamic-update-slice.3 = f32[32,294944]{1,0:T(8,128)} dynamic-update-slice(f32[32,294944]{1,0:T(8,128)} %dynamic-update-slice.2, f32[32,98304]{1,0:T(8,128)} %reshape.2656, s32[]{} %constant.514, s32[]{} %constant.515) | dynamic-update-slice | bytes 25165828
  1392.2 37.0 %dynamic-update-slice.4 = f32[32,294944]{1,0:T(8,128)} dynamic-update-slice(f32[32,294944]{1,0:T(8,128)} %dynamic-update-slice.3, f32[32,98304]{1,0:T(8,128)} %reshape.2657, s32[]{} %constant.514, s32[]{} %constant.516) | dynamic-update-slice | bytes 25165828
  1429.2 36.7 %dynamic-update-slice.5 = f32[32,294944]{1,0:T(8,128)} dynamic-update-slice(f32[32,294944]{1,0:T(8,128)} %dynamic-update-slice.4, f32[32,98304]{1,0:T(8,128)} %reshape.2658, s32[]{} %constant.514, s32[]{} %constant.517) | dynamic-update-slice | bytes 25165828 | tf_op jit(solution)/shard_map/concatenate | solution.py:63
  1465.9 41.5 %reshape.2659 = f32[9438208]{0:T(1024)} reshape(f32[32,294944]{1,0:T(8,128)} %dynamic-update-slice.5) | data formatting | bytes 75505664 | tf_op jit(solution)/shard_map/reshape | solution.py:63
  1508.1 55.5 %all-reduce.12 = (f32[128]{0:T(128)}, f32[128]{0:T(128)}) all-reduce(f32[128]{0:T(128)S(1)} %add.1002, f32[128]{0:T(128)S(1)} %add.1003), channel_id=1, replica_groups=mesh['dp'=4,'seq'=8] {'dp','seq'}, use_global_device_ids=true, to_apply=%region_39.40 | all-reduce | flops 256 | bytes 2048 | tf_op jit(solution)/shard_map/psum | solution.py:341
  1574.1 856.4 %all-reduce.17.cloned.1.call-done = (f32[6292480]{0:T(1024)}, f32[9438208]{0:T(1024)}) async-done(((f32[6292480]{0:T(1024)}, f32[9438208]{0:T(1024)}), (f32[6292480]{0:T(1024)}, f32[9438208]{0:T(1024)})) %all-reduce.17.cloned.1.call-update) | async-done | bytes 62922768
  (728 shorter events, 623.5 us)
Async XLA Ops:
  7.2 60.6 %all-gather.16.cloned.1.call-start = ((), (), s32[]{:S(2)}) async-start(), calls=%async_computation.2 | async-start | bytes 2162688 | tf_op jit(solution)/shard_map/all_gather | solution.py:114
  7.9 118.3 %all-gather.12.cloned.1.call-start = ((), (), s32[]{:S(2)}) async-start(), calls=%async_computation | async-start | bytes 2162688 | tf_op jit(solution)/shard_map/all_gather | solution.py:115
  8.7 181.1 %all-gather.20.cloned.1.call-start = ((), (), s32[]{:S(2)}) async-start(), calls=%async_computation.4 | async-start | bytes 4325376 | tf_op jit(solution)/shard_map/all_gather | solution.py:113
  9.4 230.5 %all-gather.18.cloned.1.call-start = ((), (), s32[]{:S(2)}) async-start(), calls=%async_computation.3 | async-start | bytes 2359296 | tf_op jit(solution)/shard_map/all_gather | solution.py:157
  75.2 216.6 %all-gather.14.cloned.1.call-start = ((), (), s32[]{:S(2)}) async-start(), calls=%async_computation.1 | async-start | bytes 2359296 | tf_op jit(solution)/shard_map/all_gather | solution.py:158
  129.3 226.2 %all-gather.22.cloned.1.call-start = ((), (), s32[]{:S(2)}) async-start(), calls=%async_computation.5 | async-start | bytes 4325376 | tf_op jit(solution)/shard_map/all_gather | solution.py:116
  129.9 275.9 %all-gather.32.cloned.1.call-start = ((), (), s32[]{:S(2)}) async-start(), calls=%async_computation.10 | async-start | bytes 2359296 | tf_op jit(solution)/shard_map/all_gather | solution.py:157
  131.1 326.8 %all-gather.30.cloned.1.call-start = ((), (), s32[]{:S(2)}) async-start(), calls=%async_computation.9 | async-start | bytes 2359296 | tf_op jit(solution)/shard_map/all_gather | solution.py:158
  134.2 394.9 %all-gather.24.cloned.1.call-start = ((), (), s32[]{:S(2)}) async-start(), calls=%async_computation.6 | async-start | bytes 6488064 | tf_op jit(solution)/shard_map/all_gather | solution.py:120
  135.0 464.9 %all-gather.26.cloned.1.call-start = ((), (), s32[]{:S(2)}) async-start(), calls=%async_computation.7 | async-start | bytes 6488064 | tf_op jit(solution)/shard_map/all_gather | solution.py:121
  135.6 535.3 %all-gather.28.cloned.1.call-start = ((), (), s32[]{:S(2)}) async-start(), calls=%async_computation.8 | async-start | bytes 6488064 | tf_op jit(solution)/shard_map/all_gather | solution.py:122
  136.3 2294.3 %all-reduce.17.cloned.1.call-start = ((), (), s32[]{:S(2)}) async-start(), calls=%async_computation.11 | async-start | bytes 125845504
  716.9 13.9 collective-permute-start.10
  725.8 16.3 collective-permute-start.14
  743.8 14.7 collective-permute-start.9
  748.1 16.1 collective-permute-start.11
  764.2 15.2 collective-permute-start.10
  783.4 14.6 collective-permute-start.13
  795.6 14.1 collective-permute-start.11
  809.8 16.5 collective-permute-start.8
  812.9 14.7 collective-permute-start.10
  842.8 14.4 collective-permute-start.11
  857.2 14.5 collective-permute-start.8
  858.3 14.7 collective-permute-start.10
  887.3 15.2 collective-permute-start.11
  940.4 15.1 collective-permute-start.1
  943.4 17.7 collective-permute-start.3
  984.2 14.8 collective-permute-start.1
  986.5 18.1 collective-permute-start.3
  1030.0 16.1 collective-permute-start.3
  1046.1 14.0 collective-permute-start
  1076.3 15.5 collective-permute-start.3
  (173 other events, 2900.5 us)
Sparse Core Ops, SparseCore 0:
  11.0 56.7 all-gather.15
  70.8 55.3 all-gather.11
  129.3 60.4 all-gather.19
  192.4 47.4 all-gather.17
  242.4 49.4 all-gather.13
  294.8 60.7 all-gather.21
  358.3 47.4 all-gather.31
  408.4 49.4 all-gather.29
  460.8 68.2 all-gather.23
  531.8 67.9 all-gather.25
  602.8 67.9 all-gather.27
  1507.6 922.8 all-reduce.16
where the time goes:
time: 2470 us; the launch traced here: 2450 us
  waiting for transfers between devices  1540 us (62%)
  local copies, waits for them, and re-layouts  359 us (15%)
  matrix products  276 us (11%)
  blocking collectives  94.1 us (4%)
  starting transfers between devices  90.7 us (4%)
  other arithmetic  73 us (3%)
    unnamed x13, waiting for transfers between devices  861 us
    unnamed x262, local copies, waits for them, and re-layouts  148 us
    ppermute x64, waiting for transfers between devices, from_behind(): return lax.ppermute(block, axis, route)  148 us
    ppermute x64, starting transfers between devices, from_behind(): return lax.ppermute(block, axis, route)  90.3 us
    all_gather x2, waiting for transfers between devices, shards(): piece_v = lax.all_gather(value_reduced, 'seq', axis=1, tiled=True)  87.2 us
    dot_general x14, matrix products, row_product(): lax.dot_general(left, right, (((0,), (0,)), ((), ())), preferred_element_...  85.6 us
    all_gather x2, waiting for transfers between devices, shards(): piece_k = lax.all_gather(k_low, 'seq', axis=1, tiled=True)  83.6 us
    reshape x2, local copies, waits for them, and re-layouts, pack_shares(): jnp.concatenate([m.reshape(count, -1) for m in members], axis=1).reshape(-1)  68.2 us
  transfers between devices with their start and end apart: 76, of which 56 were waited for; matrix products, arithmetic and copies ran while one was open for 9% of the time, Pallas kernels for 0%

commit v1 on v0

--- a/solution.py
+++ b/solution.py
@@ -2,6 +2,9 @@
 import jax.numpy as jnp
 from jax import lax
 from jax.sharding import PartitionSpec as P
+
+from jax.experimental import pallas as pl
+from jax.experimental.pallas import tpu as pltpu
 
 QUERY_HEADS = 16
 KEY_VALUE_HEADS = 8
@@ -356,9 +359,884 @@
     )
 
 
+BF = jnp.bfloat16
+F32 = jnp.float32
+MESH = pl.DeviceIdType.MESH
+TOKENS = 1024
+WIDTH = 1024
+LOG2E = 1.4426950408889634
+VM = pl.BlockSpec(memory_space=pltpu.VMEM)
+SM = pl.BlockSpec(memory_space=pltpu.SMEM)
+ANY = pl.BlockSpec(memory_space=pl.ANY)
+VMEM_BYTES = 60 * 1024 * 1024
+
+
+def place():
+    q = lax.axis_index("dp")
+    p = lax.axis_index("seq")
+    return q, p, q // 2, lax.rem(q, 2), p // 2, lax.rem(p, 2)
+
+
+def greet(peers):
+    barrier = pltpu.get_barrier_semaphore()
+    for peer in peers:
+        pl.semaphore_signal(barrier, inc=1, device_id=peer, device_id_type=MESH)
+    pl.semaphore_wait(barrier, len(peers))
+
+
+def remote(src, dst, send, recv, peer):
+    return pltpu.make_async_remote_copy(
+        src_ref=src, dst_ref=dst, send_sem=send, recv_sem=recv, device_id=peer, device_id_type=MESH
+    )
+
+
+def dims(left, right, lc, rc):
+    return lax.dot_general(left, right, (((lc,), (rc,)), ((), ())), preferred_element_type=F32)
+
+
+def gather_kernel(
+    tok, cot, pos, pq, pg, po, pd,
+    xf, cf, of, wq, wg, wo, wd,
+    loc, ts, tr, fs, fr, ps, pr, as_, ar, zs, zr, ys, yr,
+):
+    q, p, x, c, z, y = place()
+    peers = [(lax.rem(q + k, 4), p) for k in (1, 2, 3)]
+    peers += [(q, lax.rem(p + k, 8)) for k in range(1, 8)]
+    greet(peers)
+    owner_x, owner_c = y, z // 2
+    is_owner = jnp.logical_and(x == owner_x, c == owner_c)
+    cross = jnp.logical_and(x != owner_x, c == owner_c)
+    last = jnp.logical_and(x != owner_x, c != owner_c)
+    sends = []
+    cols = ((pq, wq), (pg, wg))
+    locals_ = []
+    for n, (src, dst) in enumerate(cols):
+        for k in (1, 2, 3):
+            t = lax.rem(q + k, 4)
+            cp = remote(src.at[t], dst.at[q, p], as_.at[n, k - 1], ar.at[n, k - 1], (t, p))
+            cp.start()
+            sends.append(cp)
+        cp = pltpu.make_async_copy(src.at[q], dst.at[q, p], loc.at[n])
+        cp.start()
+        locals_.append(cp)
+    for n, (src, dst) in enumerate(((po, wo), (pd, wd))):
+        cp = pltpu.make_async_copy(src, dst.at[p], loc.at[2 + n])
+        cp.start()
+        locals_.append(cp)
+    toks = ((tok, xf), (cot, cf))
+
+    def token_copy(a, i):
+        src, dst = toks[a]
+        goal = 4 * c + 2 * i + x
+        return goal, remote(src.at[i], dst.at[p], ts.at[a, i], tr.at[a, p], (q, goal))
+
+    def token_local(a, i):
+        src, dst = toks[a]
+        return pltpu.make_async_copy(src.at[i], dst.at[p], loc.at[4 + a])
+
+    for a in range(2):
+        for i in range(2):
+            goal, cp = token_copy(a, i)
+
+            @pl.when(goal != p)
+            def _():
+                cp.start()
+
+            @pl.when(goal == p)
+            def _():
+                token_local(a, i).start()
+
+    def share(n):
+        return (wq, wg, wo, wd)[n]
+
+    def view(n, chunk):
+        ref = share(n)
+        return ref.at[:, chunk] if n < 2 else ref.at[chunk]
+
+    def z_send(n):
+        for k in (1, 2, 3):
+            t = lax.rem(z + k, 4)
+            cp = remote(view(n, p), view(n, p), zs.at[n, k - 1], zr.at[n, k - 1], (q, 2 * t + y))
+            cp.start()
+            sends.append(cp)
+
+    def y_send(n, k):
+        chunk = 2 * lax.rem(z + 4 - k, 4) + y
+        cp = remote(view(n, chunk), view(n, chunk), ys.at[n, k], yr.at[n, k], (q, 2 * z + 1 - y))
+        cp.start()
+        sends.append(cp)
+
+    def z_wait(n, k):
+        chunk = 2 * lax.rem(z + 4 - k, 4) + y
+        remote(view(n, chunk), view(n, chunk), zs.at[n, k - 1], zr.at[n, k - 1], (q, p)).wait_recv()
+
+    def y_wait(n, k):
+        chunk = 2 * lax.rem(z + 4 - k, 4) + 1 - y
+        remote(view(n, chunk), view(n, chunk), ys.at[n, k], yr.at[n, k], (q, p)).wait_recv()
+
+    def a_wait(n):
+        src, dst = cols[n]
+        for k in (1, 2, 3):
+            f = lax.rem(q + 4 - k, 4)
+            remote(src.at[0], dst.at[f, p], as_.at[n, k - 1], ar.at[n, k - 1], (q, p)).wait_recv()
+
+    def t_wait(a, b):
+        dst = toks[a][1]
+        remote(dst.at[b], dst.at[b], ts.at[a, 0], tr.at[a, b], (q, p)).wait_recv()
+
+    def forwards(a):
+        dst = toks[a][1]
+        sib = (2 * x + 1 - c, p)
+        opp = (2 * (1 - x) + c, p)
+
+        @pl.when(is_owner)
+        def _():
+            @pl.loop(0, 8)
+            def _(b):
+                @pl.when(b != p)
+                def _():
+                    t_wait(a, b)
+
+                @pl.when(b == p)
+                def _():
+                    token_local(a, 0).wait()
+
+                remote(dst.at[b], dst.at[b], fs.at[a, 0, b], fr.at[a, b], sib).start()
+                remote(dst.at[b], dst.at[b], fs.at[a, 1, b], fr.at[a, b], opp).start()
+
+        @pl.when(jnp.logical_not(is_owner))
+        def _():
+            @pl.loop(0, 8)
+            def _(b):
+                remote(dst.at[b], dst.at[b], fs.at[a, 0, b], fr.at[a, b], sib).wait_recv()
+
+                @pl.when(cross)
+                def _():
+                    remote(dst.at[b], dst.at[b], fs.at[a, 0, b], fr.at[a, b], sib).start()
+
+    def forwards_done(a):
+        dst = toks[a][1]
+
+        @pl.when(is_owner)
+        def _():
+            @pl.loop(0, 8)
+            def _(b):
+                remote(dst.at[b], dst.at[b], fs.at[a, 0, b], fr.at[a, b], (q, p)).wait_send()
+                remote(dst.at[b], dst.at[b], fs.at[a, 1, b], fr.at[a, b], (q, p)).wait_send()
+
+        @pl.when(cross)
+        def _():
+            @pl.loop(0, 8)
+            def _(b):
+                remote(dst.at[b], dst.at[b], fs.at[a, 0, b], fr.at[a, b], (q, p)).wait_send()
+
+    pos_peers = [(lax.rem(q + k, 4), p) for k in (1, 2, 3)]
+    pos_local = pltpu.make_async_copy(pos, of, loc.at[6])
+
+    @pl.when(is_owner)
+    def _():
+        pos_local.start()
+        for k in range(3):
+            remote(pos, of, ps.at[k], pr.at[0], pos_peers[k]).start()
+        pos_local.wait()
+
+    @pl.when(jnp.logical_not(is_owner))
+    def _():
+        remote(pos, of, ps.at[0], pr.at[0], (q, p)).wait_recv()
+
+    a_wait(0)
+    locals_[0].wait()
+    z_send(0)
+    y_send(0, 0)
+    locals_[2].wait()
+    z_send(2)
+    y_send(2, 0)
+    a_wait(1)
+    locals_[1].wait()
+    z_send(1)
+    y_send(1, 0)
+    locals_[3].wait()
+    z_send(3)
+    y_send(3, 0)
+    forwards(0)
+    for n in (0, 2):
+        for k in (1, 2, 3):
+            z_wait(n, k)
+            y_send(n, k)
+    forwards(1)
+    for n in (1, 3):
+        for k in (1, 2, 3):
+            z_wait(n, k)
+            y_send(n, k)
+    for n in range(4):
+        for k in range(4):
+            y_wait(n, k)
+    for cp in sends:
+        cp.wait_send()
+    for a in range(2):
+        for i in range(2):
+            goal, cp = token_copy(a, i)
+
+            @pl.when(goal != p)
+            def _():
+                cp.wait_send()
+        forwards_done(a)
+
+    @pl.when(is_owner)
+    def _():
+        for k in range(3):
+            remote(pos, of, ps.at[k], pr.at[0], pos_peers[k]).wait_send()
+
+
+def gather_call(tok, cot, pos, pq, pg, po, pd):
+    sem = pltpu.SemaphoreType.DMA
+    shape = jax.ShapeDtypeStruct
+    return pl.pallas_call(
+        gather_kernel,
+        out_shape=(
+            shape((8, 128, WIDTH), BF),
+            shape((8, 128, WIDTH), BF),
+            shape((8, 128), jnp.int32),
+            shape((4, 8) + pq.shape[1:], BF),
+            shape((4, 8) + pg.shape[1:], BF),
+            shape((8,) + po.shape, BF),
+            shape((8,) + pd.shape, BF),
+        ),
+        in_specs=[ANY] * 7,
+        out_specs=(ANY,) * 7,
+        scratch_shapes=[
+            sem((7,)), sem((2, 2)), sem((2, 8)), sem((2, 2, 8)), sem((2, 8)), sem((3,)), sem((1,)),
+            sem((2, 3)), sem((2, 3)), sem((4, 3)), sem((4, 3)), sem((4, 4)), sem((4, 4)),
+        ],
+        compiler_params=pltpu.CompilerParams(collective_id=0, has_side_effects=True),
+        name="gather_layer",
+    )(tok, cot, pos, pq, pg, po, pd)
+
+
+def allsum_kernel(part, total, own, l1, l2, s1, r1, s2, r2, s3, r3):
+    q, p, x, c, z, y = place()
+    sib = (2 * x + 1 - c, p)
+    opp = (2 * (1 - x) + c, p)
+    greet([sib, opp])
+    steps = 4
+    rows = TOKENS // 2 // steps
+    mine = c * (TOKENS // 2)
+    other = (1 - c) * (TOKENS // 2)
+
+    def at(base, n):
+        return pl.ds(pl.multiple_of(base + n * rows, rows), rows)
+
+    first = [remote(part.at[at(other, n)], l1.at[n], s1.at[n], r1.at[n], sib) for n in range(steps)]
+    second = [remote(own.at[n], l2.at[n], s2.at[n], r2.at[n], opp) for n in range(steps)]
+    third = [remote(total.at[at(mine, n)], total.at[at(mine, n)], s3.at[n], r3.at[n], sib) for n in range(steps)]
+    for cp in first:
+        cp.start()
+    for n in range(steps):
+        first[n].wait_recv()
+        own[n] = (part[at(mine, n), :].astype(F32) + l1[n].astype(F32)).astype(BF)
+        second[n].start()
+    for n in range(steps):
+        second[n].wait_recv()
+        total[at(mine, n), :] = (own[n].astype(F32) + l2[n].astype(F32)).astype(BF)
+        third[n].start()
+    for n in range(steps):
+        remote(total.at[at(other, n)], total.at[at(other, n)], s3.at[n], r3.at[n], sib).wait_recv()
+    for cp in first + second + third:
+        cp.wait_send()
+
+
+def allsum(part, ident):
+    sem = pltpu.SemaphoreType.DMA
+    return pl.pallas_call(
+        allsum_kernel,
+        out_shape=jax.ShapeDtypeStruct((TOKENS, WIDTH), BF),
+        in_specs=[VM],
+        out_specs=VM,
+        scratch_shapes=[pltpu.VMEM((4, 128, WIDTH), BF)] * 3 + [sem((4,))] * 6,
+        compiler_params=pltpu.CompilerParams(
+            collective_id=ident, has_side_effects=True, vmem_limit_bytes=VMEM_BYTES
+        ),
+        name=f"sum_quarters_{ident}",
+    )(part)
+
+
+def unit(v):
+    return lax.rsqrt(jnp.mean(v * v, axis=-1, keepdims=True) + EPS)
+
+
+def blocks(ref, order, first, count):
+    return jnp.concatenate(
+        [ref[pl.ds(pl.multiple_of(order[first + t] * BLK, BLK), BLK), :] for t in range(count)], axis=0
+    )
+
+
+def pieces(ref, order, first, count):
+    return jnp.concatenate([ref[order[first + t]] for t in range(count)], axis=0)
+
+
+def rotate(v, cosine, sine):
+    return v * cosine + pltpu.roll(v, HEAD_SIZE // 2, 1) * sine
+
+
+def rotate_back(v, cosine, sine):
+    return v * cosine + pltpu.roll(v * sine, HEAD_SIZE // 2, 1)
+
+
+def lower(s, fill):
+    n = s.shape[0]
+    i = lax.broadcasted_iota(jnp.int32, (n, n), 0)
+    j = lax.broadcasted_iota(jnp.int32, (n, n), 1)
+    width = s.shape[1]
+    diag = jnp.where(j <= i, s[:, width - n :], fill)
+    return diag if width == n else jnp.concatenate([s[:, : width - n], diag], axis=1)
+
+
+def forward_kernel(inv, x, w, cosf, sinf, qg, kg, wo, xhat, raw_o, qb, kb, vb, ob, lse, part):
+    @pl.loop(0, 4)
+    def _(n):
+        rows = pl.ds(pl.multiple_of(n * 256, 256), 256)
+        v = blocks(x, inv, n * 4, 4).astype(F32)
+        h = (v * unit(v)).astype(BF)
+        xhat[rows, :] = h
+        raw = jnp.dot(h, w[...], preferred_element_type=F32)
+        raw_o[rows, :] = raw[:, :768]
+        cosine = cosf[rows, :]
+        sine = sinf[rows, :]
+        for t in range(2):
+            vb[t, rows, :] = raw[:, 768 + t * 128 : 896 + t * 128].astype(BF)
+        for t in range(6):
+            u = raw[:, t * 128 : (t + 1) * 128]
+            n_ = u * unit(u) * (qg[...] if t < 4 else kg[...])
+            r = rotate(n_, cosine, sine).astype(BF)
+            if t < 4:
+                qb[t, rows, :] = r
+            else:
+                kb[t - 4, rows, :] = r
+
+    @pl.loop(0, 4)
+    def _(h):
+        g = h // 2
+        for i in range(4):
+            length = (i + 1) * 256
+            rows = slice(i * 256, length)
+            s = dims(qb[h, rows, :], kb[g, :length, :], 1, 1) * (HEAD_SIZE**-0.5 * LOG2E)
+            s = lower(s, NEGATIVE_FILL)
+            top = jnp.max(s, axis=-1, keepdims=True)
+            e = jnp.exp2(s - top)
+            total = jnp.sum(e, axis=-1, keepdims=True)
+            o = jnp.dot(e.astype(BF), vb[g, :length, :], preferred_element_type=F32) / total
+            ob[rows, pl.ds(pl.multiple_of(h * 128, 128), 128)] = o.astype(BF)
+            lse[h, rows, :] = top + jnp.log2(total)
+
+    @pl.loop(0, 4)
+    def _(n):
+        rows = pl.ds(pl.multiple_of(n * 256, 256), 256)
+        part[rows, :] = jnp.dot(ob[rows, :], wo[...], preferred_element_type=F32).astype(BF)
+
+
+def forward_call(inv, x, w, cosf, sinf, qg, kg, wo):
+    shape = jax.ShapeDtypeStruct
+    return pl.pallas_call(
+        forward_kernel,
+        out_shape=(
+            shape((TOKENS, WIDTH), BF),
+            shape((TOKENS, 768), F32),
+            shape((4, TOKENS, 128), BF),
+            shape((2, TOKENS, 128), BF),
+            shape((2, TOKENS, 128), BF),
+            shape((TOKENS, 512), BF),
+            shape((4, TOKENS, 1), F32),
+            shape((TOKENS, WIDTH), BF),
+        ),
+        in_specs=[SM] + [VM] * 7,
+        out_specs=(VM,) * 8,
+        compiler_params=pltpu.CompilerParams(vmem_limit_bytes=VMEM_BYTES),
+        name="attention_forward",
+    )(inv, x, w, cosf, sinf, qg, kg, wo)
+
+
+def mlp_kernel(inv, order, x, total, cot, wgu, wd, hidden, part, dpart, gd, ggu, a2, cs, mb, dgu):
+    @pl.loop(0, 4)
+    def _(n):
+        rows = pl.ds(pl.multiple_of(n * 256, 256), 256)
+        h = blocks(x, inv, n * 4, 4).astype(F32) + total[rows, :].astype(F32)
+        hidden[rows, :] = h
+        a = (h * unit(h)).astype(BF)
+        a2[rows, :] = a
+        gu = jnp.dot(a, wgu[...], preferred_element_type=F32)
+        gate = gu[:, :768]
+        up = gu[:, 768:]
+        sig = 1.0 / (1.0 + jnp.exp2(gate * -LOG2E))
+        silu = gate * sig
+        mb[rows, :] = (silu * up).astype(BF)
+        cc = blocks(cot, inv, n * 4, 4)
+        cs[rows, :] = cc
+        dm = dims(cc, wd[...], 1, 1)
+        dg = (dm * up * sig * (1.0 + gate * (1.0 - sig))).astype(BF)
+        du = (dm * silu).astype(BF)
+        both = jnp.concatenate([dg, du], axis=1)
+        dgu[rows, :] = both
+        dpart[rows, :] = dims(both, wgu[...], 1, 1).astype(BF)
+
+    @pl.loop(0, 4)
+    def _(n):
+        rows = pl.ds(pl.multiple_of(n * 256, 256), 256)
+        part[rows, :] = jnp.dot(blocks(mb, order, n * 4, 4), wd[...], preferred_element_type=F32).astype(BF)
+
+    @pl.loop(0, 2)
+    def _(n):
+        g = dims(mb[:, pl.ds(pl.multiple_of(n * 384, 128), 384)], cs[...], 0, 0).astype(BF)
+        g = g.reshape(2, 2, 96, WIDTH)
+        for t in range(2):
+            gd[t, pl.ds(n * 2, 2)] = g[:, t]
+
+    @pl.loop(0, 4)
+    def _(n):
+        g = dims(a2[:, pl.ds(pl.multiple_of(n * 256, 256), 256)], dgu[...], 0, 0).astype(BF)
+        g = g.reshape(4, 2, 32, 1536)
+        for t in range(2):
+            ggu[t, :, n] = g[:, t]
+
+
+def mlp_call(inv, order, x, total, cot, wgu, wd):
+    shape = jax.ShapeDtypeStruct
+    return pl.pallas_call(
+        mlp_kernel,
+        out_shape=(
+            shape((TOKENS, WIDTH), F32),
+            shape((TOKENS, WIDTH), BF),
+            shape((TOKENS, WIDTH), BF),
+            shape((2, 4, 96, WIDTH), BF),
+            shape((2, 4, 4, 32, 1536), BF),
+        ),
+        in_specs=[SM] * 2 + [VM] * 5,
+        out_specs=(VM,) * 5,
+        scratch_shapes=[
+            pltpu.VMEM((TOKENS, WIDTH), BF),
+            pltpu.VMEM((TOKENS, WIDTH), BF),
+            pltpu.VMEM((TOKENS, 768), BF),
+            pltpu.VMEM((TOKENS, 1536), BF),
+        ],
+        compiler_params=pltpu.CompilerParams(vmem_limit_bytes=VMEM_BYTES),
+        name="feed_forward_both",
+    )(inv, order, x, total, cot, wgu, wd)
+
+
+def backward_kernel(
+    inv, order, cot, hidden, dtotal, wo, w, xhat, raw_i, qb, kb, vb, ob, lse, cosf, sinf, qg, kg,
+    dh, go, gqkv, part, heads, dy, dob, dqkv, dkv,
+):
+    @pl.loop(0, 4)
+    def _(n):
+        rows = pl.ds(pl.multiple_of(n * 256, 256), 256)
+        h = hidden[rows, :]
+        r = unit(h)
+        da = dtotal[rows, :].astype(F32)
+        back = r * da - h * (r * r * r * jnp.mean(h * da, axis=-1, keepdims=True))
+        d = blocks(cot, inv, n * 4, 4).astype(F32) + back
+        dh[rows, :] = d
+        low = d.astype(BF)
+        dy[rows, :] = low
+        do = dims(low, wo[...], 1, 1).astype(BF)
+        for t in range(4):
+            dob[t, rows, :] = do[:, t * 128 : (t + 1) * 128]
+
+    @pl.loop(0, 2)
+    def _(n):
+        g = dims(ob[:, pl.ds(pl.multiple_of(n * 256, 256), 256)], dy[...], 0, 0).astype(BF)
+        g = g.reshape(2, 2, 64, WIDTH)
+        for t in range(2):
+            go[t, pl.ds(n * 2, 2)] = g[:, t]
+
+    heads[...] = jnp.zeros_like(heads)
+    scale = HEAD_SIZE**-0.5
+
+    def norm_back(dn, u, gain, rows):
+        dn = rotate_back(dn, cosf[rows, :], sinf[rows, :])
+        r = unit(u)
+        gd = gain * dn
+        du = r * gd - u * (r * r * r * jnp.mean(u * gd, axis=-1, keepdims=True))
+        return du.astype(BF), jnp.sum(dn * u * r, axis=0, keepdims=True)
+
+    @pl.loop(0, 2)
+    def _(g):
+        dkv[...] = jnp.zeros_like(dkv)
+        for t in range(2):
+            h = g * 2 + t
+            lanes = pl.ds(pl.multiple_of(h * 128, 128), 128)
+            for i in range(4):
+                length = (i + 1) * 256
+                rows = slice(i * 256, length)
+                qv = qb[h, rows, :]
+                kv = kb[g, :length, :]
+                dov = dob[h, rows, :]
+                s = dims(qv, kv, 1, 1) * (scale * LOG2E)
+                pr = lower(jnp.exp2(s - lse[h, rows, :]), 0.0)
+                dp = dims(dov, vb[g, :length, :], 1, 1)
+                delta = jnp.sum(dov.astype(F32) * ob[rows, lanes].astype(F32), axis=-1, keepdims=True)
+                ds_ = lower(pr * (dp - delta), 0.0).astype(BF)
+                dq = jnp.dot(ds_, kv, preferred_element_type=F32) * scale
+                dkv[0, :length, :] += dims(ds_, qv, 0, 0)
+                dkv[1, :length, :] += dims(pr.astype(BF), dov, 0, 0)
+                du, dgain = norm_back(dq, raw_i[rows, lanes], qg[...], pl.ds(i * 256, 256))
+                dqkv[rows, lanes] = du
+                heads[0:1, :] += dgain
+        lanes = pl.ds(pl.multiple_of(512 + g * 128, 128), 128)
+        for i in range(4):
+            rows = slice(i * 256, (i + 1) * 256)
+            du, dgain = norm_back(dkv[0, rows, :] * scale, raw_i[rows, lanes], kg[...], pl.ds(i * 256, 256))
+            dqkv[rows, lanes] = du
+            heads[1:2, :] += dgain
+        dqkv[:, pl.ds(pl.multiple_of(768 + g * 128, 128), 128)] = dkv[1].astype(BF)
+
+    @pl.loop(0, 4)
+    def _(n):
+        rows = pl.ds(pl.multiple_of(n * 256, 256), 256)
+        part[rows, :] = dims(blocks(dqkv, order, n * 4, 4), w[...], 1, 1).astype(BF)
+
+    @pl.loop(0, 4)
+    def _(n):
+        g = dims(xhat[:, pl.ds(pl.multiple_of(n * 256, 256), 256)], dqkv[...], 0, 0).astype(BF)
+        g = g.reshape(4, 2, 32, WIDTH)
+        for t in range(2):
+            gqkv[t, :, n] = g[:, t]
+
+
+def backward_call(*args):
+    shape = jax.ShapeDtypeStruct
+    return pl.pallas_call(
+        backward_kernel,
+        out_shape=(
+            shape((TOKENS, WIDTH), F32),
+            shape((2, 4, 64, WIDTH), BF),
+            shape((2, 4, 4, 32, WIDTH), BF),
+            shape((TOKENS, WIDTH), BF),
+            shape((8, 128), F32),
+        ),
+        in_specs=[SM] * 2 + [VM] * 16,
+        out_specs=(VM,) * 5,
+        scratch_shapes=[
+            pltpu.VMEM((TOKENS, WIDTH), BF),
+            pltpu.VMEM((4, TOKENS, 128), BF),
+            pltpu.VMEM((TOKENS, WIDTH), BF),
+            pltpu.VMEM((2, TOKENS, 128), F32),
+        ],
+        compiler_params=pltpu.CompilerParams(vmem_limit_bytes=VMEM_BYTES),
+        name="attention_backward",
+    )(*args)
+
+
+def scatter_kernel(
+    gd, ggu, go, gqkv, heads, part, dpart, order, hidden, dh, x,
+    out, igrad, od, ogu, oo, oqkv, oheads,
+    yd, ygu, yo, yqkv, zd, zgu, zo, zqkv, dgu, dqkv, rgu, rqkv,
+    hy, hz, hdp, l1, l2, own, fin,
+    ys, yr, zs, zr, ds_, dr, hs, hr, s1, r1, s2, r2, fs, fr, loc,
+):
+    q, p, x_, c, z, y = place()
+    peers = [(2 * x_ + cc, lax.rem(p + k, 8)) for k in range(1, 8) for cc in (0, 1)]
+    peers += [(lax.rem(q + k, 4), p) for k in (1, 2, 3)]
+    greet(peers)
+    ynb = (q, 2 * z + 1 - y)
+    sib = (2 * x_ + 1 - c, p)
+    opp = (2 * (1 - x_) + c, p)
+    owner_x, owner_c = y, z // 2
+    half = TOKENS // 2
+    sends = []
+
+    def go_(cp):
+        cp.start()
+        sends.append(cp)
+
+    grads = ((gd, yd, zd), (ggu, ygu, zgu), (go, yo, zo), (gqkv, yqkv, zqkv))
+    for n, (g, ly, lz) in enumerate(grads):
+        go_(remote(g.at[1 - y], ly, ys.at[n], yr.at[n], ynb))
+    go_(remote(heads, hy, hs.at[0], hr.at[0], ynb))
+    mine = pl.ds(pl.multiple_of(c * half, half), half)
+    other = pl.ds(pl.multiple_of((1 - c) * half, half), half)
+    parts = (part, dpart)
+    for a in range(2):
+        go_(remote(parts[a].at[other], l1.at[a], s1.at[a], r1.at[a], sib))
+
+    for a in range(2):
+        remote(parts[a].at[other], l1.at[a], s1.at[a], r1.at[a], sib).wait_recv()
+        own[a] = (parts[a][mine, :].astype(F32) + l1[a].astype(F32)).astype(BF)
+
+        @pl.when(x_ != owner_x)
+        def _():
+            remote(own.at[a], l2.at[a], s2.at[a], r2.at[a], opp).start()
+
+    remote(heads, hy, hs.at[0], hr.at[0], ynb).wait_recv()
+    hz[z] = heads[...] + hy[...]
+    for k in (1, 2, 3):
+        t = lax.rem(z + k, 4)
+        go_(remote(hz.at[z], hz.at[z], hs.at[k], hr.at[k], (q, 2 * t + y)))
+
+    def z_step(n):
+        g, ly, lz = grads[n]
+        remote(g.at[1 - y], ly, ys.at[n], yr.at[n], ynb).wait_recv()
+
+        @pl.loop(0, 4)
+        def _(t):
+            ly[t] = (ly[t].astype(F32) + g[y, t].astype(F32)).astype(BF)
+
+        for k in (1, 2, 3):
+            t = lax.rem(z + k, 4)
+            go_(remote(ly.at[t], lz.at[k - 1], zs.at[n, k - 1], zr.at[n, k - 1], (q, 2 * t + y)))
+
+    def z_sum(n):
+        g, ly, lz = grads[n]
+        for k in (1, 2, 3):
+            remote(ly.at[0], lz.at[k - 1], zs.at[n, k - 1], zr.at[n, k - 1], (q, p)).wait_recv()
+        return ly[z].astype(F32) + lz[0].astype(F32) + lz[1].astype(F32) + lz[2].astype(F32)
+
+    z_step(0)
+    z_step(1)
+
+    @pl.when(x_ == owner_x)
+    def _():
+        for a in range(2):
+            remote(own.at[a], l2.at[a], s2.at[a], r2.at[a], opp).wait_recv()
+
+            @pl.loop(0, 4)
+            def _(n):
+                rows = pl.ds(pl.multiple_of(n * 128, 128), 128)
+                s = own[a, rows, :].astype(F32) + l2[a, rows, :].astype(F32)
+                first = c * 8 + n * 2
+                if a == 0:
+                    s = s + pieces(hidden, order, first, 2)
+                else:
+                    v = x[pl.ds(pl.multiple_of(c * half + n * 128, 128), 128), :].astype(F32)
+                    r = unit(v)
+                    s = r * s - v * (r * r * r * jnp.mean(v * s, axis=-1, keepdims=True))
+                    s = s + pieces(dh, order, first, 2)
+                fin[a, n] = s.astype(BF)
+
+    outs = (out, igrad)
+    slot = lax.rem(z, 2)
+    goal_q = 2 * owner_x + owner_c
+
+    def home(a, n):
+        return remote(fin.at[a, n], outs[a].at[slot], fs.at[a, n], fr.at[a, slot], (goal_q, 4 * c + n))
+
+    def is_self(n):
+        return jnp.logical_and(goal_q == q, 4 * c + n == p)
+
+    @pl.when(x_ == owner_x)
+    def _():
+        for a in range(2):
+            for n in range(4):
+
+                @pl.when(jnp.logical_not(is_self(n)))
+                def _():
+                    home(a, n).start()
+
+                @pl.when(is_self(n))
+                def _():
+                    cp = pltpu.make_async_copy(fin.at[a, n], outs[a].at[slot], loc.at[a])
+                    cp.start()
+                    cp.wait()
+
+    z_step(2)
+    z_step(3)
+    for k in (1, 2, 3):
+        f = lax.rem(z + 4 - k, 4)
+        remote(hz.at[f], hz.at[f], hs.at[k], hr.at[k], (q, p)).wait_recv()
+    hdp[q] = hz[0] + hz[1] + hz[2] + hz[3]
+    for k in (1, 2, 3):
+        t = lax.rem(q + k, 4)
+        go_(remote(hdp.at[q], hdp.at[q], hs.at[3 + k], hr.at[3 + k], (t, p)))
+    od[...] = z_sum(0)
+    for n, r, land in ((1, rgu, dgu), (3, rqkv, dqkv)):
+        if n == 3:
+            oo[...] = z_sum(2)
+        s = z_sum(n).reshape(r.shape)
+        r[...] = s.astype(BF)
+        m = n // 2
+        for k in (1, 2, 3):
+            t = lax.rem(q + k, 4)
+            go_(remote(r.at[t], land.at[q], ds_.at[m, k - 1], dr.at[m, k - 1], (t, p)))
+        (ogu if n == 1 else oqkv)[q] = r[q].astype(F32)
+    for n, r, land, o in ((1, rgu, dgu, ogu), (3, rqkv, dqkv, oqkv)):
+        m = n // 2
+        for k in (1, 2, 3):
+            f = lax.rem(q + 4 - k, 4)
+            remote(r.at[0], land.at[f], ds_.at[m, k - 1], dr.at[m, k - 1], (q, p)).wait_recv()
+            o[f] = land[f].astype(F32)
+    for k in (1, 2, 3):
+        f = lax.rem(q + 4 - k, 4)
+        remote(hdp.at[f], hdp.at[f], hs.at[3 + k], hr.at[3 + k], (q, p)).wait_recv()
+    oheads[...] = hdp[0] + hdp[1] + hdp[2] + hdp[3]
+    for a in range(2):
+        for i in range(2):
+            group = 4 * c + 2 * i + x_
+            from_c = p // 4
+            here = jnp.logical_and(group == p, from_c == c)
+
+            @pl.when(jnp.logical_not(here))
+            def _():
+                remote(fin.at[a, 0], outs[a].at[i], fs.at[a, 0], fr.at[a, i], (q, p)).wait_recv()
+
+    for cp in sends:
+        cp.wait_send()
+
+    @pl.when(x_ != owner_x)
+    def _():
+        for a in range(2):
+            remote(own.at[a], l2.at[a], s2.at[a], r2.at[a], opp).wait_send()
+
+    @pl.when(x_ == owner_x)
+    def _():
+        for a in range(2):
+            for n in range(4):
+
+                @pl.when(jnp.logical_not(is_self(n)))
+                def _():
+                    home(a, n).wait_send()
+
+
+def scatter_call(gd, ggu, go, gqkv, heads, part, dpart, order, hidden, dh, x):
+    shape = jax.ShapeDtypeStruct
+    sem = pltpu.SemaphoreType.DMA
+    vm = pltpu.VMEM
+    ggu = ggu.reshape(2, 4, 128, 1536)
+    gqkv = gqkv.reshape(2, 4, 128, WIDTH)
+
+    def y_land(g):
+        return vm(g.shape[1:], BF)
+
+    def z_land(g):
+        return vm((3,) + g.shape[2:], BF)
+
+    return pl.pallas_call(
+        scatter_kernel,
+        out_shape=(
+            shape((2, 128, WIDTH), BF),
+            shape((2, 128, WIDTH), BF),
+            shape((96, WIDTH), F32),
+            shape((4, 32, 1536), F32),
+            shape((64, WIDTH), F32),
+            shape((4, 32, WIDTH), F32),
+            shape((8, 128), F32),
+        ),
+        in_specs=[VM] * 7 + [SM] + [VM] * 3,
+        out_specs=(VM,) * 7,
+        scratch_shapes=[
+            y_land(gd), y_land(ggu), y_land(go), y_land(gqkv),
+            z_land(gd), z_land(ggu), z_land(go), z_land(gqkv),
+            vm((4, 32, 1536), BF), vm((4, 32, WIDTH), BF), vm((4, 32, 1536), BF), vm((4, 32, WIDTH), BF),
+            vm((8, 128), F32), vm((4, 8, 128), F32), vm((4, 8, 128), F32),
+            vm((2, 512, WIDTH), BF), vm((2, 512, WIDTH), BF), vm((2, 512, WIDTH), BF),
+            vm((2, 4, 128, WIDTH), BF),
+            sem((4,)), sem((4,)), sem((4, 3)), sem((4, 3)), sem((2, 3)), sem((2, 3)), sem((7,)), sem((7,)),
+            sem((2,)), sem((2,)), sem((2,)), sem((2,)), sem((2, 4)), sem((2, 2)), sem((2,)),
+        ],
+        compiler_params=pltpu.CompilerParams(
+            collective_id=3, has_side_effects=True, vmem_limit_bytes=VMEM_BYTES
+        ),
+        name="scatter_layer",
+    )(
+        gd, ggu, go, gqkv, heads, part, dpart, order,
+        hidden.reshape(16, BLK, WIDTH), dh.reshape(16, BLK, WIDTH), x,
+    )
+
+
+def quarter_columns(w, gain):
+    rows, cols = w.shape
+    v = w if gain is None else (w.astype(F32) * gain).astype(BF)
+    return jnp.transpose(v.reshape(rows, 4, cols // 4), (1, 0, 2))
+
+
+def whole_sequences(
+    tokens, attn_gain, w_query, key_projection, value_projection, query_head_gain, key_gain, w_out,
+    mlp_gain, w_gate, w_up, w_down, cotangent, span_order,
+):
+    p = lax.axis_index("seq")
+    ga = attn_gain.astype(F32)[:, None]
+    gm = mlp_gain.astype(F32)[:, None]
+    pq = jnp.concatenate(
+        [quarter_columns(w, ga) for w in (w_query, key_projection, value_projection)], axis=2
+    )
+    pg = jnp.concatenate([quarter_columns(w, gm) for w in (w_gate, w_up)], axis=2)
+    row = jnp.where(lax.rem(p // 2, 2) == 0, span_order[0], span_order[1])
+    spots = lax.iota(jnp.int32, 16)
+    inverse = jnp.sum(jnp.where(row[None, :] == spots[:, None], spots[None, :], 0), axis=1)
+    pos = jnp.zeros((8, 128), jnp.int32)
+    pos = pos.at[0, :16].set(row).at[1, :16].set(inverse)
+    xf, cf, of, wq, wg, wo, wd = gather_call(tokens, cotangent, pos, pq, pg, w_out, w_down)
+    order = of[0, :16]
+    inv = of[1, :16]
+    x = xf.reshape(TOKENS, WIDTH)
+    cot = cf.reshape(TOKENS, WIDTH)
+    w = wq.reshape(WIDTH, WIDTH)
+    wgu = wg.reshape(WIDTH, 1536)
+    wo = wo.reshape(512, WIDTH)
+    wd = wd.reshape(768, WIDTH)
+    freqs = BASE ** (-(lax.iota(F32, HEAD_SIZE // 2) * 2.0) / HEAD_SIZE)
+    angles = lax.iota(F32, TOKENS)[:, None] * freqs[None, :]
+    cosine = jnp.cos(angles)
+    sine = jnp.sin(angles)
+    cosf = jnp.concatenate([cosine, cosine], axis=1)
+    sinf = jnp.concatenate([-sine, sine], axis=1)
+    qg = query_head_gain.astype(F32)[None, :]
+    kg = key_gain.astype(F32)[None, :]
+    xhat, raw, qb, kb, vb, ob, lse, part1 = forward_call(inv, x, w, cosf, sinf, qg, kg, wo)
+    total = allsum(part1, 1)
+    hidden, part2, dpart, gd, ggu = mlp_call(inv, order, x, total, cot, wgu, wd)
+    dtotal = allsum(dpart, 2)
+    dh, go, gqkv, part3, heads = backward_call(
+        inv, order, cot, hidden, dtotal, wo, w, xhat, raw, qb, kb, vb, ob, lse, cosf, sinf, qg, kg
+    )
+    out, igrad, od, ogu, oo, oqkv, oheads = scatter_call(
+        gd, ggu, go, gqkv, heads, part2, part3, order, hidden, dh, x
+    )
+    return finish(
+        out, igrad, od, ogu, oo, oqkv, oheads, ga, gm, w_query, key_projection, value_projection, w_gate, w_up
+    )
+
+
+def finish(out, igrad, od, ogu, oo, oqkv, oheads, ga, gm, w_query, key_projection, value_projection, w_gate, w_up):
+    def join(part):
+        return jnp.transpose(part, (1, 0, 2)).reshape(part.shape[1], -1)
+
+    hq, hk, hv = join(oqkv[:, :, :512]), join(oqkv[:, :, 512:768]), join(oqkv[:, :, 768:])
+    hg, hu = join(ogu[:, :, :768]), join(ogu[:, :, 768:])
+
+    def along(w, h):
+        return jnp.sum(w.astype(F32) * h, axis=1)
+
+    grad_attn_gain = along(w_query, hq) + along(key_projection, hk) + along(value_projection, hv)
+    grad_mlp_gain = along(w_gate, hg) + along(w_up, hu)
+    return (
+        out,
+        igrad,
+        grad_attn_gain,
+        ga * hq,
+        ga * hk,
+        ga * hv,
+        oheads[0],
+        oheads[1],
+        oo,
+        grad_mlp_gain,
+        gm * hg,
+        gm * hu,
+        od,
+    )
+
+
+def layer(tokens, *rest):
+    whole = (
+        lax.axis_size("dp") == 4
+        and lax.axis_size("seq") == 8
+        and tokens.shape == (2, 128, WIDTH)
+        and rest[-1].shape == (2, 16)
+    )
+    return (whole_sequences if whole else shards)(tokens, *rest)
+
+
 def solution(mesh):
     return jax.shard_map(
-        shards,
+        layer,
         mesh=mesh,
         in_specs=(
             P("dp", "seq", None),

time: 2470 us -> 559 us (0.23)
  waiting for transfers between devices: 1540 us -> 0 us
  Pallas kernels: 0 us -> 532 us
  local copies, waits for them, and re-layouts: 359 us -> 7.95 us
  matrix products: 276 us -> 0 us
  blocking collectives: 94.1 us -> 0 us
  starting transfers between devices: 90.7 us -> 0 us
  other arithmetic: 73 us -> 16 us
    unnamed x13 -> x0, waiting for transfers between devices: 861 us -> none
    pallas_call x0 -> x7, Pallas kernels: none -> 532 us  [the longest x1 242 us: scatter_call(): pl.pallas_call(scatter_kernel, out_shape=(shape((2, 128, WIDTH), BF), sha...]
    all_gather x11 -> x0, waiting for transfers between devices: 529 us -> none  [the longest x2 87.2 us: shards(): piece_v = lax.all_gather(value_reduced, 'seq', axis=1, tiled=True)]
    dot_general x126 -> x0, matrix products: 276 us -> none  [the longest x14 85.6 us: row_product(): lax.dot_general(left, right, (((0,), (0,)), ((), ())), preferred_element_...]
    ppermute x64 -> x0, waiting for transfers between devices: 148 us -> none  [from_behind(): return lax.ppermute(block, axis, route)]
    unnamed x262 -> x29, local copies, waits for them, and re-layouts: 148 us -> 5.1 us
    reshape x19 -> x6, local copies, waits for them, and re-layouts: 130 us -> 0.11 us  [the longest x5 0.09 us: join(): return jnp.transpose(part, (1, 0, 2)).reshape(part.shape[1], -1)]
    ppermute x64 -> x0, starting transfers between devices: 90.3 us -> none  [from_behind(): return lax.ppermute(block, axis, route)]
  transfers between devices with their start and end apart: 76 -> 0, of which waited for: 56 -> 0; matrix products, arithmetic and copies ran while one was open for 9% -> 0% of each run, Pallas kernels for 0% -> 0%
where the time goes in v1:
time: 559 us; the launch traced here: 556 us
  Pallas kernels  532 us (95%)
  other arithmetic  16 us (3%)
  local copies, waits for them, and re-layouts  7.95 us (1%)
    pallas_call x1, Pallas kernels, scatter_call(): pl.pallas_call(scatter_kernel, out_shape=(shape((2, 128, WIDTH), BF), sha...  242 us
    pallas_call x1, Pallas kernels, gather_call(): pl.pallas_call(gather_kernel, out_shape=(shape((8, 128, WIDTH), BF), shap...  142 us
    pallas_call x2, Pallas kernels, allsum(): pl.pallas_call(allsum_kernel, out_shape=jax.ShapeDtypeStruct((TOKENS, WID...  65.5 us
    pallas_call x1, Pallas kernels, backward_call(): pl.pallas_call(backward_kernel, out_shape=(shape((TOKENS, WIDTH), F32), s...  35.2 us
    pallas_call x1, Pallas kernels, mlp_call(): pl.pallas_call(mlp_kernel, out_shape=(shape((TOKENS, WIDTH), F32), shape(...  26.9 us
    pallas_call x1, Pallas kernels, forward_call(): pl.pallas_call(forward_kernel, out_shape=(shape((TOKENS, WIDTH), BF), sha...  20 us

profile of v1, /device:TPU:27, one launch (start us, length us, event | category | flops | bytes accessed | tf_op | source)
XLA Modules:
  0.0 556.5 jit_solution(11220520228453724060)
XLA Ops:
  0.7 0.7 convert_element_type.44
  1.3 0.7 convert_element_type.51
  2.0 0.8 fusion.13
  2.7 0.8 broadcast_select_fusion
  3.6 1.2 bitcast_convert_fusion
  5.0 1.0 fusion.6
  6.0 1.0 fusion.9
  7.0 0.7 pad_maximum_fusion.3.pq
  7.7 1.2 fusion.2
  8.9 0.8 pad_maximum_fusion.2.pg
  9.7 2.0 fusion.8
  11.7 1.3 pad_maximum_fusion
  13.0 142.3 %gather_layer.1 = (bf16[8,128,1024]{2,1,0:T(8,128)(2,1)}, bf16[8,128,1024]{2,1,0:T(8,128)(2,1)}, s32[8,128]{1,0:T(8,128)}, bf16[4,8,32,1024]{3,2,1,0:T(8,128)(2,...) custom-call(bf16[2,128,1024]{2,1,0:T(8,128)(2,1)} %tok.1, ...), custom_call_target="tpu_custom_call" | custom-call | tf_op jit(solution)/shard_map/gather_layer/pallas_call | solution.py:594
  155.3 1.3 slice_bitcast_fusion.7
  156.6 20.0 %attention_forward.1 = (bf16[1024,1024]{1,0:T(8,128)(2,1)}, f32[1024,768]{1,0:T(8,128)}, bf16[4,1024,128]{2,1,0:T(8,128)(2,1)}, bf16[2,1024,128]{2,1,0:T(8,128)(...) custom-call(s32[16]{0:T(128)} %get-tuple-element.118.inv, ...), custom_call_target="tpu_custom_call" | custom-call | tf_op jit(solution)/shard_map/attention_forward/pallas_call | solution.py:739
  176.6 34.2 %sum_quarters_1.1.total = bf16[1024,1024]{1,0:T(8,128)(2,1)} custom-call(bf16[1024,1024]{1,0:T(8,128)(2,1)} %get-tuple-element.73.part), custom_call_target="tpu_custom_call" | custom-call | tf_op jit(solution)/shard_map/sum_quarters_1/pallas_call | solution.py:650
  210.7 26.9 %feed_forward_both.1 = (f32[1024,1024]{1,0:T(8,128)}, bf16[1024,1024]{1,0:T(8,128)(2,1)}, bf16[1024,1024]{1,0:T(8,128)(2,1)}, bf16[2,4,96,1024]{3,2,1,0:T(8,128)(2,1)}, bf16[2,4,4,32,1536]{4,3,2,1,0:T(8,128)(2,1)}) custom-call(s32[16]{0:T(128)} %get-tuple-element.118.inv, s32[16]{0:T(128)} %get-tuple-element.117.order, bf16[1024,1024]{1,0:T(8,128)(2,1)} %bitcast.75, ...), custom_call_target="tpu_custom_call" | custom-call | tf_op jit(solution)/shard_map/feed_forward_both/pallas_call | solution.py:803
  237.6 31.3 %sum_quarters_2.1.dtotal = bf16[1024,1024]{1,0:T(8,128)(2,1)} custom-call(bf16[1024,1024]{1,0:T(8,128)(2,1)} %get-tuple-element.80.part), custom_call_target="tpu_custom_call" | custom-call | tf_op jit(solution)/shard_map/sum_quarters_2/pallas_call | solution.py:650
  268.9 35.2 %attention_backward.1 = (f32[1024,1024]{1,0:T(8,128)}, bf16[2,4,64,1024]{3,2,1,0:T(8,128)(2,1)}, bf16[2,4,4,32,1024]{4,3,2,1,0:T(8,128)(2,1)}, bf16[1024,1024]{1,0:T(8,128)(2,1)}, f32[8,128]{1,0:T(8,128)}) custom-call(s32[16]{0:T(128)} %get-tuple-element.118.inv, s32[16]{0:T(128)} %get-tuple-element.117.order, bf16[1024,1024]{1,0:T(8,128)(2,1)} %bitcast.81, ...), custom_call_target="tpu_custom_call" | custom-call | tf_op jit(solution)/shard_map/attention_backward/pallas_call | solution.py:907
  304.2 241.7 %scatter_layer.1 = (bf16[2,128,1024]{2,1,0:T(8,128)(2,1)}, bf16[2,128,1024]{2,1,0:T(8,128)(2,1)}, f32[96,1024]{1,0:T(8,128)}, f32[4,32,1536]{2,1,0:T(8,128)}, f3...) custom-call(bf16[2,4,96,1024]{3,2,1,0:T(8,128)(2,1)} %get-tuple-element.77.gd, ...), custom_call_target="tpu_custom_call" | custom-call | tf_op jit(solution)/shard_map/scatter_layer/pallas_call | solution.py:1111
  545.9 1.3 slice_bitcast_fusion.5
  547.2 1.0 slice_bitcast_fusion.2
  548.2 1.0 slice_bitcast_fusion.4
  549.2 0.9 broadcast_multiply_fusion.2
  550.2 0.9 broadcast_multiply_fusion.3
  551.1 0.5 add_add_fusion
  551.8 1.1 broadcast_multiply_fusion
  552.9 0.5 add.18
  553.4 0.8 copy.68
  554.2 0.8 copy.69
  555.0 0.7 copy.70
  555.7 0.7 copy.71
  (35 shorter events, 0.5 us)
Async XLA Ops:
  5.0 6.7 %copy-start.10 = (s32[8,128]{1,0:T(8,128)}, s32[8,128]{1,0:T(8,128)S(1)}, u32[]{:S(2)}) copy-start(s32[8,128]{1,0:T(8,128)S(1)} %scatter.9.pos) | copy-start | bytes 12292
  304.2 245.0 %copy-start.3 = (bf16[32,2048]{1,0:T(8,128)(2,1)S(1)}, bf16[32,2048]{1,0:T(8,128)(2,1)}, u32[]{:S(2)}) copy-start(bf16[32,2048]{1,0:T(8,128)(2,1)} %param.20) | copy-start | bytes 393220
  545.9 4.3 copy-start.8
  545.9 4.3 copy-start.9
  545.9 5.7 %copy-start = (f32[4,32,1536]{2,1,0:T(8,128)S(1)}, f32[4,32,1536]{2,1,0:T(8,128)}, u32[]{:S(2)}) copy-start(f32[4,32,1536]{2,1,0:T(8,128)} %get-tuple-element.99) | copy-start | bytes 2359300
  550.1 1.6 copy-start.1
  550.1 1.6 copy-start.2
  551.7 1.8 copy-start.5
  551.7 2.5 copy-start.4
  551.7 3.3 copy-start.7
  551.8 3.9 copy-start.6

commit v2 on v0

--- a/solution.py
+++ b/solution.py
@@ -2,6 +2,9 @@
 import jax.numpy as jnp
 from jax import lax
 from jax.sharding import PartitionSpec as P
+
+from jax.experimental import pallas as pl
+from jax.experimental.pallas import tpu as pltpu
 
 QUERY_HEADS = 16
 KEY_VALUE_HEADS = 8
@@ -356,9 +359,1008 @@
     )
 
 
+BF = jnp.bfloat16
+F32 = jnp.float32
+MESH = pl.DeviceIdType.MESH
+TOKENS = 1024
+WIDTH = 1024
+LOG2E = 1.4426950408889634
+VM = pl.BlockSpec(memory_space=pltpu.VMEM)
+SM = pl.BlockSpec(memory_space=pltpu.SMEM)
+ANY = pl.BlockSpec(memory_space=pl.ANY)
+VMEM_BYTES = 65100 * 1024
+
+
+def place():
+    q = lax.axis_index("dp")
+    p = lax.axis_index("seq")
+    return q, p, q // 2, lax.rem(q, 2), p // 2, lax.rem(p, 2)
+
+
+def greet(peers):
+    barrier = pltpu.get_barrier_semaphore()
+    for peer in peers:
+        pl.semaphore_signal(barrier, inc=1, device_id=peer, device_id_type=MESH)
+    pl.semaphore_wait(barrier, len(peers))
+
+
+def remote(src, dst, send, recv, peer):
+    return pltpu.make_async_remote_copy(
+        src_ref=src, dst_ref=dst, send_sem=send, recv_sem=recv, device_id=peer, device_id_type=MESH
+    )
+
+
+def dims(left, right, lc, rc):
+    return lax.dot_general(left, right, (((lc,), (rc,)), ((), ())), preferred_element_type=F32)
+
+
+def mod(a, n):
+    return a % n
+
+
+def unit(v):
+    return lax.rsqrt(jnp.mean(v * v, axis=-1, keepdims=True) + EPS)
+
+
+def pieces(ref, spots, which, first, count):
+    return jnp.concatenate([ref[spots[which, first + t]] for t in range(count)], axis=0)
+
+
+def rotate(v, cosine, sine):
+    return v * cosine + pltpu.roll(v, HEAD_SIZE // 2, 1) * sine
+
+
+def rotate_back(v, cosine, sine):
+    return v * cosine + pltpu.roll(v * sine, HEAD_SIZE // 2, 1)
+
+
+def lower(s, fill):
+    n = s.shape[0]
+    i = lax.broadcasted_iota(jnp.int32, (n, n), 0)
+    j = lax.broadcasted_iota(jnp.int32, (n, n), 1)
+    width = s.shape[1]
+    diag = jnp.where(j <= i, s[:, width - n :], fill)
+    return diag if width == n else jnp.concatenate([s[:, : width - n], diag], axis=1)
+
+
+class Sum:
+    def __init__(self, part, total, l1, own, l2, sems, base):
+        self.q, self.p, self.x, self.c, _, _ = place()
+        self.part, self.total, self.l1, self.own, self.l2 = part, total, l1, own, l2
+        self.sems, self.base = sems, base
+        self.sib = (2 * self.x + 1 - self.c, self.p)
+        self.opp = (2 * (1 - self.x) + self.c, self.p)
+
+    def rows(self, n, c):
+        return pl.ds(pl.multiple_of(n * 256 + c * 128, 128), 128)
+
+    def copy(self, step, n):
+        s, r = self.sems.at[self.base + 2 * step, n], self.sems.at[self.base + 2 * step + 1, n]
+        mine = self.rows(n, self.c)
+        if step == 0:
+            return remote(self.part.at[self.rows(n, 1 - self.c)], self.l1.at[n], s, r, self.sib)
+        if step == 1:
+            return remote(self.own.at[n], self.l2.at[n], s, r, self.opp)
+        return remote(self.total.at[mine], self.total.at[mine], s, r, self.sib)
+
+    def beside(self, n):
+        self.copy(0, n).start()
+
+    def across(self, n):
+        self.copy(0, n).wait_recv()
+        mine = self.part[self.rows(n, self.c), :].astype(F32)
+        self.own[n] = (mine + self.l1[n].astype(F32)).astype(BF)
+        self.copy(1, n).start()
+
+    def back(self, n):
+        self.copy(1, n).wait_recv()
+        self.total[self.rows(n, self.c), :] = (self.own[n].astype(F32) + self.l2[n].astype(F32)).astype(BF)
+        self.copy(2, n).start()
+
+    def ready(self, n):
+        other = self.rows(n, 1 - self.c)
+        s, r = self.sems.at[self.base + 4, n], self.sems.at[self.base + 5, n]
+        remote(self.total.at[other], self.total.at[other], s, r, self.sib).wait_recv()
+
+    def close(self):
+        @pl.loop(0, 4)
+        def _(n):
+            for step in range(3):
+                self.copy(step, n).wait_send()
+
+
+def block(ref, b):
+    return ref.at[pl.ds(2 * b, 2)]
+
+
+class Gather:
+    def __init__(self, srcs, dsts, sems):
+        self.q, self.p, self.x, self.c, self.z, self.y = place()
+        self.tok, self.cot, self.pos, self.pq, self.pg, self.po, self.pd = srcs
+        self.xf, self.cf, self.of, *self.w = dsts
+        (self.loc, self.ts, self.tr, self.fs, self.fr, self.ps, self.pr,
+         self.as_, self.ar, self.zs, self.zr, self.ys, self.yr) = sems
+        q, p, x, c, z, y = self.q, self.p, self.x, self.c, self.z, self.y
+        self.owner_x, self.owner_c = y, z // 2
+        self.is_owner = jnp.logical_and(x == self.owner_x, c == self.owner_c)
+        self.cross = jnp.logical_and(x != self.owner_x, c == self.owner_c)
+        self.sib = (2 * x + 1 - c, p)
+        self.opp = (2 * (1 - x) + c, p)
+
+    def peers(self):
+        q, p = self.q, self.p
+        return [(mod(q + k, 4), p) for k in (1, 2, 3)] + [(q, mod(p + k, 8)) for k in range(1, 8)]
+
+    def col(self, n):
+        return (self.pq, self.pg)[n], self.w[n]
+
+    def own_copy(self, n):
+        q, p = self.q, self.p
+        if n < 2:
+            src, dst = self.col(n)
+            return pltpu.make_async_copy(src.at[q], dst.at[q, p], self.loc.at[n])
+        return pltpu.make_async_copy((self.po, self.pd)[n - 2], self.w[n].at[p], self.loc.at[n])
+
+    def column_copy(self, n, k):
+        q, p = self.q, self.p
+        src, dst = self.col(n)
+        t = mod(q + k, 4)
+        return remote(src.at[t], dst.at[q, p], self.as_.at[n, k - 1], self.ar.at[n, k - 1], (t, p))
+
+    def column_start(self, n):
+        for k in (1, 2, 3):
+            self.column_copy(n, k).start()
+
+    def column_wait(self, n):
+        q, p = self.q, self.p
+        src, dst = self.col(n)
+        for k in (1, 2, 3):
+            f = mod(q + 4 - k, 4)
+            remote(src.at[0], dst.at[f, p], self.as_.at[n, k - 1], self.ar.at[n, k - 1], (q, p)).wait_recv()
+
+    def view(self, n, chunk):
+        return self.w[n].at[:, chunk] if n < 2 else self.w[n].at[chunk]
+
+    def z_copy(self, n, k):
+        t = mod(self.z + k, 4)
+        v = self.view(n, self.p)
+        return remote(v, v, self.zs.at[n, k - 1], self.zr.at[n, k - 1], (self.q, 2 * t + self.y))
+
+    def z_send(self, n):
+        for k in (1, 2, 3):
+            self.z_copy(n, k).start()
+
+    def y_copy(self, n, k):
+        v = self.view(n, 2 * mod(self.z + 4 - k, 4) + self.y)
+        return remote(v, v, self.ys.at[n, k], self.yr.at[n, k], (self.q, 2 * self.z + 1 - self.y))
+
+    def y_send(self, n, k):
+        self.y_copy(n, k).start()
+
+    def z_wait(self, n, k):
+        v = self.view(n, 2 * mod(self.z + 4 - k, 4) + self.y)
+        remote(v, v, self.zs.at[n, k - 1], self.zr.at[n, k - 1], (self.q, self.p)).wait_recv()
+
+    def y_wait(self, n):
+        for k in range(4):
+            v = self.view(n, 2 * mod(self.z + 4 - k, 4) + 1 - self.y)
+            remote(v, v, self.ys.at[n, k], self.yr.at[n, k], (self.q, self.p)).wait_recv()
+
+    def pass_on(self, n, k):
+        self.z_wait(n, k)
+        self.y_send(n, k)
+
+    def tok_dst(self, a):
+        return (self.xf, self.cf)[a]
+
+    def token_copy(self, a, i):
+        src, dst = (self.tok, self.cot)[a], self.tok_dst(a)
+        goal = 4 * self.c + 2 * i + self.x
+        return goal, remote(src.at[i], block(dst, self.p), self.ts.at[a, i], self.tr.at[a, self.p], (self.q, goal))
+
+    def token_local(self, a, i):
+        return pltpu.make_async_copy((self.tok, self.cot)[a].at[i], block(self.tok_dst(a), self.p), self.loc.at[4 + a])
+
+    def token_start(self, a):
+        for i in range(2):
+            goal, cp = self.token_copy(a, i)
+
+            @pl.when(goal != self.p)
+            def _():
+                cp.start()
+
+            @pl.when(goal == self.p)
+            def _():
+                self.token_local(a, i).start()
+
+    def token_pass(self, a, first=0, end=8):
+        dst = self.tok_dst(a)
+        q, p = self.q, self.p
+
+        @pl.when(self.is_owner)
+        def _():
+            @pl.loop(first, end)
+            def _(b):
+                @pl.when(b != p)
+                def _():
+                    remote(block(dst, b), block(dst, b), self.ts.at[a, 0], self.tr.at[a, b], (q, p)).wait_recv()
+
+                @pl.when(b == p)
+                def _():
+                    self.token_local(a, 0).wait()
+
+                remote(block(dst, b), block(dst, b), self.fs.at[a, 0, b], self.fr.at[a, b], self.sib).start()
+                remote(block(dst, b), block(dst, b), self.fs.at[a, 1, b], self.fr.at[a, b], self.opp).start()
+
+        @pl.when(jnp.logical_not(self.is_owner))
+        def _():
+            @pl.loop(first, end)
+            def _(b):
+                remote(block(dst, b), block(dst, b), self.fs.at[a, 0, b], self.fr.at[a, b], self.sib).wait_recv()
+
+                @pl.when(self.cross)
+                def _():
+                    remote(block(dst, b), block(dst, b), self.fs.at[a, 0, b], self.fr.at[a, b], self.sib).start()
+
+    def token_close(self, a):
+        dst = self.tok_dst(a)
+        q, p = self.q, self.p
+        for i in range(2):
+            goal, cp = self.token_copy(a, i)
+
+            @pl.when(goal != p)
+            def _():
+                cp.wait_send()
+
+        @pl.when(self.is_owner)
+        def _():
+            @pl.loop(0, 8)
+            def _(b):
+                remote(block(dst, b), block(dst, b), self.fs.at[a, 0, b], self.fr.at[a, b], (q, p)).wait_send()
+                remote(block(dst, b), block(dst, b), self.fs.at[a, 1, b], self.fr.at[a, b], (q, p)).wait_send()
+
+        @pl.when(self.cross)
+        def _():
+            @pl.loop(0, 8)
+            def _(b):
+                remote(block(dst, b), block(dst, b), self.fs.at[a, 0, b], self.fr.at[a, b], (q, p)).wait_send()
+
+    def pos_copy(self, k):
+        return remote(self.pos, self.of, self.ps.at[k], self.pr.at[0], (mod(self.q + k + 1, 4), self.p))
+
+    def pos_start(self):
+        @pl.when(self.is_owner)
+        def _():
+            pltpu.make_async_copy(self.pos, self.of, self.loc.at[6]).start()
+            for k in range(3):
+                self.pos_copy(k).start()
+
+    def pos_finish(self):
+        @pl.when(self.is_owner)
+        def _():
+            pltpu.make_async_copy(self.pos, self.of, self.loc.at[6]).wait()
+            for k in range(3):
+                self.pos_copy(k).wait_send()
+
+        @pl.when(jnp.logical_not(self.is_owner))
+        def _():
+            self.pos_copy(0).wait_recv()
+
+    def close(self):
+        for n in range(4):
+            for k in (1, 2, 3):
+                if n < 2:
+                    self.column_copy(n, k).wait_send()
+                self.z_copy(n, k).wait_send()
+            for k in range(4):
+                self.y_copy(n, k).wait_send()
+        self.token_close(0)
+        self.token_close(1)
+
+
+GATHER_SEMS = ((7,), (2, 2), (2, 8), (2, 2, 8), (2, 8), (3,), (1,), (2, 3), (2, 3), (4, 3), (4, 3), (4, 4), (4, 4))
+
+
+def first_kernel(
+    tok, cot, pos, pq, pg, po, pd, cosf, sinf, qg, kg,
+    xf, of, wq, wo, xhat, raw_o, qb, kb, vb, ob, lse, hidden, cs, part2, dtotal, gd, ggu,
+    cf, wg, wd, part1, total, dpart, a2, mb, dgu, l1, own, l2, l1b, ownb, l2b, sorts, sorts_sem, sums, *sems,
+):
+    g = Gather((tok, cot, pos, pq, pg, po, pd), (xf, cf, of, wq, wg, wo, wd), sems)
+    greet(g.peers())
+    g.pos_start()
+    g.column_start(0)
+    g.token_start(0)
+    for n in range(4):
+        g.own_copy(n).start()
+    g.column_start(1)
+    g.own_copy(0).wait()
+    g.column_wait(0)
+    g.z_send(0)
+    g.y_send(0, 0)
+    g.pos_finish()
+    sort = pltpu.make_async_copy(of, sorts, sorts_sem.at[0])
+    sort.start()
+    g.token_pass(0, 0, 4)
+    for k in (1, 3, 2):
+        g.pass_on(0, k)
+    g.own_copy(2).wait()
+    g.z_send(2)
+    g.y_send(2, 0)
+    g.token_pass(0, 4, 8)
+    g.own_copy(1).wait()
+    g.column_wait(1)
+    g.z_send(1)
+    g.y_send(1, 0)
+    g.own_copy(3).wait()
+    g.z_send(3)
+    g.y_send(3, 0)
+    g.token_start(1)
+    sort.wait()
+    g.y_wait(0)
+
+    @pl.loop(0, 4)
+    def _(n):
+        rows = pl.ds(pl.multiple_of(n * 256, 256), 256)
+        v = pieces(xf, sorts, 1, n * 4, 4).astype(F32)
+        h = (v * unit(v)).astype(BF)
+        xhat[rows, :] = h
+        raw = jnp.dot(h, wq[...].reshape(WIDTH, WIDTH), preferred_element_type=F32)
+        raw_o[rows, :] = raw[:, :768]
+        cosine = cosf[rows, :]
+        sine = sinf[rows, :]
+        for t in range(2):
+            vb[t, rows, :] = raw[:, 768 + t * 128 : 896 + t * 128].astype(BF)
+        for t in range(6):
+            u = raw[:, t * 128 : (t + 1) * 128]
+            n_ = u * unit(u) * (qg[...] if t < 4 else kg[...])
+            r = rotate(n_, cosine, sine).astype(BF)
+            if t < 4:
+                qb[t, rows, :] = r
+            else:
+                kb[t - 4, rows, :] = r
+
+    @pl.loop(0, 4)
+    def _(h):
+        for turn, todo in enumerate((((2, 1), (2, 3), (2, 2)), ((1, 1),), ((1, 3),), ((1, 2),))):
+
+            @pl.when(h == turn)
+            def _():
+                for n, k in todo:
+                    g.pass_on(n, k)
+
+        kv = h // 2
+        for i in range(4):
+            length = (i + 1) * 256
+            rows = slice(i * 256, length)
+            s = dims(qb[h, rows, :], kb[kv, :length, :], 1, 1) * (HEAD_SIZE**-0.5 * LOG2E)
+            s = lower(s, NEGATIVE_FILL)
+            top = jnp.max(s, axis=-1, keepdims=True)
+            e = jnp.exp2(s - top)
+            sum_e = jnp.sum(e, axis=-1, keepdims=True)
+            o = jnp.dot(e.astype(BF), vb[kv, :length, :], preferred_element_type=F32) / sum_e
+            ob[rows, pl.ds(pl.multiple_of(h * 128, 128), 128)] = o.astype(BF)
+            lse[h, rows, :] = top + jnp.log2(sum_e)
+
+    g.y_wait(2)
+    s1 = Sum(part1, total, l1, own, l2, sums, 0)
+    s2 = Sum(dpart, dtotal, l1b, ownb, l2b, sums, 6)
+
+    @pl.loop(0, 4)
+    def _(n):
+        rows = pl.ds(pl.multiple_of(n * 256, 256), 256)
+        out_w = wo[...].reshape(512, WIDTH)
+        part1[rows, :] = jnp.dot(ob[rows, :], out_w, preferred_element_type=F32).astype(BF)
+        s1.beside(n)
+
+        @pl.when(n > 0)
+        def _():
+            s1.across(n - 1)
+
+    s1.across(3)
+    for k in (1, 3, 2):
+        g.pass_on(3, k)
+    s1.back(0)
+    g.token_pass(1)
+    g.y_wait(1)
+    g.y_wait(3)
+
+    @pl.loop(0, 4)
+    def _(n):
+        s1.ready(n)
+
+        @pl.when(n < 3)
+        def _():
+            s1.back(n + 1)
+
+        rows = pl.ds(pl.multiple_of(n * 256, 256), 256)
+        h = pieces(xf, sorts, 1, n * 4, 4).astype(F32) + total[rows, :].astype(F32)
+        hidden[rows, :] = h
+        a = (h * unit(h)).astype(BF)
+        a2[rows, :] = a
+        wgu = wg[...].reshape(WIDTH, 1536)
+        gu = jnp.dot(a, wgu, preferred_element_type=F32)
+        gate = gu[:, :768]
+        up = gu[:, 768:]
+        sig = 1.0 / (1.0 + jnp.exp2(gate * -LOG2E))
+        silu = gate * sig
+        mb[pl.ds(n * 4, 4)] = (silu * up).astype(BF).reshape(4, BLK, 768)
+        cc = pieces(cf, sorts, 1, n * 4, 4)
+        cs[rows, :] = cc
+        dm = dims(cc, wd[...].reshape(768, WIDTH), 1, 1)
+        dg = (dm * up * sig * (1.0 + gate * (1.0 - sig))).astype(BF)
+        du = (dm * silu).astype(BF)
+        both = jnp.concatenate([dg, du], axis=1)
+        dgu[rows, :] = both
+        dpart[rows, :] = dims(both, wgu, 1, 1).astype(BF)
+        s2.beside(n)
+
+        @pl.when(n > 0)
+        def _():
+            s2.across(n - 1)
+
+    s2.across(3)
+
+    @pl.loop(0, 2)
+    def _(n):
+        m_all = mb[...].reshape(TOKENS, 768)
+        for t in range(2):
+
+            @pl.when(n == t)
+            def _():
+                v = dims(m_all[:, t * 384 : (t + 1) * 384], cs[...], 0, 0).astype(BF)
+                v = v.reshape(2, 2, 96, WIDTH)
+                for u in range(2):
+                    gd[u, 2 * t : 2 * t + 2] = v[:, u]
+
+        s2.back(n)
+
+    @pl.loop(0, 4)
+    def _(n):
+        v = dims(a2[:, pl.ds(pl.multiple_of(n * 256, 256), 256)], dgu[...], 0, 0).astype(BF)
+        v = v.reshape(4, 2, 32, 1536)
+        for t in range(2):
+            ggu[t, n] = v[:, t]
+
+        @pl.when(n < 2)
+        def _():
+            s2.back(n + 2)
+
+    @pl.loop(0, 4)
+    def _(n):
+        rows = pl.ds(pl.multiple_of(n * 256, 256), 256)
+        m = pieces(mb, sorts, 0, n * 4, 4)
+        part2[rows, :] = jnp.dot(m, wd[...].reshape(768, WIDTH), preferred_element_type=F32).astype(BF)
+
+    for n in range(4):
+        s2.ready(n)
+    s1.close()
+    s2.close()
+    g.close()
+
+
+def first_call(tok, cot, pos, pq, pg, po, pd, cosf, sinf, qg, kg):
+    sem = pltpu.SemaphoreType.DMA
+    shape = jax.ShapeDtypeStruct
+    vm = pltpu.VMEM
+    full = (TOKENS, WIDTH)
+    return pl.pallas_call(
+        first_kernel,
+        out_shape=(
+            shape((16, BLK, WIDTH), BF),
+            shape((8, 128), jnp.int32),
+            shape((4, 8) + pq.shape[1:], BF),
+            shape((8,) + po.shape, BF),
+            shape(full, BF),
+            shape((TOKENS, 768), F32),
+            shape((4, TOKENS, 128), BF),
+            shape((2, TOKENS, 128), BF),
+            shape((2, TOKENS, 128), BF),
+            shape((TOKENS, 512), BF),
+            shape((4, TOKENS, 1), F32),
+            shape(full, F32),
+            shape(full, BF),
+            shape(full, BF),
+            shape(full, BF),
+            shape((2, 4, 96, WIDTH), BF),
+            shape((2, 4, 4, 32, 1536), BF),
+        ),
+        in_specs=[ANY] * 7 + [VM] * 4,
+        out_specs=(VM, ANY) + (VM,) * 15,
+        scratch_shapes=[
+            vm((16, BLK, WIDTH), BF),
+            vm((4, 8) + pg.shape[1:], BF),
+            vm((8,) + pd.shape, BF),
+            vm(full, BF), vm(full, BF), vm(full, BF), vm(full, BF),
+            vm((16, BLK, 768), BF), vm((TOKENS, 1536), BF),
+        ]
+        + [vm((4, 128, WIDTH), BF)] * 6
+        + [pltpu.SMEM((8, 128), jnp.int32), sem((1,)), sem((12, 4))]
+        + [sem(n) for n in GATHER_SEMS],
+        compiler_params=pltpu.CompilerParams(
+            collective_id=0, has_side_effects=True, vmem_limit_bytes=VMEM_BYTES
+        ),
+        name="forward_and_mlp",
+    )(tok, cot, pos, pq, pg, po, pd, cosf, sinf, qg, kg)
+
+
+class Home:
+    def __init__(self, part, out, l1, own, l2, sems, here, base):
+        self.q, self.p, self.x, self.c, self.z, self.y = place()
+        self.part, self.out, self.l1, self.own, self.l2 = part, out, l1, own, l2
+        self.sems, self.here, self.base = sems, here, base
+        self.owner_x, self.owner_c = self.y, self.z // 2
+        self.keeps = self.x == self.owner_x
+        self.sib = (2 * self.x + 1 - self.c, self.p)
+        self.opp = (2 * (1 - self.x) + self.c, self.p)
+        self.goal_q = 2 * self.owner_x + self.owner_c
+
+    def rows(self, n, c):
+        return pl.ds(pl.multiple_of(n * 256 + c * 128, 128), 128)
+
+    def sem(self, k, n):
+        return self.sems.at[self.base + k, n]
+
+    def first(self, n):
+        return remote(
+            self.part.at[self.rows(n, 1 - self.c)], self.l1.at[n], self.sem(0, n), self.sem(1, n), self.sib
+        )
+
+    def second(self, n):
+        return remote(self.own.at[n], self.l2.at[n], self.sem(2, n), self.sem(3, n), self.opp)
+
+    def third(self, n):
+        slot = mod(self.z, 2)
+        return remote(
+            self.own.at[n], self.out.at[slot], self.sem(4, n), self.sem(5, slot), (self.goal_q, 2 * n + self.c)
+        )
+
+    def is_self(self, n):
+        return jnp.logical_and(self.goal_q == self.q, 2 * n + self.c == self.p)
+
+    def beside(self, n):
+        self.first(n).start()
+
+    def across(self, n):
+        self.first(n).wait_recv()
+        mine = self.part[self.rows(n, self.c), :].astype(F32)
+        self.own[n] = (mine + self.l1[n].astype(F32)).astype(BF)
+
+        @pl.when(jnp.logical_not(self.keeps))
+        def _():
+            self.second(n).start()
+
+    def finish(self, n, rest):
+        @pl.when(self.keeps)
+        def _():
+            self.second(n).wait_recv()
+            s = self.own[n].astype(F32) + self.l2[n].astype(F32)
+            self.own[n] = rest(n, s).astype(BF)
+
+            @pl.when(jnp.logical_not(self.is_self(n)))
+            def _():
+                self.third(n).start()
+
+            @pl.when(self.is_self(n))
+            def _():
+                cp = pltpu.make_async_copy(self.own.at[n], self.out.at[mod(self.z, 2)], self.here)
+                cp.start()
+                cp.wait()
+
+    def close(self):
+        for i in range(2):
+            group = 4 * self.c + 2 * i + self.x
+            same = jnp.logical_and(group == self.p, self.y == self.c)
+
+            @pl.when(jnp.logical_not(same))
+            def _():
+                remote(self.own.at[0], self.out.at[i], self.sem(4, 0), self.sem(5, i), (self.q, self.p)).wait_recv()
+
+        for n in range(4):
+            self.first(n).wait_send()
+
+            @pl.when(jnp.logical_not(self.keeps))
+            def _():
+                self.second(n).wait_send()
+
+            @pl.when(jnp.logical_and(self.keeps, jnp.logical_not(self.is_self(n))))
+            def _():
+                self.third(n).wait_send()
+
+
+class Scatter:
+    def __init__(self, g, ly, lz, sems, base):
+        self.q, self.p, _, _, self.z, self.y = place()
+        self.g, self.ly, self.lz, self.sems, self.base = g, ly, lz, sems, base
+
+    def y_copy(self, n):
+        s, r = self.sems.at[self.base + n, 0], self.sems.at[self.base + n, 1]
+        return remote(self.g.at[1 - self.y, n], self.ly.at[n], s, r, (self.q, 2 * self.z + 1 - self.y))
+
+    def z_copy(self, n, k):
+        t = mod(self.z + k, 4)
+        s, r = self.sems.at[self.base + n, 2 * k], self.sems.at[self.base + n, 2 * k + 1]
+        return remote(self.ly.at[n, t], self.lz.at[n, k - 1], s, r, (self.q, 2 * t + self.y))
+
+    def y_send(self, n):
+        self.y_copy(n).start()
+
+    def z_step(self, n):
+        self.y_copy(n).wait_recv()
+
+        @pl.loop(0, 4)
+        def _(t):
+            self.ly[n, t] = (self.ly[n, t].astype(F32) + self.g[self.y, n, t].astype(F32)).astype(BF)
+
+        for k in (1, 2, 3):
+            self.z_copy(n, k).start()
+
+    def z_sum(self, n):
+        for k in (1, 2, 3):
+            self.z_copy(n, k).wait_recv()
+        s = self.ly[n, self.z].astype(F32) + self.lz[n, 0].astype(F32)
+        return s + self.lz[n, 1].astype(F32) + self.lz[n, 2].astype(F32)
+
+    def close(self, count):
+        @pl.loop(0, count)
+        def _(n):
+            self.y_copy(n).wait_send()
+            for k in (1, 2, 3):
+                self.z_copy(n, k).wait_send()
+
+
+class Columns:
+    def __init__(self, scatter, r, land, out, sems, base):
+        self.scatter, self.r, self.land, self.out = scatter, r, land, out
+        self.sems, self.base = sems, base
+        self.q, self.p = scatter.q, scatter.p
+
+    def copy(self, t):
+        s, r = self.sems.at[self.base, t], self.sems.at[self.base + 1, self.q]
+        return remote(self.r.at[t], self.land.at[self.q], s, r, (t, self.p))
+
+    def step(self, t):
+        s = self.scatter.z_sum(t)
+        self.r[t] = s.astype(BF)
+
+        @pl.when(t != self.q)
+        def _():
+            self.copy(t).start()
+
+        @pl.when(t == self.q)
+        def _():
+            self.out[t] = s
+
+    def close(self):
+        @pl.loop(0, 4)
+        def _(t):
+            @pl.when(t != self.q)
+            def _():
+                r = self.sems.at[self.base + 1, t]
+                remote(self.r.at[t], self.land.at[t], self.sems.at[self.base, t], r, (self.q, self.p)).wait_recv()
+                self.out[t] = self.land[t].astype(F32)
+                self.copy(t).wait_send()
+
+
+def second_kernel(
+    spots, gd, ggu, part2, dtotal, hidden, cs, wo, wq, xhat, raw_i, qb, kb, vb, ob, lse, xf, cosf, sinf, qg, kg,
+    out, igrad, od, ogu, oo, oqkv, oheads,
+    dh, dy, dob, dqkv, dkv, go, gqkv, heads,
+    yd, ygu, yo, yqkv, zd, zgu, zo, zqkv, lgu, lqkv, rgu, rqkv, hy, hz, hdp,
+    l1, own, l2, l1b, ownb, l2b,
+    gsem, csem, hs, hr, homes, here,
+):
+    q, p, x_, c, z, y = place()
+    peers = [(2 * x_ + cc, mod(p + k, 8)) for k in range(1, 8) for cc in (0, 1)]
+    peers += [(mod(q + k, 4), p) for k in (1, 2, 3)]
+    greet(peers)
+    sd = Scatter(gd, yd, zd, gsem, 0)
+    sgu = Scatter(ggu, ygu, zgu, gsem, 1)
+    so = Scatter(go, yo, zo, gsem, 5)
+    sqkv = Scatter(gqkv, yqkv, zqkv, gsem, 6)
+    cgu = Columns(sgu, rgu, lgu, ogu, csem, 0)
+    cqkv = Columns(sqkv, rqkv, lqkv, oqkv, csem, 2)
+    h_out = Home(part2, out, l1, own, l2, homes, here.at[0], 0)
+    h_in = Home(dy, igrad, l1b, ownb, l2b, homes, here.at[1], 6)
+    sd.y_send(0)
+    for n in range(4):
+        h_out.beside(n)
+    for n in range(4):
+        sgu.y_send(n)
+
+    @pl.loop(0, 4)
+    def _(n):
+        rows = pl.ds(pl.multiple_of(n * 256, 256), 256)
+        h = hidden[pl.ds(n * 4, 4)].reshape(256, WIDTH)
+        r = unit(h)
+        da = dtotal[rows, :].astype(F32)
+        back = r * da - h * (r * r * r * jnp.mean(h * da, axis=-1, keepdims=True))
+        d = cs[rows, :].astype(F32) + back
+        dh[pl.ds(n * 4, 4)] = d.reshape(4, BLK, WIDTH)
+        low = d.astype(BF)
+        dy[rows, :] = low
+        do = dims(low, wo[...].reshape(512, WIDTH), 1, 1).astype(BF)
+        for t in range(4):
+            dob[t, rows, :] = do[:, t * 128 : (t + 1) * 128]
+        h_out.across(n)
+
+    @pl.loop(0, 2)
+    def _(n):
+        v = dims(ob[:, pl.ds(pl.multiple_of(n * 256, 256), 256)], dy[...], 0, 0).astype(BF)
+        v = v.reshape(2, 2, 64, WIDTH)
+        for t in range(2):
+            go[t, 0, pl.ds(n * 2, 2)] = v[:, t]
+
+    so.y_send(0)
+    heads[...] = jnp.zeros_like(heads)
+    scale = HEAD_SIZE**-0.5
+
+    def norm_back(dn, u, gain, rows):
+        dn = rotate_back(dn, cosf[rows, :], sinf[rows, :])
+        r = unit(u)
+        gd_ = gain * dn
+        du = r * gd_ - u * (r * r * r * jnp.mean(u * gd_, axis=-1, keepdims=True))
+        return du.astype(BF), jnp.sum(dn * u * r, axis=0, keepdims=True)
+
+    def result(n, s):
+        return s + pieces(hidden, spots, 0, 4 * n + 2 * c, 2)
+
+    def inward(n, s):
+        v = xf[pl.ds(4 * n + 2 * c, 2)].reshape(128, WIDTH).astype(F32)
+        r = unit(v)
+        s = r * s - v * (r * r * r * jnp.mean(v * s, axis=-1, keepdims=True))
+        return s + pieces(dh, spots, 0, 4 * n + 2 * c, 2)
+
+    @pl.loop(0, 2)
+    def _(g):
+        dkv[...] = jnp.zeros_like(dkv)
+        for t in range(2):
+            if t == 0:
+
+                @pl.when(g == 0)
+                def _():
+                    sd.z_step(0)
+
+                @pl.when(g == 1)
+                def _():
+                    sgu.z_step(2)
+                    sgu.z_step(3)
+            else:
+
+                @pl.when(g == 0)
+                def _():
+                    sgu.z_step(0)
+                    sgu.z_step(1)
+
+                @pl.when(g == 1)
+                def _():
+                    @pl.loop(0, 4)
+                    def _(n):
+                        h_out.finish(n, result)
+
+            h = g * 2 + t
+            lanes = pl.ds(pl.multiple_of(h * 128, 128), 128)
+            for i in range(4):
+                length = (i + 1) * 256
+                rows = slice(i * 256, length)
+                qv = qb[h, rows, :]
+                kv = kb[g, :length, :]
+                dov = dob[h, rows, :]
+                s = dims(qv, kv, 1, 1) * (scale * LOG2E)
+                pr = lower(jnp.exp2(s - lse[h, rows, :]), 0.0)
+                dp = dims(dov, vb[g, :length, :], 1, 1)
+                delta = jnp.sum(dov.astype(F32) * ob[rows, lanes].astype(F32), axis=-1, keepdims=True)
+                ds_ = lower(pr * (dp - delta), 0.0).astype(BF)
+                dq = jnp.dot(ds_, kv, preferred_element_type=F32) * scale
+                dkv[0, :length, :] += dims(ds_, qv, 0, 0)
+                dkv[1, :length, :] += dims(pr.astype(BF), dov, 0, 0)
+                du, dgain = norm_back(dq, raw_i[rows, lanes], qg[...], pl.ds(i * 256, 256))
+                dqkv[i * 4 : i * 4 + 4, :, lanes] = du.reshape(4, BLK, 128)
+                heads[0:1, :] += dgain
+        lanes = pl.ds(pl.multiple_of(512 + g * 128, 128), 128)
+        for i in range(4):
+            rows = slice(i * 256, (i + 1) * 256)
+            du, dgain = norm_back(dkv[0, rows, :] * scale, raw_i[rows, lanes], kg[...], pl.ds(i * 256, 256))
+            dqkv[i * 4 : i * 4 + 4, :, lanes] = du.reshape(4, BLK, 128)
+            heads[1:2, :] += dgain
+        dqkv[:, :, pl.ds(pl.multiple_of(768 + g * 128, 128), 128)] = dkv[1].astype(BF).reshape(16, BLK, 128)
+
+    hy_copy = remote(heads, hy, hs.at[0], hr.at[0], (q, 2 * z + 1 - y))
+    hy_copy.start()
+
+    @pl.loop(0, 4)
+    def _(n):
+        rows = pl.ds(pl.multiple_of(n * 256, 256), 256)
+        d = pieces(dqkv, spots, 0, n * 4, 4)
+        dy[rows, :] = dims(d, wq[...].reshape(WIDTH, WIDTH), 1, 1).astype(BF)
+        h_in.beside(n)
+
+        @pl.when(n > 0)
+        def _():
+            h_in.across(n - 1)
+
+    h_in.across(3)
+
+    @pl.loop(0, 4)
+    def _(n):
+        v = dims(xhat[:, pl.ds(pl.multiple_of(n * 256, 256), 256)], dqkv[...].reshape(TOKENS, WIDTH), 0, 0).astype(BF)
+        v = v.reshape(4, 2, 32, WIDTH)
+        for t in range(2):
+            gqkv[t, n] = v[:, t]
+        sqkv.y_send(n)
+
+    def z_heads(k):
+        return remote(hz.at[z], hz.at[z], hs.at[k], hr.at[k], (q, 2 * mod(z + k, 4) + y))
+
+    def dp_heads(k):
+        return remote(hdp.at[q], hdp.at[q], hs.at[3 + k], hr.at[3 + k], (mod(q + k, 4), p))
+
+    hy_copy.wait_recv()
+    hz[z] = heads[...] + hy[...]
+    for k in (1, 2, 3):
+        z_heads(k).start()
+    so.z_step(0)
+    od[...] = sd.z_sum(0)
+
+    @pl.loop(0, 4)
+    def _(n):
+        cgu.step(n)
+        sqkv.z_step(n)
+        h_in.finish(n, inward)
+
+    for k in (1, 2, 3):
+        f = mod(z + 4 - k, 4)
+        remote(hz.at[f], hz.at[f], hs.at[k], hr.at[k], (q, p)).wait_recv()
+    hdp[q] = hz[0] + hz[1] + hz[2] + hz[3]
+    for k in (1, 2, 3):
+        dp_heads(k).start()
+    oo[...] = so.z_sum(0)
+
+    @pl.loop(0, 4)
+    def _(n):
+        cqkv.step(n)
+
+    cgu.close()
+    for k in (1, 2, 3):
+        f = mod(q + 4 - k, 4)
+        remote(hdp.at[f], hdp.at[f], hs.at[3 + k], hr.at[3 + k], (q, p)).wait_recv()
+    oheads[...] = hdp[0] + hdp[1] + hdp[2] + hdp[3]
+    cqkv.close()
+    h_out.close()
+    h_in.close()
+    sd.close(1)
+    sgu.close(4)
+    so.close(1)
+    sqkv.close(4)
+    hy_copy.wait_send()
+    for k in (1, 2, 3):
+        z_heads(k).wait_send()
+        dp_heads(k).wait_send()
+
+
+def second_call(spots, gd, ggu, part2, dtotal, hidden, cs, wo, wq, xhat, raw, qb, kb, vb, ob, lse, xf, cosf, sinf, qg, kg):
+    shape = jax.ShapeDtypeStruct
+    sem = pltpu.SemaphoreType.DMA
+    vm = pltpu.VMEM
+    full = (TOKENS, WIDTH)
+    return pl.pallas_call(
+        second_kernel,
+        out_shape=(
+            shape((2, 128, WIDTH), BF),
+            shape((2, 128, WIDTH), BF),
+            shape((96, WIDTH), F32),
+            shape((4, 32, 1536), F32),
+            shape((64, WIDTH), F32),
+            shape((4, 32, WIDTH), F32),
+            shape((8, 128), F32),
+        ),
+        in_specs=[SM] + [VM] * 20,
+        out_specs=(VM,) * 7,
+        scratch_shapes=[
+            vm((16, BLK, WIDTH), F32), vm(full, BF), vm((4, TOKENS, 128), BF), vm((16, BLK, WIDTH), BF),
+            vm((2, TOKENS, 128), F32), vm((2, 1, 4, 64, WIDTH), BF), vm((2, 4, 4, 32, WIDTH), BF),
+            vm((8, 128), F32),
+            vm((1, 4, 96, WIDTH), BF), vm((4, 4, 32, 1536), BF), vm((1, 4, 64, WIDTH), BF), vm((4, 4, 32, WIDTH), BF),
+            vm((1, 3, 96, WIDTH), BF), vm((4, 3, 32, 1536), BF), vm((1, 3, 64, WIDTH), BF), vm((4, 3, 32, WIDTH), BF),
+            vm((4, 32, 1536), BF), vm((4, 32, WIDTH), BF), vm((4, 32, 1536), BF), vm((4, 32, WIDTH), BF),
+            vm((8, 128), F32), vm((4, 8, 128), F32), vm((4, 8, 128), F32),
+        ]
+        + [vm((4, 128, WIDTH), BF)] * 6
+        + [sem((10, 8)), sem((4, 4)), sem((7,)), sem((7,)), sem((12, 4)), sem((2,))],
+        compiler_params=pltpu.CompilerParams(
+            collective_id=1, has_side_effects=True, vmem_limit_bytes=VMEM_BYTES
+        ),
+        name="backward_and_scatter",
+    )(
+        spots, gd.reshape(2, 1, 4, 96, WIDTH), ggu, part2, dtotal, hidden.reshape(16, BLK, WIDTH), cs, wo, wq, xhat,
+        raw, qb, kb, vb, ob, lse, xf, cosf, sinf, qg, kg,
+    )
+
+
+def quarter_columns(w, gain):
+    rows, cols = w.shape
+    v = w if gain is None else (w.astype(F32) * gain).astype(BF)
+    return jnp.transpose(v.reshape(rows, 4, cols // 4), (1, 0, 2))
+
+
+def whole_sequences(
+    tokens, attn_gain, w_query, key_projection, value_projection, query_head_gain, key_gain, w_out,
+    mlp_gain, w_gate, w_up, w_down, cotangent, span_order,
+):
+    p = lax.axis_index("seq")
+    ga = attn_gain.astype(F32)[:, None]
+    gm = mlp_gain.astype(F32)[:, None]
+    pq = jnp.concatenate(
+        [quarter_columns(w, ga) for w in (w_query, key_projection, value_projection)], axis=2
+    )
+    pg = jnp.concatenate([quarter_columns(w, gm) for w in (w_gate, w_up)], axis=2)
+    row = jnp.where(lax.rem(p // 2, 2) == 0, span_order[0], span_order[1])
+    spots = lax.iota(jnp.int32, 16)
+    inverse = jnp.sum(jnp.where(row[None, :] == spots[:, None], spots[None, :], 0), axis=1)
+    pos = jnp.zeros((8, 128), jnp.int32)
+    pos = pos.at[0, :16].set(row).at[1, :16].set(inverse)
+    freqs = BASE ** (-(lax.iota(F32, HEAD_SIZE // 2) * 2.0) / HEAD_SIZE)
+    angles = lax.iota(F32, TOKENS)[:, None] * freqs[None, :]
+    cosine = jnp.cos(angles)
+    sine = jnp.sin(angles)
+    cosf = jnp.concatenate([cosine, cosine], axis=1)
+    sinf = jnp.concatenate([-sine, sine], axis=1)
+    qg = query_head_gain.astype(F32)[None, :]
+    kg = key_gain.astype(F32)[None, :]
+    xf, of, wq, wo, xhat, raw, qb, kb, vb, ob, lse, hidden, cs, part2, dtotal, gd, ggu = first_call(
+        tokens.reshape(2, 2, BLK, WIDTH), cotangent.reshape(2, 2, BLK, WIDTH), pos, pq, pg, w_out, w_down,
+        cosf, sinf, qg, kg,
+    )
+    out, igrad, od, ogu, oo, oqkv, oheads = second_call(
+        of, gd, ggu, part2, dtotal, hidden, cs, wo, wq, xhat, raw, qb, kb, vb, ob, lse, xf, cosf, sinf, qg, kg
+    )
+    return finish(
+        out, igrad, od, ogu, oo, oqkv, oheads, ga, gm, w_query, key_projection, value_projection, w_gate, w_up
+    )
+
+
+def finish(out, igrad, od, ogu, oo, oqkv, oheads, ga, gm, w_query, key_projection, value_projection, w_gate, w_up):
+    def join(part):
+        return jnp.transpose(part, (1, 0, 2)).reshape(part.shape[1], -1)
+
+    hq, hk, hv = join(oqkv[:, :, :512]), join(oqkv[:, :, 512:768]), join(oqkv[:, :, 768:])
+    hg, hu = join(ogu[:, :, :768]), join(ogu[:, :, 768:])
+
+    def along(w, h):
+        return jnp.sum(w.astype(F32) * h, axis=1)
+
+    grad_attn_gain = along(w_query, hq) + along(key_projection, hk) + along(value_projection, hv)
+    grad_mlp_gain = along(w_gate, hg) + along(w_up, hu)
+    return (
+        out,
+        igrad,
+        grad_attn_gain,
+        ga * hq,
+        ga * hk,
+        ga * hv,
+        oheads[0],
+        oheads[1],
+        oo,
+        grad_mlp_gain,
+        gm * hg,
+        gm * hu,
+        od,
+    )
+
+
+def layer(tokens, *rest):
+    whole = (
+        lax.axis_size("dp") == 4
+        and lax.axis_size("seq") == 8
+        and tokens.shape == (2, 128, WIDTH)
+        and rest[-1].shape == (2, 16)
+    )
+    return (whole_sequences if whole else shards)(tokens, *rest)
+
+
 def solution(mesh):
     return jax.shard_map(
-        shards,
+        layer,
         mesh=mesh,
         in_specs=(
             P("dp", "seq", None),

time: 2470 us -> 403 us (0.16)
  waiting for transfers between devices: 1540 us -> 0 us
  Pallas kernels: 0 us -> 373 us
  local copies, waits for them, and re-layouts: 359 us -> 6.69 us
  matrix products: 276 us -> 0 us
  blocking collectives: 94.1 us -> 0 us
  starting transfers between devices: 90.7 us -> 0 us
  other arithmetic: 73 us -> 16 us
    unnamed x13 -> x0, waiting for transfers between devices: 861 us -> none
    all_gather x11 -> x0, waiting for transfers between devices: 529 us -> none  [the longest x2 87.2 us: shards(): piece_v = lax.all_gather(value_reduced, 'seq', axis=1, tiled=True)]
    pallas_call x0 -> x2, Pallas kernels: none -> 373 us  [the longest x1 195 us: first_call(): pl.pallas_call(first_kernel, out_shape=(shape((16, BLK, WIDTH), BF), shap...]
    dot_general x126 -> x0, matrix products: 276 us -> none  [the longest x14 85.6 us: row_product(): lax.dot_general(left, right, (((0,), (0,)), ((), ())), preferred_element_...]
    ppermute x64 -> x0, waiting for transfers between devices: 148 us -> none  [from_behind(): return lax.ppermute(block, axis, route)]
    unnamed x262 -> x29, local copies, waits for them, and re-layouts: 148 us -> 5.1 us
    reshape x19 -> x6, local copies, waits for them, and re-layouts: 130 us -> 0.11 us  [the longest x5 0.09 us: join(): return jnp.transpose(part, (1, 0, 2)).reshape(part.shape[1], -1)]
    ppermute x64 -> x0, starting transfers between devices: 90.3 us -> none  [from_behind(): return lax.ppermute(block, axis, route)]
  transfers between devices with their start and end apart: 76 -> 0, of which waited for: 56 -> 0; matrix products, arithmetic and copies ran while one was open for 9% -> 0% of each run, Pallas kernels for 0% -> 0%
where the time goes in v2:
time: 403 us; the launch traced here: 397 us
  Pallas kernels  373 us (93%)
  other arithmetic  16 us (4%)
  local copies, waits for them, and re-layouts  6.69 us (2%)
    pallas_call x1, Pallas kernels, first_call(): pl.pallas_call(first_kernel, out_shape=(shape((16, BLK, WIDTH), BF), shap...  195 us
    pallas_call x1, Pallas kernels, second_call(): pl.pallas_call(second_kernel, out_shape=(shape((2, 128, WIDTH), BF), shap...  178 us

profile of v2, /device:TPU:27, one launch (start us, length us, event | category | flops | bytes accessed | tf_op | source)
XLA Modules:
  0.0 397.0 jit_solution(11920291316818782167)
XLA Ops:
  0.7 0.7 convert_element_type.44
  1.3 0.7 convert_element_type.51
  2.0 0.8 fusion.13
  2.7 0.8 broadcast_select_fusion
  3.5 0.1 select_reduce_fusion
  3.6 1.2 bitcast_convert_fusion
  4.8 0.2 scatter.9.pos
  5.0 0.0 copy-start.10
  5.0 1.0 fusion.6
  6.0 1.0 fusion.9
  7.0 0.7 pad_maximum_fusion.3.pq
  7.7 1.2 fusion.2
  8.9 0.8 pad_maximum_fusion.2.pg
  9.7 2.0 fusion.8
  11.7 1.3 pad_maximum_fusion
  13.0 195.1 %forward_and_mlp.1 = (bf16[16,64,1024]{2,1,0:T(8,128)(2,1)}, s32[8,128]{1,0:T(8,128)}, bf16[4,8,32,1024]{3,2,1,0:T(8,128)(2,1)}, bf16[8,64,1024]{2,1,0:T(8,128)(...) custom-call(bf16[2,2,64,1024]{3,2,1,0:T(8,128)(2,1)} %bitcast.75, ...), custom_call_target="tpu_custom_call" | custom-call | tf_op jit(solution)/shard_map/forward_and_mlp/pallas_call | solution.py:847
  208.1 0.0 copy-start.3
  208.1 178.3 %backward_and_scatter.1 = (bf16[2,128,1024]{2,1,0:T(8,128)(2,1)}, bf16[2,128,1024]{2,1,0:T(8,128)(2,1)}, f32[96,1024]{1,0:T(8,128)}, f32[4,32,1536]{2,1,0:T(8,12...) custom-call(s32[8,128]{1,0:T(8,128)} %get-tuple-element.61.spots, ...), custom_call_target="tpu_custom_call" | custom-call | tf_op jit(solution)/shard_map/backward_and_scatter/pallas_call | solution.py:1246
  386.5 0.0 copy-start.8
  386.5 1.3 slice_bitcast_fusion.5
  387.8 1.0 slice_bitcast_fusion.2
  388.8 1.0 slice_bitcast_fusion.4
  389.8 0.9 broadcast_multiply_fusion.2
  390.8 0.9 broadcast_multiply_fusion.3
  391.7 0.5 add_add_fusion
  392.2 0.1 slice_bitcast_fusion
  392.4 1.1 broadcast_multiply_fusion
  393.5 0.5 add.18
  394.0 0.8 copy.68
  394.8 0.8 copy.69
  395.6 0.7 copy.70
  396.3 0.7 copy.71
  (29 shorter events, 0.2 us)
Async XLA Ops:
  5.0 6.7 %copy-start.10 = (s32[8,128]{1,0:T(8,128)}, s32[8,128]{1,0:T(8,128)S(1)}, u32[]{:S(2)}) copy-start(s32[8,128]{1,0:T(8,128)S(1)} %scatter.9.pos) | copy-start | bytes 12292
  208.1 181.7 %copy-start.3 = (bf16[32,2048]{1,0:T(8,128)(2,1)S(1)}, bf16[32,2048]{1,0:T(8,128)(2,1)}, u32[]{:S(2)}) copy-start(bf16[32,2048]{1,0:T(8,128)(2,1)} %param.20) | copy-start | bytes 393220
  386.5 4.3 %copy-start.8 = (bf16[32,1024]{1,0:T(8,128)(2,1)S(1)}, bf16[32,1024]{1,0:T(8,128)(2,1)}, u32[]{:S(2)}) copy-start(bf16[32,1024]{1,0:T(8,128)(2,1)} %param.21) | copy-start | bytes 196612
  386.5 4.3 %copy-start.9 = (bf16[32,1024]{1,0:T(8,128)(2,1)S(1)}, bf16[32,1024]{1,0:T(8,128)(2,1)}, u32[]{:S(2)}) copy-start(bf16[32,1024]{1,0:T(8,128)(2,1)} %param.22) | copy-start | bytes 196612
  386.5 5.7 %copy-start = (f32[4,32,1536]{2,1,0:T(8,128)S(1)}, f32[4,32,1536]{2,1,0:T(8,128)}, u32[]{:S(2)}) copy-start(f32[4,32,1536]{2,1,0:T(8,128)} %get-tuple-element.83) | copy-start | bytes 2359300
  390.7 1.6 copy-start.1
  390.7 1.6 copy-start.2
  392.2 1.8 copy-start.5
  392.3 2.5 copy-start.4
  392.3 3.3 copy-start.7
  392.4 3.9 copy-start.6

commit v3 on v2

--- a/solution.py
+++ b/solution.py
@@ -3,6 +3,7 @@
 from jax import lax
 from jax.sharding import PartitionSpec as P
 
+import numpy as np
 from jax.experimental import pallas as pl
 from jax.experimental.pallas import tpu as pltpu
 
@@ -406,6 +407,12 @@
     return jnp.concatenate([ref[spots[which, first + t]] for t in range(count)], axis=0)
 
 
+def turns(table):
+    other = pltpu.roll(table, HEAD_SIZE // 2, 1)
+    first = lax.broadcasted_iota(jnp.int32, table.shape, 1) < HEAD_SIZE // 2
+    return jnp.where(first, table, other), jnp.where(first, -other, table)
+
+
 def rotate(v, cosine, sine):
     return v * cosine + pltpu.roll(v, HEAD_SIZE // 2, 1) * sine
 
@@ -436,12 +443,17 @@
 
     def copy(self, step, n):
         s, r = self.sems.at[self.base + 2 * step, n], self.sems.at[self.base + 2 * step + 1, n]
-        mine = self.rows(n, self.c)
         if step == 0:
             return remote(self.part.at[self.rows(n, 1 - self.c)], self.l1.at[n], s, r, self.sib)
         if step == 1:
             return remote(self.own.at[n], self.l2.at[n], s, r, self.opp)
-        return remote(self.total.at[mine], self.total.at[mine], s, r, self.sib)
+        mine = self.total_at(n, self.c)
+        return remote(mine, mine, s, r, self.sib)
+
+    def total_at(self, n, c):
+        if len(self.total.shape) == 2:
+            return self.total.at[self.rows(n, c)]
+        return self.total.at[(2 * n + c) // 4, (2 * n + c) % 4]
 
     def beside(self, n):
         self.copy(0, n).start()
@@ -454,19 +466,23 @@
 
     def back(self, n):
         self.copy(1, n).wait_recv()
-        self.total[self.rows(n, self.c), :] = (self.own[n].astype(F32) + self.l2[n].astype(F32)).astype(BF)
+        total = self.total_at(n, self.c)
+        total[...] = (self.own[n].astype(F32) + self.l2[n].astype(F32)).astype(BF).reshape(total.shape)
         self.copy(2, n).start()
 
     def ready(self, n):
-        other = self.rows(n, 1 - self.c)
+        other = self.total_at(n, 1 - self.c)
         s, r = self.sems.at[self.base + 4, n], self.sems.at[self.base + 5, n]
-        remote(self.total.at[other], self.total.at[other], s, r, self.sib).wait_recv()
-
-    def close(self):
+        remote(other, other, s, r, self.sib).wait_recv()
+
+    def close(self, *steps):
         @pl.loop(0, 4)
         def _(n):
-            for step in range(3):
+            for step in steps:
                 self.copy(step, n).wait_send()
+
+
+PIECES = ((0, None), (2, None), (1, 0), (1, 1), (1, 2), (1, 3), (3, None))
 
 
 def block(ref, b):
@@ -518,37 +534,65 @@
             f = mod(q + 4 - k, 4)
             remote(src.at[0], dst.at[f, p], self.as_.at[n, k - 1], self.ar.at[n, k - 1], (q, p)).wait_recv()
 
-    def view(self, n, chunk):
-        return self.w[n].at[:, chunk] if n < 2 else self.w[n].at[chunk]
-
-    def z_copy(self, n, k):
-        t = mod(self.z + k, 4)
-        v = self.view(n, self.p)
-        return remote(v, v, self.zs.at[n, k - 1], self.zr.at[n, k - 1], (self.q, 2 * t + self.y))
-
-    def z_send(self, n):
-        for k in (1, 2, 3):
-            self.z_copy(n, k).start()
-
-    def y_copy(self, n, k):
-        v = self.view(n, 2 * mod(self.z + 4 - k, 4) + self.y)
-        return remote(v, v, self.ys.at[n, k], self.yr.at[n, k], (self.q, 2 * self.z + 1 - self.y))
-
-    def y_send(self, n, k):
-        self.y_copy(n, k).start()
-
-    def z_wait(self, n, k):
-        v = self.view(n, 2 * mod(self.z + 4 - k, 4) + self.y)
-        remote(v, v, self.zs.at[n, k - 1], self.zr.at[n, k - 1], (self.q, self.p)).wait_recv()
-
-    def y_wait(self, n):
-        for k in range(4):
-            v = self.view(n, 2 * mod(self.z + 4 - k, 4) + 1 - self.y)
-            remote(v, v, self.ys.at[n, k], self.yr.at[n, k], (self.q, self.p)).wait_recv()
-
-    def pass_on(self, n, k):
-        self.z_wait(n, k)
-        self.y_send(n, k)
+    def view(self, piece, chunk):
+        n, part = PIECES[piece]
+        if n >= 2:
+            return self.w[n].at[chunk]
+        return self.w[n].at[:, chunk] if part is None else self.w[n].at[part, chunk]
+
+    def z_copy(self, piece, src, way):
+        v = self.view(piece, 2 * src + self.y)
+        s = self.zs.at[piece, src + (4 if way < 0 else 0)]
+        return remote(v, v, s, self.zr.at[piece, src], (self.q, 2 * (self.z + way) + self.y))
+
+    def y_copy(self, piece, src):
+        v = self.view(piece, 2 * src + self.y)
+        return remote(v, v, self.ys.at[piece, src], self.yr.at[piece, src], (self.q, 2 * self.z + 1 - self.y))
+
+    def spread(self, piece, src, up, down):
+        if up:
+
+            @pl.when(self.z < 3)
+            def _():
+                self.z_copy(piece, src, 1).start()
+
+        if down:
+
+            @pl.when(self.z > 0)
+            def _():
+                self.z_copy(piece, src, -1).start()
+
+        self.y_copy(piece, src).start()
+
+    def begin(self, *pieces_):
+        for piece in pieces_:
+            self.spread(piece, self.z, True, True)
+
+    def step(self, piece, dist):
+        low, high = self.z - dist, self.z + dist
+
+        @pl.when(low >= 0)
+        def _():
+            v = self.view(piece, 2 * low + self.y)
+            remote(v, v, self.zs.at[piece, 0], self.zr.at[piece, low], (self.q, self.p)).wait_recv()
+            self.spread(piece, low, True, False)
+
+        @pl.when(high < 4)
+        def _():
+            v = self.view(piece, 2 * high + self.y)
+            remote(v, v, self.zs.at[piece, 0], self.zr.at[piece, high], (self.q, self.p)).wait_recv()
+            self.spread(piece, high, False, True)
+
+    def steps(self, *pieces_):
+        for piece in pieces_:
+            for dist in (1, 2, 3):
+                self.step(piece, dist)
+
+    def y_wait(self, *pieces_):
+        for piece in pieces_:
+            for src in range(4):
+                v = self.view(piece, 2 * src + 1 - self.y)
+                remote(v, v, self.ys.at[piece, src], self.yr.at[piece, src], (self.q, self.p)).wait_recv()
 
     def tok_dst(self, a):
         return (self.xf, self.cf)[a]
@@ -647,55 +691,249 @@
             self.pos_copy(0).wait_recv()
 
     def close(self):
-        for n in range(4):
+        for n in range(2):
             for k in (1, 2, 3):
-                if n < 2:
-                    self.column_copy(n, k).wait_send()
-                self.z_copy(n, k).wait_send()
-            for k in range(4):
-                self.y_copy(n, k).wait_send()
+                self.column_copy(n, k).wait_send()
+        for piece in range(len(PIECES)):
+            for src in range(4):
+                self.y_copy(piece, src).wait_send()
+
+                @pl.when(jnp.logical_and(self.z < 3, src <= self.z))
+                def _():
+                    self.z_copy(piece, src, 1).wait_send()
+
+                @pl.when(jnp.logical_and(self.z > 0, src >= self.z))
+                def _():
+                    self.z_copy(piece, src, -1).wait_send()
+
         self.token_close(0)
         self.token_close(1)
 
 
-GATHER_SEMS = ((7,), (2, 2), (2, 8), (2, 2, 8), (2, 8), (3,), (1,), (2, 3), (2, 3), (4, 3), (4, 3), (4, 4), (4, 4))
-
-
-def first_kernel(
-    tok, cot, pos, pq, pg, po, pd, cosf, sinf, qg, kg,
-    xf, of, wq, wo, xhat, raw_o, qb, kb, vb, ob, lse, hidden, cs, part2, dtotal, gd, ggu,
-    cf, wg, wd, part1, total, dpart, a2, mb, dgu, l1, own, l2, l1b, ownb, l2b, sorts, sorts_sem, sums, *sems,
+GATHER_SEMS = ((7,), (2, 2), (2, 8), (2, 2, 8), (2, 8), (3,), (1,), (2, 3), (2, 3), (7, 8), (7, 4), (7, 4), (7, 4))
+
+
+class Home:
+    def __init__(self, part, out, l1, own, l2, sems, here, base):
+        self.q, self.p, self.x, self.c, self.z, self.y = place()
+        self.part, self.out, self.l1, self.own, self.l2 = part, out, l1, own, l2
+        self.sems, self.here, self.base = sems, here, base
+        self.owner_x, self.owner_c = self.y, self.z // 2
+        self.keeps = self.x == self.owner_x
+        self.sib = (2 * self.x + 1 - self.c, self.p)
+        self.opp = (2 * (1 - self.x) + self.c, self.p)
+        self.goal_q = 2 * self.owner_x + self.owner_c
+
+    def rows(self, n, c):
+        return pl.ds(pl.multiple_of(n * 256 + c * 128, 128), 128)
+
+    def sem(self, k, n):
+        return self.sems.at[self.base + k, n]
+
+    def first(self, n):
+        return remote(
+            self.part.at[self.rows(n, 1 - self.c)], self.l1.at[n], self.sem(0, n), self.sem(1, n), self.sib
+        )
+
+    def second(self, n):
+        return remote(self.own.at[n], self.l2.at[n], self.sem(2, n), self.sem(3, n), self.opp)
+
+    def third(self, n):
+        slot = mod(self.z, 2)
+        return remote(
+            self.own.at[n], self.out.at[slot], self.sem(4, n), self.sem(5, slot), (self.goal_q, 2 * n + self.c)
+        )
+
+    def is_self(self, n):
+        return jnp.logical_and(self.goal_q == self.q, 2 * n + self.c == self.p)
+
+    def beside(self, n):
+        self.first(n).start()
+
+    def across(self, n):
+        self.first(n).wait_recv()
+        mine = self.part[self.rows(n, self.c), :].astype(F32)
+        self.own[n] = (mine + self.l1[n].astype(F32)).astype(BF)
+
+        @pl.when(jnp.logical_not(self.keeps))
+        def _():
+            self.second(n).start()
+
+    def finish(self, n, rest):
+        @pl.when(self.keeps)
+        def _():
+            self.second(n).wait_recv()
+            s = self.own[n].astype(F32) + self.l2[n].astype(F32)
+            self.own[n] = rest(n, s).astype(BF)
+
+            @pl.when(jnp.logical_not(self.is_self(n)))
+            def _():
+                self.third(n).start()
+
+            @pl.when(self.is_self(n))
+            def _():
+                cp = pltpu.make_async_copy(self.own.at[n], self.out.at[mod(self.z, 2)], self.here)
+                cp.start()
+                cp.wait()
+
+    def close(self):
+        for i in range(2):
+            group = 4 * self.c + 2 * i + self.x
+            same = jnp.logical_and(group == self.p, self.y == self.c)
+
+            @pl.when(jnp.logical_not(same))
+            def _():
+                remote(self.own.at[0], self.out.at[i], self.sem(4, 0), self.sem(5, i), (self.q, self.p)).wait_recv()
+
+        for n in range(4):
+            self.first(n).wait_send()
+
+            @pl.when(jnp.logical_not(self.keeps))
+            def _():
+                self.second(n).wait_send()
+
+            @pl.when(jnp.logical_and(self.keeps, jnp.logical_not(self.is_self(n))))
+            def _():
+                self.third(n).wait_send()
+
+
+class Scatter:
+    def __init__(self, g, ly, lz, sems, base):
+        self.q, self.p, _, _, self.z, self.y = place()
+        self.g, self.ly, self.lz, self.sems, self.base = g, ly, lz, sems, base
+
+    def y_copy(self, n):
+        s, r = self.sems.at[self.base + n, 0], self.sems.at[self.base + n, 1]
+        return remote(self.g.at[1 - self.y, n], self.ly(n), s, r, (self.q, 2 * self.z + 1 - self.y))
+
+    def z_copy(self, n, k):
+        t = mod(self.z + k, 4)
+        s, r = self.sems.at[self.base + n, 2 * k], self.sems.at[self.base + n, 2 * k + 1]
+        return remote(self.ly(n).at[t], self.lz(n).at[k - 1], s, r, (self.q, 2 * t + self.y))
+
+    def y_send(self, n):
+        self.y_copy(n).start()
+
+    def z_step(self, n):
+        self.y_copy(n).wait_recv()
+        ly = self.ly(n)
+
+        @pl.loop(0, 4)
+        def _(t):
+            ly[t] = (ly[t].astype(F32) + self.g[self.y, n, t].astype(F32)).astype(BF)
+
+        for k in (1, 2, 3):
+            self.z_copy(n, k).start()
+
+    def z_sum(self, n):
+        for k in (1, 2, 3):
+            self.z_copy(n, k).wait_recv()
+        ly, lz = self.ly(n), self.lz(n)
+        return ly[self.z].astype(F32) + lz[0].astype(F32) + lz[1].astype(F32) + lz[2].astype(F32)
+
+    def close(self, count):
+        @pl.loop(0, count)
+        def _(n):
+            self.y_copy(n).wait_send()
+            for k in (1, 2, 3):
+                self.z_copy(n, k).wait_send()
+
+
+class Columns:
+    def __init__(self, scatter, land, sems, base):
+        self.scatter, self.land = scatter, land
+        self.sems, self.base = sems, base
+        self.q, self.p = scatter.q, scatter.p
+
+    def copy(self, t):
+        s, r = self.sems.at[self.base, t], self.sems.at[self.base + 1, self.q]
+        return remote(self.scatter.ly(t).at[self.scatter.z], self.land.at[self.q], s, r, (t, self.p))
+
+    def step(self, t):
+        s = self.scatter.z_sum(t).astype(BF)
+
+        @pl.when(t != self.q)
+        def _():
+            ly = self.scatter.ly(t)
+            ly[self.scatter.z] = s
+            self.copy(t).start()
+
+        @pl.when(t == self.q)
+        def _():
+            self.land[t] = s
+
+    def close(self):
+        for t in range(4):
+
+            @pl.when(t != self.q)
+            def _():
+                r = self.sems.at[self.base + 1, t]
+                remote(self.land.at[t], self.land.at[t], self.sems.at[self.base, t], r, (self.q, self.p)).wait_recv()
+                self.copy(t).wait_send()
+
+
+def column(table, h):
+    lane = lax.broadcasted_iota(jnp.int32, table.shape, 1)
+    return jnp.sum(jnp.where(lane == h, table, 0.0), axis=1, keepdims=True)
+
+
+def layer_kernel(
+    tok, cot, pos, pq, pg, po, pd, table, qg, kg,
+    out, igrad, od, ogu, oo, oqkv, oheads, of,
+    xf, cf, wq, wg, wo, wd, raw_o, qb, kb, vb, ob, lse, hidden, rest, cs, pa, pb, pc, mb, dgu, gd, ggu,
+    dkv, go, gqkv, yo, yqkv, zo, zqkv, heads, hy, hz, hdp,
+    l1, own, l2, l1b, ownb, l2b, l2c, sorts, sorts_sem, free, sums, gsem, csem, hs, hr, homes, here, *sems,
 ):
+    q, p, x_, c, z, y = place()
+    sd = Scatter(gd, lambda n: wd.at[pl.ds(0, 4)], lambda n: wd.at[pl.ds(4, 3)], gsem, 0)
+    sgu = Scatter(ggu, lambda n: wg.at[n, pl.ds(0, 4)], lambda n: wg.at[n, pl.ds(4, 3)], gsem, 1)
+    so = Scatter(go, lambda n: yo.at[n], lambda n: zo.at[n], gsem, 5)
+    sqkv = Scatter(gqkv, lambda n: yqkv.at[n], lambda n: zqkv.at[n], gsem, 6)
+    cgu = Columns(sgu, ogu, csem, 0)
+    cqkv = Columns(sqkv, oqkv, csem, 2)
+    h_out = Home(pb, out, l1, own, l2, homes, here.at[0], 0)
+    h_in = Home(pc, igrad, l1b, ownb, l2c, homes, here.at[1], 6)
+    order = [(sd, 0)] + [(sgu, n) for n in range(4)] + [(so, 0)] + [(sqkv, n) for n in range(4)]
+
+    def y_send(j):
+        which, n = order[j]
+        which.y_send(n)
+
+    def step(j):
+        which, n = order[j]
+        which.z_step(n)
+        if j + 2 < len(order):
+            y_send(j + 2)
+
     g = Gather((tok, cot, pos, pq, pg, po, pd), (xf, cf, of, wq, wg, wo, wd), sems)
-    greet(g.peers())
+    peers = [(2 * x_ + cc, mod(p + k, 8)) for k in range(1, 8) for cc in (0, 1)]
+    peers += [(mod(q + k, 4), p) for k in (1, 2, 3)]
+    greet(peers)
     g.pos_start()
+    g.token_start(0)
     g.column_start(0)
-    g.token_start(0)
     for n in range(4):
         g.own_copy(n).start()
     g.column_start(1)
     g.own_copy(0).wait()
     g.column_wait(0)
-    g.z_send(0)
-    g.y_send(0, 0)
+    g.begin(0)
     g.pos_finish()
     sort = pltpu.make_async_copy(of, sorts, sorts_sem.at[0])
     sort.start()
+    lse[...] = jnp.zeros_like(lse)
+    g.step(0, 1)
     g.token_pass(0, 0, 4)
-    for k in (1, 3, 2):
-        g.pass_on(0, k)
+    g.step(0, 2)
     g.own_copy(2).wait()
-    g.z_send(2)
-    g.y_send(2, 0)
-    g.token_pass(0, 4, 8)
+    g.begin(1)
+    g.step(0, 3)
     g.own_copy(1).wait()
     g.column_wait(1)
-    g.z_send(1)
-    g.y_send(1, 0)
+    g.begin(2)
+    g.token_pass(0, 4, 8)
     g.own_copy(3).wait()
-    g.z_send(3)
-    g.y_send(3, 0)
-    g.token_start(1)
+    g.begin(3)
     sort.wait()
     g.y_wait(0)
 
@@ -704,11 +942,20 @@
         rows = pl.ds(pl.multiple_of(n * 256, 256), 256)
         v = pieces(xf, sorts, 1, n * 4, 4).astype(F32)
         h = (v * unit(v)).astype(BF)
-        xhat[rows, :] = h
+
+        @pl.when(n == 1)
+        def _():
+            g.step(1, 1)
+            g.begin(4)
+
+        @pl.when(n == 3)
+        def _():
+            g.step(1, 2)
+            g.step(2, 1)
+
         raw = jnp.dot(h, wq[...].reshape(WIDTH, WIDTH), preferred_element_type=F32)
         raw_o[rows, :] = raw[:, :768]
-        cosine = cosf[rows, :]
-        sine = sinf[rows, :]
+        cosine, sine = turns(table[rows, :])
         for t in range(2):
             vb[t, rows, :] = raw[:, 768 + t * 128 : 896 + t * 128].astype(BF)
         for t in range(6):
@@ -722,12 +969,16 @@
 
     @pl.loop(0, 4)
     def _(h):
-        for turn, todo in enumerate((((2, 1), (2, 3), (2, 2)), ((1, 1),), ((1, 3),), ((1, 2),))):
+        for turn, (piece, dist) in enumerate(((1, 3), (2, 2), (2, 3), (3, 1))):
 
             @pl.when(h == turn)
             def _():
-                for n, k in todo:
-                    g.pass_on(n, k)
+                g.step(piece, dist)
+                if turn == 0:
+                    g.begin(5)
+                if turn == 2:
+                    g.begin(6)
+                    g.token_start(1)
 
         kv = h // 2
         for i in range(4):
@@ -740,17 +991,18 @@
             sum_e = jnp.sum(e, axis=-1, keepdims=True)
             o = jnp.dot(e.astype(BF), vb[kv, :length, :], preferred_element_type=F32) / sum_e
             ob[rows, pl.ds(pl.multiple_of(h * 128, 128), 128)] = o.astype(BF)
-            lse[h, rows, :] = top + jnp.log2(sum_e)
-
-    g.y_wait(2)
-    s1 = Sum(part1, total, l1, own, l2, sums, 0)
-    s2 = Sum(dpart, dtotal, l1b, ownb, l2b, sums, 6)
+            lane = lax.broadcasted_iota(jnp.int32, (256, 128), 1)
+            lse[rows, :] = jnp.where(lane == h, top + jnp.log2(sum_e), lse[rows, :])
+
+    g.y_wait(1)
+    s1 = Sum(pa, pb, l1, own, l2, sums, 0)
+    s2 = Sum(pc, gqkv, l1b, ownb, l2b, sums, 6)
 
     @pl.loop(0, 4)
     def _(n):
         rows = pl.ds(pl.multiple_of(n * 256, 256), 256)
         out_w = wo[...].reshape(512, WIDTH)
-        part1[rows, :] = jnp.dot(ob[rows, :], out_w, preferred_element_type=F32).astype(BF)
+        pa[rows, :] = jnp.dot(ob[rows, :], out_w, preferred_element_type=F32).astype(BF)
         s1.beside(n)
 
         @pl.when(n > 0)
@@ -758,26 +1010,35 @@
             s1.across(n - 1)
 
     s1.across(3)
-    for k in (1, 3, 2):
-        g.pass_on(3, k)
+    g.step(3, 2)
+    g.step(4, 1)
     s1.back(0)
-    g.token_pass(1)
-    g.y_wait(1)
-    g.y_wait(3)
+    g.step(3, 3)
+    g.step(4, 2)
+    s1.back(1)
+    g.step(4, 3)
+    g.step(5, 1)
+    s1.back(2)
+    g.step(5, 2)
+    g.token_pass(1, 0, 3)
+    s1.back(3)
+    g.step(5, 3)
+    g.token_pass(1, 3, 6)
+    g.step(6, 1)
+    g.step(6, 2)
+    g.step(6, 3)
+    g.token_pass(1, 6, 8)
+    g.y_wait(2, 3, 4, 5, 6)
+    s1.close(0)
 
     @pl.loop(0, 4)
     def _(n):
         s1.ready(n)
-
-        @pl.when(n < 3)
-        def _():
-            s1.back(n + 1)
-
         rows = pl.ds(pl.multiple_of(n * 256, 256), 256)
-        h = pieces(xf, sorts, 1, n * 4, 4).astype(F32) + total[rows, :].astype(F32)
-        hidden[rows, :] = h
+        h = pieces(xf, sorts, 1, n * 4, 4).astype(F32) + pb[rows, :].astype(F32)
+        hidden[pl.ds(n * 4, 4)] = h.reshape(4, BLK, WIDTH)
         a = (h * unit(h)).astype(BF)
-        a2[rows, :] = a
+        pa[rows, :] = a
         wgu = wg[...].reshape(WIDTH, 1536)
         gu = jnp.dot(a, wgu, preferred_element_type=F32)
         gate = gu[:, :768]
@@ -792,7 +1053,7 @@
         du = (dm * silu).astype(BF)
         both = jnp.concatenate([dg, du], axis=1)
         dgu[rows, :] = both
-        dpart[rows, :] = dims(both, wgu, 1, 1).astype(BF)
+        pc[rows, :] = dims(both, wgu, 1, 1).astype(BF)
         s2.beside(n)
 
         @pl.when(n > 0)
@@ -800,6 +1061,21 @@
             s2.across(n - 1)
 
     s2.across(3)
+    s1.close(1, 2)
+
+    @pl.loop(0, 4)
+    def _(n):
+        rows = pl.ds(pl.multiple_of(n * 256, 256), 256)
+        m = pieces(mb, sorts, 0, n * 4, 4)
+        pb[rows, :] = jnp.dot(m, wd[...].reshape(768, WIDTH), preferred_element_type=F32).astype(BF)
+        rest[n] = pieces(hidden, sorts, 0, 4 * n + 2 * g.c, 2)
+
+    g.close()
+    near = [(q, 2 * z + 1 - y), (2 * x_ + 1 - c, p), (2 * (1 - x_) + c, p)]
+    near += [(q, 2 * mod(z + k, 4) + y) for k in (1, 2, 3)]
+    for peer in near:
+        pl.semaphore_signal(free, inc=1, device_id=peer, device_id_type=MESH)
+    s2.back(0)
 
     @pl.loop(0, 2)
     def _(n):
@@ -811,332 +1087,84 @@
                 v = dims(m_all[:, t * 384 : (t + 1) * 384], cs[...], 0, 0).astype(BF)
                 v = v.reshape(2, 2, 96, WIDTH)
                 for u in range(2):
-                    gd[u, 2 * t : 2 * t + 2] = v[:, u]
-
-        s2.back(n)
+                    gd[u, 0, 2 * t : 2 * t + 2] = v[:, u]
+
+    s2.back(1)
+    pl.semaphore_wait(free, len(near))
+    y_send(0)
+    for n in range(4):
+        h_out.beside(n)
 
     @pl.loop(0, 4)
     def _(n):
-        v = dims(a2[:, pl.ds(pl.multiple_of(n * 256, 256), 256)], dgu[...], 0, 0).astype(BF)
+        v = dims(pa[:, pl.ds(pl.multiple_of(n * 256, 256), 256)], dgu[...], 0, 0).astype(BF)
         v = v.reshape(4, 2, 32, 1536)
         for t in range(2):
             ggu[t, n] = v[:, t]
 
+        @pl.when(n == 0)
+        def _():
+            y_send(1)
+
         @pl.when(n < 2)
         def _():
             s2.back(n + 2)
-
-    @pl.loop(0, 4)
-    def _(n):
-        rows = pl.ds(pl.multiple_of(n * 256, 256), 256)
-        m = pieces(mb, sorts, 0, n * 4, 4)
-        part2[rows, :] = jnp.dot(m, wd[...].reshape(768, WIDTH), preferred_element_type=F32).astype(BF)
-
-    for n in range(4):
-        s2.ready(n)
-    s1.close()
-    s2.close()
-    g.close()
-
-
-def first_call(tok, cot, pos, pq, pg, po, pd, cosf, sinf, qg, kg):
-    sem = pltpu.SemaphoreType.DMA
-    shape = jax.ShapeDtypeStruct
-    vm = pltpu.VMEM
-    full = (TOKENS, WIDTH)
-    return pl.pallas_call(
-        first_kernel,
-        out_shape=(
-            shape((16, BLK, WIDTH), BF),
-            shape((8, 128), jnp.int32),
-            shape((4, 8) + pq.shape[1:], BF),
-            shape((8,) + po.shape, BF),
-            shape(full, BF),
-            shape((TOKENS, 768), F32),
-            shape((4, TOKENS, 128), BF),
-            shape((2, TOKENS, 128), BF),
-            shape((2, TOKENS, 128), BF),
-            shape((TOKENS, 512), BF),
-            shape((4, TOKENS, 1), F32),
-            shape(full, F32),
-            shape(full, BF),
-            shape(full, BF),
-            shape(full, BF),
-            shape((2, 4, 96, WIDTH), BF),
-            shape((2, 4, 4, 32, 1536), BF),
-        ),
-        in_specs=[ANY] * 7 + [VM] * 4,
-        out_specs=(VM, ANY) + (VM,) * 15,
-        scratch_shapes=[
-            vm((16, BLK, WIDTH), BF),
-            vm((4, 8) + pg.shape[1:], BF),
-            vm((8,) + pd.shape, BF),
-            vm(full, BF), vm(full, BF), vm(full, BF), vm(full, BF),
-            vm((16, BLK, 768), BF), vm((TOKENS, 1536), BF),
-        ]
-        + [vm((4, 128, WIDTH), BF)] * 6
-        + [pltpu.SMEM((8, 128), jnp.int32), sem((1,)), sem((12, 4))]
-        + [sem(n) for n in GATHER_SEMS],
-        compiler_params=pltpu.CompilerParams(
-            collective_id=0, has_side_effects=True, vmem_limit_bytes=VMEM_BYTES
-        ),
-        name="forward_and_mlp",
-    )(tok, cot, pos, pq, pg, po, pd, cosf, sinf, qg, kg)
-
-
-class Home:
-    def __init__(self, part, out, l1, own, l2, sems, here, base):
-        self.q, self.p, self.x, self.c, self.z, self.y = place()
-        self.part, self.out, self.l1, self.own, self.l2 = part, out, l1, own, l2
-        self.sems, self.here, self.base = sems, here, base
-        self.owner_x, self.owner_c = self.y, self.z // 2
-        self.keeps = self.x == self.owner_x
-        self.sib = (2 * self.x + 1 - self.c, self.p)
-        self.opp = (2 * (1 - self.x) + self.c, self.p)
-        self.goal_q = 2 * self.owner_x + self.owner_c
-
-    def rows(self, n, c):
-        return pl.ds(pl.multiple_of(n * 256 + c * 128, 128), 128)
-
-    def sem(self, k, n):
-        return self.sems.at[self.base + k, n]
-
-    def first(self, n):
-        return remote(
-            self.part.at[self.rows(n, 1 - self.c)], self.l1.at[n], self.sem(0, n), self.sem(1, n), self.sib
-        )
-
-    def second(self, n):
-        return remote(self.own.at[n], self.l2.at[n], self.sem(2, n), self.sem(3, n), self.opp)
-
-    def third(self, n):
-        slot = mod(self.z, 2)
-        return remote(
-            self.own.at[n], self.out.at[slot], self.sem(4, n), self.sem(5, slot), (self.goal_q, 2 * n + self.c)
-        )
-
-    def is_self(self, n):
-        return jnp.logical_and(self.goal_q == self.q, 2 * n + self.c == self.p)
-
-    def beside(self, n):
-        self.first(n).start()
-
-    def across(self, n):
-        self.first(n).wait_recv()
-        mine = self.part[self.rows(n, self.c), :].astype(F32)
-        self.own[n] = (mine + self.l1[n].astype(F32)).astype(BF)
-
-        @pl.when(jnp.logical_not(self.keeps))
-        def _():
-            self.second(n).start()
-
-    def finish(self, n, rest):
-        @pl.when(self.keeps)
-        def _():
-            self.second(n).wait_recv()
-            s = self.own[n].astype(F32) + self.l2[n].astype(F32)
-            self.own[n] = rest(n, s).astype(BF)
-
-            @pl.when(jnp.logical_not(self.is_self(n)))
-            def _():
-                self.third(n).start()
-
-            @pl.when(self.is_self(n))
-            def _():
-                cp = pltpu.make_async_copy(self.own.at[n], self.out.at[mod(self.z, 2)], self.here)
-                cp.start()
-                cp.wait()
-
-    def close(self):
-        for i in range(2):
-            group = 4 * self.c + 2 * i + self.x
-            same = jnp.logical_and(group == self.p, self.y == self.c)
-
-            @pl.when(jnp.logical_not(same))
-            def _():
-                remote(self.own.at[0], self.out.at[i], self.sem(4, 0), self.sem(5, i), (self.q, self.p)).wait_recv()
-
-        for n in range(4):
-            self.first(n).wait_send()
-
-            @pl.when(jnp.logical_not(self.keeps))
-            def _():
-                self.second(n).wait_send()
-
-            @pl.when(jnp.logical_and(self.keeps, jnp.logical_not(self.is_self(n))))
-            def _():
-                self.third(n).wait_send()
-
-
-class Scatter:
-    def __init__(self, g, ly, lz, sems, base):
-        self.q, self.p, _, _, self.z, self.y = place()
-        self.g, self.ly, self.lz, self.sems, self.base = g, ly, lz, sems, base
-
-    def y_copy(self, n):
-        s, r = self.sems.at[self.base + n, 0], self.sems.at[self.base + n, 1]
-        return remote(self.g.at[1 - self.y, n], self.ly.at[n], s, r, (self.q, 2 * self.z + 1 - self.y))
-
-    def z_copy(self, n, k):
-        t = mod(self.z + k, 4)
-        s, r = self.sems.at[self.base + n, 2 * k], self.sems.at[self.base + n, 2 * k + 1]
-        return remote(self.ly.at[n, t], self.lz.at[n, k - 1], s, r, (self.q, 2 * t + self.y))
-
-    def y_send(self, n):
-        self.y_copy(n).start()
-
-    def z_step(self, n):
-        self.y_copy(n).wait_recv()
-
-        @pl.loop(0, 4)
-        def _(t):
-            self.ly[n, t] = (self.ly[n, t].astype(F32) + self.g[self.y, n, t].astype(F32)).astype(BF)
-
-        for k in (1, 2, 3):
-            self.z_copy(n, k).start()
-
-    def z_sum(self, n):
-        for k in (1, 2, 3):
-            self.z_copy(n, k).wait_recv()
-        s = self.ly[n, self.z].astype(F32) + self.lz[n, 0].astype(F32)
-        return s + self.lz[n, 1].astype(F32) + self.lz[n, 2].astype(F32)
-
-    def close(self, count):
-        @pl.loop(0, count)
-        def _(n):
-            self.y_copy(n).wait_send()
-            for k in (1, 2, 3):
-                self.z_copy(n, k).wait_send()
-
-
-class Columns:
-    def __init__(self, scatter, r, land, out, sems, base):
-        self.scatter, self.r, self.land, self.out = scatter, r, land, out
-        self.sems, self.base = sems, base
-        self.q, self.p = scatter.q, scatter.p
-
-    def copy(self, t):
-        s, r = self.sems.at[self.base, t], self.sems.at[self.base + 1, self.q]
-        return remote(self.r.at[t], self.land.at[self.q], s, r, (t, self.p))
-
-    def step(self, t):
-        s = self.scatter.z_sum(t)
-        self.r[t] = s.astype(BF)
-
-        @pl.when(t != self.q)
-        def _():
-            self.copy(t).start()
-
-        @pl.when(t == self.q)
-        def _():
-            self.out[t] = s
-
-    def close(self):
-        @pl.loop(0, 4)
-        def _(t):
-            @pl.when(t != self.q)
-            def _():
-                r = self.sems.at[self.base + 1, t]
-                remote(self.r.at[t], self.land.at[t], self.sems.at[self.base, t], r, (self.q, self.p)).wait_recv()
-                self.out[t] = self.land[t].astype(F32)
-                self.copy(t).wait_send()
-
-
-def second_kernel(
-    spots, gd, ggu, part2, dtotal, hidden, cs, wo, wq, xhat, raw_i, qb, kb, vb, ob, lse, xf, cosf, sinf, qg, kg,
-    out, igrad, od, ogu, oo, oqkv, oheads,
-    dh, dy, dob, dqkv, dkv, go, gqkv, heads,
-    yd, ygu, yo, yqkv, zd, zgu, zo, zqkv, lgu, lqkv, rgu, rqkv, hy, hz, hdp,
-    l1, own, l2, l1b, ownb, l2b,
-    gsem, csem, hs, hr, homes, here,
-):
-    q, p, x_, c, z, y = place()
-    peers = [(2 * x_ + cc, mod(p + k, 8)) for k in range(1, 8) for cc in (0, 1)]
-    peers += [(mod(q + k, 4), p) for k in (1, 2, 3)]
-    greet(peers)
-    sd = Scatter(gd, yd, zd, gsem, 0)
-    sgu = Scatter(ggu, ygu, zgu, gsem, 1)
-    so = Scatter(go, yo, zo, gsem, 5)
-    sqkv = Scatter(gqkv, yqkv, zqkv, gsem, 6)
-    cgu = Columns(sgu, rgu, lgu, ogu, csem, 0)
-    cqkv = Columns(sqkv, rqkv, lqkv, oqkv, csem, 2)
-    h_out = Home(part2, out, l1, own, l2, homes, here.at[0], 0)
-    h_in = Home(dy, igrad, l1b, ownb, l2b, homes, here.at[1], 6)
-    sd.y_send(0)
-    for n in range(4):
-        h_out.beside(n)
-    for n in range(4):
-        sgu.y_send(n)
 
     @pl.loop(0, 4)
     def _(n):
         rows = pl.ds(pl.multiple_of(n * 256, 256), 256)
         h = hidden[pl.ds(n * 4, 4)].reshape(256, WIDTH)
         r = unit(h)
-        da = dtotal[rows, :].astype(F32)
+        s2.ready(n)
+        da = gqkv[n // 2, pl.ds(2 * (n % 2), 2)].reshape(256, WIDTH).astype(F32)
         back = r * da - h * (r * r * r * jnp.mean(h * da, axis=-1, keepdims=True))
         d = cs[rows, :].astype(F32) + back
-        dh[pl.ds(n * 4, 4)] = d.reshape(4, BLK, WIDTH)
+        hidden[pl.ds(n * 4, 4)] = d.reshape(4, BLK, WIDTH)
         low = d.astype(BF)
-        dy[rows, :] = low
+        pa[rows, :] = low
         do = dims(low, wo[...].reshape(512, WIDTH), 1, 1).astype(BF)
-        for t in range(4):
-            dob[t, rows, :] = do[:, t * 128 : (t + 1) * 128]
+        cs[rows, :512] = do
         h_out.across(n)
 
     @pl.loop(0, 2)
     def _(n):
-        v = dims(ob[:, pl.ds(pl.multiple_of(n * 256, 256), 256)], dy[...], 0, 0).astype(BF)
+        v = dims(ob[:, pl.ds(pl.multiple_of(n * 256, 256), 256)], pa[...], 0, 0).astype(BF)
         v = v.reshape(2, 2, 64, WIDTH)
         for t in range(2):
             go[t, 0, pl.ds(n * 2, 2)] = v[:, t]
 
-    so.y_send(0)
+    s2.close(0, 1, 2)
     heads[...] = jnp.zeros_like(heads)
     scale = HEAD_SIZE**-0.5
 
     def norm_back(dn, u, gain, rows):
-        dn = rotate_back(dn, cosf[rows, :], sinf[rows, :])
+        dn = rotate_back(dn, *turns(table[rows, :]))
         r = unit(u)
         gd_ = gain * dn
         du = r * gd_ - u * (r * r * r * jnp.mean(u * gd_, axis=-1, keepdims=True))
         return du.astype(BF), jnp.sum(dn * u * r, axis=0, keepdims=True)
 
     def result(n, s):
-        return s + pieces(hidden, spots, 0, 4 * n + 2 * c, 2)
+        return s + rest[n]
 
     def inward(n, s):
         v = xf[pl.ds(4 * n + 2 * c, 2)].reshape(128, WIDTH).astype(F32)
         r = unit(v)
         s = r * s - v * (r * r * r * jnp.mean(v * s, axis=-1, keepdims=True))
-        return s + pieces(dh, spots, 0, 4 * n + 2 * c, 2)
+        return s + pieces(hidden, sorts, 0, 4 * n + 2 * c, 2)
 
     @pl.loop(0, 2)
     def _(g):
         dkv[...] = jnp.zeros_like(dkv)
         for t in range(2):
-            if t == 0:
-
-                @pl.when(g == 0)
+            for turn in range(2):
+
+                @pl.when(g == turn)
                 def _():
-                    sd.z_step(0)
-
-                @pl.when(g == 1)
-                def _():
-                    sgu.z_step(2)
-                    sgu.z_step(3)
-            else:
-
-                @pl.when(g == 0)
-                def _():
-                    sgu.z_step(0)
-                    sgu.z_step(1)
-
-                @pl.when(g == 1)
-                def _():
-                    @pl.loop(0, 4)
-                    def _(n):
-                        h_out.finish(n, result)
+                    step(2 * turn + t)
+                    if turn == 1:
+                        h_out.finish(2 * t, result)
+                        h_out.finish(2 * t + 1, result)
 
             h = g * 2 + t
             lanes = pl.ds(pl.multiple_of(h * 128, 128), 128)
@@ -1145,25 +1173,25 @@
                 rows = slice(i * 256, length)
                 qv = qb[h, rows, :]
                 kv = kb[g, :length, :]
-                dov = dob[h, rows, :]
+                dov = cs[rows, lanes]
                 s = dims(qv, kv, 1, 1) * (scale * LOG2E)
-                pr = lower(jnp.exp2(s - lse[h, rows, :]), 0.0)
+                pr = lower(jnp.exp2(s - column(lse[rows, :], h)), 0.0)
                 dp = dims(dov, vb[g, :length, :], 1, 1)
                 delta = jnp.sum(dov.astype(F32) * ob[rows, lanes].astype(F32), axis=-1, keepdims=True)
                 ds_ = lower(pr * (dp - delta), 0.0).astype(BF)
                 dq = jnp.dot(ds_, kv, preferred_element_type=F32) * scale
                 dkv[0, :length, :] += dims(ds_, qv, 0, 0)
                 dkv[1, :length, :] += dims(pr.astype(BF), dov, 0, 0)
-                du, dgain = norm_back(dq, raw_i[rows, lanes], qg[...], pl.ds(i * 256, 256))
-                dqkv[i * 4 : i * 4 + 4, :, lanes] = du.reshape(4, BLK, 128)
+                du, dgain = norm_back(dq, raw_o[rows, lanes], qg[...], pl.ds(i * 256, 256))
+                cf[i * 4 : i * 4 + 4, :, lanes] = du.reshape(4, BLK, 128)
                 heads[0:1, :] += dgain
         lanes = pl.ds(pl.multiple_of(512 + g * 128, 128), 128)
         for i in range(4):
             rows = slice(i * 256, (i + 1) * 256)
-            du, dgain = norm_back(dkv[0, rows, :] * scale, raw_i[rows, lanes], kg[...], pl.ds(i * 256, 256))
-            dqkv[i * 4 : i * 4 + 4, :, lanes] = du.reshape(4, BLK, 128)
+            du, dgain = norm_back(dkv[0, rows, :] * scale, raw_o[rows, lanes], kg[...], pl.ds(i * 256, 256))
+            cf[i * 4 : i * 4 + 4, :, lanes] = du.reshape(4, BLK, 128)
             heads[1:2, :] += dgain
-        dqkv[:, :, pl.ds(pl.multiple_of(768 + g * 128, 128), 128)] = dkv[1].astype(BF).reshape(16, BLK, 128)
+        cf[:, :, pl.ds(pl.multiple_of(768 + g * 128, 128), 128)] = dkv[1].astype(BF).reshape(16, BLK, 128)
 
     hy_copy = remote(heads, hy, hs.at[0], hr.at[0], (q, 2 * z + 1 - y))
     hy_copy.start()
@@ -1171,8 +1199,8 @@
     @pl.loop(0, 4)
     def _(n):
         rows = pl.ds(pl.multiple_of(n * 256, 256), 256)
-        d = pieces(dqkv, spots, 0, n * 4, 4)
-        dy[rows, :] = dims(d, wq[...].reshape(WIDTH, WIDTH), 1, 1).astype(BF)
+        d = pieces(cf, sorts, 0, n * 4, 4)
+        pc[rows, :] = dims(d, wq[...].reshape(WIDTH, WIDTH), 1, 1).astype(BF)
         h_in.beside(n)
 
         @pl.when(n > 0)
@@ -1183,11 +1211,18 @@
 
     @pl.loop(0, 4)
     def _(n):
-        v = dims(xhat[:, pl.ds(pl.multiple_of(n * 256, 256), 256)], dqkv[...].reshape(TOKENS, WIDTH), 0, 0).astype(BF)
+        rows = pl.ds(pl.multiple_of(n * 256, 256), 256)
+        v = pieces(xf, sorts, 1, n * 4, 4).astype(F32)
+        pa[rows, :] = (v * unit(v)).astype(BF)
+
+    @pl.loop(0, 4)
+    def _(n):
+        v = dims(pa[:, pl.ds(pl.multiple_of(n * 256, 256), 256)], cf[...].reshape(TOKENS, WIDTH), 0, 0).astype(BF)
         v = v.reshape(4, 2, 32, WIDTH)
         for t in range(2):
             gqkv[t, n] = v[:, t]
-        sqkv.y_send(n)
+
+    step(4)
 
     def z_heads(k):
         return remote(hz.at[z], hz.at[z], hs.at[k], hr.at[k], (q, 2 * mod(z + k, 4) + y))
@@ -1199,15 +1234,14 @@
     hz[z] = heads[...] + hy[...]
     for k in (1, 2, 3):
         z_heads(k).start()
-    so.z_step(0)
+    h_in.finish(0, inward)
     od[...] = sd.z_sum(0)
-
-    @pl.loop(0, 4)
-    def _(n):
+    for n in range(4):
+        step(5 + n)
         cgu.step(n)
-        sqkv.z_step(n)
-        h_in.finish(n, inward)
-
+        if n < 3:
+            h_in.finish(n + 1, inward)
+    step(9)
     for k in (1, 2, 3):
         f = mod(z + 4 - k, 4)
         remote(hz.at[f], hz.at[f], hs.at[k], hr.at[k], (q, p)).wait_recv()
@@ -1238,43 +1272,52 @@
         dp_heads(k).wait_send()
 
 
-def second_call(spots, gd, ggu, part2, dtotal, hidden, cs, wo, wq, xhat, raw, qb, kb, vb, ob, lse, xf, cosf, sinf, qg, kg):
+def layer_call(tok, cot, pos, pq, pg, po, pd, table, qg, kg):
+    sem = pltpu.SemaphoreType.DMA
     shape = jax.ShapeDtypeStruct
-    sem = pltpu.SemaphoreType.DMA
     vm = pltpu.VMEM
     full = (TOKENS, WIDTH)
     return pl.pallas_call(
-        second_kernel,
+        layer_kernel,
         out_shape=(
             shape((2, 128, WIDTH), BF),
             shape((2, 128, WIDTH), BF),
             shape((96, WIDTH), F32),
-            shape((4, 32, 1536), F32),
+            shape((4, 32, 1536), BF),
             shape((64, WIDTH), F32),
-            shape((4, 32, WIDTH), F32),
+            shape((4, 32, WIDTH), BF),
             shape((8, 128), F32),
+            shape((8, 128), jnp.int32),
         ),
-        in_specs=[SM] + [VM] * 20,
-        out_specs=(VM,) * 7,
+        in_specs=[ANY] * 7 + [VM] * 3,
+        out_specs=(ANY, ANY) + (VM,) * 5 + (ANY,),
         scratch_shapes=[
-            vm((16, BLK, WIDTH), F32), vm(full, BF), vm((4, TOKENS, 128), BF), vm((16, BLK, WIDTH), BF),
-            vm((2, TOKENS, 128), F32), vm((2, 1, 4, 64, WIDTH), BF), vm((2, 4, 4, 32, WIDTH), BF),
-            vm((8, 128), F32),
-            vm((1, 4, 96, WIDTH), BF), vm((4, 4, 32, 1536), BF), vm((1, 4, 64, WIDTH), BF), vm((4, 4, 32, WIDTH), BF),
-            vm((1, 3, 96, WIDTH), BF), vm((4, 3, 32, 1536), BF), vm((1, 3, 64, WIDTH), BF), vm((4, 3, 32, WIDTH), BF),
-            vm((4, 32, 1536), BF), vm((4, 32, WIDTH), BF), vm((4, 32, 1536), BF), vm((4, 32, WIDTH), BF),
-            vm((8, 128), F32), vm((4, 8, 128), F32), vm((4, 8, 128), F32),
+            vm((16, BLK, WIDTH), BF), vm((16, BLK, WIDTH), BF),
+            vm((4, 8) + pq.shape[1:], BF), vm((4, 8) + pg.shape[1:], BF),
+            vm((8,) + po.shape, BF), vm((8,) + pd.shape, BF),
+            vm((TOKENS, 768), F32),
+            vm((4, TOKENS, 128), BF), vm((2, TOKENS, 128), BF), vm((2, TOKENS, 128), BF), vm((TOKENS, 512), BF),
+            vm((TOKENS, 128), F32), vm((16, BLK, WIDTH), F32), vm((4, 128, WIDTH), F32),
+            vm(full, BF), vm(full, BF), vm(full, BF), vm(full, BF),
+            vm((16, BLK, 768), BF), vm((TOKENS, 1536), BF),
+            vm((2, 1, 4, 96, WIDTH), BF), vm((2, 4, 4, 32, 1536), BF),
+            vm((2, TOKENS, 128), F32),
+            vm((2, 1, 4, 64, WIDTH), BF), vm((2, 4, 4, 32, WIDTH), BF),
+            vm((1, 4, 64, WIDTH), BF), vm((4, 4, 32, WIDTH), BF),
+            vm((1, 3, 64, WIDTH), BF), vm((4, 3, 32, WIDTH), BF),
+            vm((8, 128), F32), vm((8, 128), F32), vm((4, 8, 128), F32), vm((4, 8, 128), F32),
         ]
-        + [vm((4, 128, WIDTH), BF)] * 6
-        + [sem((10, 8)), sem((4, 4)), sem((7,)), sem((7,)), sem((12, 4)), sem((2,))],
+        + [vm((4, 128, WIDTH), BF)] * 7
+        + [
+            pltpu.SMEM((8, 128), jnp.int32), sem((1,)), pltpu.SemaphoreType.REGULAR, sem((12, 4)),
+            sem((10, 8)), sem((4, 4)), sem((7,)), sem((7,)), sem((12, 4)), sem((2,)),
+        ]
+        + [sem(n) for n in GATHER_SEMS],
         compiler_params=pltpu.CompilerParams(
-            collective_id=1, has_side_effects=True, vmem_limit_bytes=VMEM_BYTES
+            collective_id=0, has_side_effects=True, vmem_limit_bytes=VMEM_BYTES
         ),
-        name="backward_and_scatter",
-    )(
-        spots, gd.reshape(2, 1, 4, 96, WIDTH), ggu, part2, dtotal, hidden.reshape(16, BLK, WIDTH), cs, wo, wq, xhat,
-        raw, qb, kb, vb, ob, lse, xf, cosf, sinf, qg, kg,
-    )
+        name="layer_both_ways",
+    )(tok, cot, pos, pq, pg, po, pd, table, qg, kg)
 
 
 def quarter_columns(w, gain):
@@ -1299,21 +1342,16 @@
     inverse = jnp.sum(jnp.where(row[None, :] == spots[:, None], spots[None, :], 0), axis=1)
     pos = jnp.zeros((8, 128), jnp.int32)
     pos = pos.at[0, :16].set(row).at[1, :16].set(inverse)
-    freqs = BASE ** (-(lax.iota(F32, HEAD_SIZE // 2) * 2.0) / HEAD_SIZE)
-    angles = lax.iota(F32, TOKENS)[:, None] * freqs[None, :]
-    cosine = jnp.cos(angles)
-    sine = jnp.sin(angles)
-    cosf = jnp.concatenate([cosine, cosine], axis=1)
-    sinf = jnp.concatenate([-sine, sine], axis=1)
+    freqs = BASE ** (-np.arange(HEAD_SIZE // 2) * 2.0 / HEAD_SIZE)
+    angles = np.arange(TOKENS)[:, None] * freqs.astype(np.float32)[None, :].astype(np.float64)
+    table = np.concatenate([np.cos(angles), np.sin(angles)], axis=1).astype(np.float32)
     qg = query_head_gain.astype(F32)[None, :]
     kg = key_gain.astype(F32)[None, :]
-    xf, of, wq, wo, xhat, raw, qb, kb, vb, ob, lse, hidden, cs, part2, dtotal, gd, ggu = first_call(
+    out, igrad, od, ogu, oo, oqkv, oheads, _ = layer_call(
         tokens.reshape(2, 2, BLK, WIDTH), cotangent.reshape(2, 2, BLK, WIDTH), pos, pq, pg, w_out, w_down,
-        cosf, sinf, qg, kg,
+        table, qg, kg,
     )
-    out, igrad, od, ogu, oo, oqkv, oheads = second_call(
-        of, gd, ggu, part2, dtotal, hidden, cs, wo, wq, xhat, raw, qb, kb, vb, ob, lse, xf, cosf, sinf, qg, kg
-    )
+    ogu, oqkv = ogu.astype(F32), oqkv.astype(F32)
     return finish(
         out, igrad, od, ogu, oo, oqkv, oheads, ga, gm, w_query, key_projection, value_projection, w_gate, w_up
     )

time: 403 us -> 321 us (0.80); the launches traced: 397 us -> 320 us
  Pallas kernels: 373 us -> 300 us
  other arithmetic: 16 us -> 10.5 us
    pallas_call x2 -> x1, Pallas kernels: 373 us -> 300 us  [layer_call(): pl.pallas_call(layer_kernel, out_shape=(shape((2, 128, WIDTH), BF), shape...]
where the time goes in v3:
time: 321 us; the launch traced here: 320 us
  Pallas kernels  300 us (93%)
  other arithmetic  10.5 us (3%)
  local copies, waits for them, and re-layouts  8.87 us (3%)
    pallas_call x1, Pallas kernels, layer_call(): pl.pallas_call(layer_kernel, out_shape=(shape((2, 128, WIDTH), BF), shape...  300 us
    unnamed x39, local copies, waits for them, and re-layouts  7.27 us

profile of v3, /device:TPU:27, one launch (start us, length us, event | category | flops | bytes accessed | tf_op | source)
XLA Modules:
  0.0 320.2 jit_solution(498922435469845646)
XLA Ops:
  0.7 0.8 broadcast_select_fusion
  1.4 0.8 fusion.10
  2.2 0.1 select_reduce_fusion
  2.3 0.2 scatter.9.pos
  2.5 0.7 convert_element_type.50
  3.2 0.9 fusion.6
  4.2 0.9 copy-done.3
  5.0 0.1 fusion.4
  5.2 0.7 pad_maximum_fusion.1.pq
  5.9 0.2 copy-done
  6.2 0.1 copy-done.1
  6.3 0.1 fusion
  6.5 0.8 pad_maximum_fusion.pg
  7.3 0.5 bitcast_convert_fusion
  7.8 299.9 %layer_both_ways.1 = (bf16[2,128,1024]{2,1,0:T(8,128)(2,1)}, bf16[2,128,1024]{2,1,0:T(8,128)(2,1)}, f32[96,1024]{1,0:T(8,128)}, bf16[4,32,1536]{2,1,0:T(8,128)(2...) custom-call(bf16[2,2,64,1024]{3,2,1,0:T(8,128)(2,1)} %bitcast.71, ...), custom_call_target="tpu_custom_call" | custom-call | tf_op jit(solution)/shard_map/layer_both_ways/pallas_call | solution.py:1280
  307.7 1.1 convert_element_type.62
  308.8 0.1 slice_bitcast_fusion
  308.9 0.9 copy-done.2
  309.8 1.1 broadcast_multiply_fusion
  310.9 0.5 add.18
  311.6 0.8 copy-done.10
  312.4 0.9 broadcast_multiply_fusion.3
  313.4 0.9 broadcast_multiply_fusion.2
  314.3 0.5 add_add_fusion
  314.8 1.3 slice_bitcast_fusion.5
  316.1 0.8 copy.69
  316.9 0.4 copy-done.4
  317.3 0.8 copy.70
  318.1 0.3 copy-done.8
  318.4 0.7 copy.71
  319.1 0.4 copy-done.6
  319.5 0.7 copy.72
  (37 shorter events, 0.3 us)
Async XLA Ops:
  0.6 2.5 copy-start.9
  2.5 1.6 copy-start.12
  4.1 0.9 copy-start.3
  5.1 0.8 copy-start.15
  5.2 1.0 copy-start
  5.2 1.1 copy-start.1
  6.5 0.8 copy-start.13
  6.5 0.8 copy-start.14
  308.9 0.9 copy-start.2
  309.8 1.6 copy-start.7
  311.6 0.8 copy-start.10
  311.6 0.9 copy-start.11
  313.3 2.7 copy-start.5
  316.1 1.2 copy-start.4
  317.3 1.1 copy-start.8
  318.4 1.1 copy-start.6

commit v4 on v3

--- a/solution.py
+++ b/solution.py
@@ -378,6 +378,10 @@
     return q, p, q // 2, lax.rem(q, 2), p // 2, lax.rem(p, 2)
 
 
+def home_group(x, c, i):
+    return 4 * c + 2 * i + (x if i == 0 else 1 - x)
+
+
 def greet(peers):
     barrier = pltpu.get_barrier_semaphore()
     for peer in peers:
@@ -482,6 +486,7 @@
                 self.copy(step, n).wait_send()
 
 
+LINES = 6
 PIECES = ((0, None), (2, None), (1, 0), (1, 1), (1, 2), (1, 3), (3, None))
 
 
@@ -495,9 +500,9 @@
         self.tok, self.cot, self.pos, self.pq, self.pg, self.po, self.pd = srcs
         self.xf, self.cf, self.of, *self.w = dsts
         (self.loc, self.ts, self.tr, self.fs, self.fr, self.ps, self.pr,
-         self.as_, self.ar, self.zs, self.zr, self.ys, self.yr) = sems
+         self.as_, self.ar, self.zs, self.zr, self.ys, self.yr, self.ls, self.lr) = sems
         q, p, x, c, z, y = self.q, self.p, self.x, self.c, self.z, self.y
-        self.owner_x, self.owner_c = y, z // 2
+        self.owner_x, self.owner_c = mod(y + z, 2), z // 2
         self.is_owner = jnp.logical_and(x == self.owner_x, c == self.owner_c)
         self.cross = jnp.logical_and(x != self.owner_x, c == self.owner_c)
         self.sib = (2 * x + 1 - c, p)
@@ -568,6 +573,49 @@
         for piece in pieces_:
             self.spread(piece, self.z, True, True)
 
+    def line_copy(self, line, src, way):
+        v = self.view(LINES, 2 * src + line)
+        s = self.ls.at[line, src + (4 if way < 0 else 0)]
+        return remote(v, v, s, self.lr.at[line, src], (self.q, 2 * (self.z + way) + self.y))
+
+    def line_spread(self, line, src, up, down):
+        if up:
+
+            @pl.when(self.z < 3)
+            def _():
+                self.line_copy(line, src, 1).start()
+
+        if down:
+
+            @pl.when(self.z > 0)
+            def _():
+                self.line_copy(line, src, -1).start()
+
+    def lines_begin(self):
+        self.y_copy(LINES, self.z).start()
+        self.line_spread(self.y, self.z, True, True)
+
+    def lines_turn(self):
+        v = self.view(LINES, 2 * self.z + 1 - self.y)
+        remote(v, v, self.ys.at[LINES, self.z], self.yr.at[LINES, self.z], (self.q, self.p)).wait_recv()
+        self.line_spread(1 - self.y, self.z, True, True)
+
+    def line_step(self, other, dist):
+        line = 1 - self.y if other else self.y
+        low, high = self.z - dist, self.z + dist
+
+        @pl.when(low >= 0)
+        def _():
+            v = self.view(LINES, 2 * low + line)
+            remote(v, v, self.ls.at[line, 0], self.lr.at[line, low], (self.q, self.p)).wait_recv()
+            self.line_spread(line, low, True, False)
+
+        @pl.when(high < 4)
+        def _():
+            v = self.view(LINES, 2 * high + line)
+            remote(v, v, self.ls.at[line, 0], self.lr.at[line, high], (self.q, self.p)).wait_recv()
+            self.line_spread(line, high, False, True)
+
     def step(self, piece, dist):
         low, high = self.z - dist, self.z + dist
 
@@ -599,7 +647,7 @@
 
     def token_copy(self, a, i):
         src, dst = (self.tok, self.cot)[a], self.tok_dst(a)
-        goal = 4 * self.c + 2 * i + self.x
+        goal = home_group(self.x, self.c, i)
         return goal, remote(src.at[i], block(dst, self.p), self.ts.at[a, i], self.tr.at[a, self.p], (self.q, goal))
 
     def token_local(self, a, i):
@@ -694,7 +742,19 @@
         for n in range(2):
             for k in (1, 2, 3):
                 self.column_copy(n, k).wait_send()
-        for piece in range(len(PIECES)):
+        self.y_copy(LINES, self.z).wait_send()
+        for line in range(2):
+            for src in range(4):
+
+                @pl.when(jnp.logical_and(self.z < 3, src <= self.z))
+                def _():
+                    self.line_copy(line, src, 1).wait_send()
+
+                @pl.when(jnp.logical_and(self.z > 0, src >= self.z))
+                def _():
+                    self.line_copy(line, src, -1).wait_send()
+
+        for piece in range(LINES):
             for src in range(4):
                 self.y_copy(piece, src).wait_send()
 
@@ -710,7 +770,7 @@
         self.token_close(1)
 
 
-GATHER_SEMS = ((7,), (2, 2), (2, 8), (2, 2, 8), (2, 8), (3,), (1,), (2, 3), (2, 3), (7, 8), (7, 4), (7, 4), (7, 4))
+GATHER_SEMS = ((7,), (2, 2), (2, 8), (2, 2, 8), (2, 8), (3,), (1,), (2, 3), (2, 3), (7, 8), (7, 4), (7, 4), (7, 4), (2, 8), (2, 4))
 
 
 class Home:
@@ -718,7 +778,7 @@
         self.q, self.p, self.x, self.c, self.z, self.y = place()
         self.part, self.out, self.l1, self.own, self.l2 = part, out, l1, own, l2
         self.sems, self.here, self.base = sems, here, base
-        self.owner_x, self.owner_c = self.y, self.z // 2
+        self.owner_x, self.owner_c = mod(self.y + self.z, 2), self.z // 2
         self.keeps = self.x == self.owner_x
         self.sib = (2 * self.x + 1 - self.c, self.p)
         self.opp = (2 * (1 - self.x) + self.c, self.p)
@@ -778,7 +838,7 @@
 
     def close(self):
         for i in range(2):
-            group = 4 * self.c + 2 * i + self.x
+            group = home_group(self.x, self.c, i)
             same = jnp.logical_and(group == self.p, self.y == self.c)
 
             @pl.when(jnp.logical_not(same))
@@ -923,17 +983,18 @@
     sort.start()
     lse[...] = jnp.zeros_like(lse)
     g.step(0, 1)
-    g.token_pass(0, 0, 4)
+    g.token_pass(0, 0, 2)
     g.step(0, 2)
+    g.token_pass(0, 2, 4)
+    g.token_start(1)
+    g.step(0, 3)
+    g.token_pass(0, 4, 8)
     g.own_copy(2).wait()
     g.begin(1)
-    g.step(0, 3)
     g.own_copy(1).wait()
     g.column_wait(1)
     g.begin(2)
-    g.token_pass(0, 4, 8)
     g.own_copy(3).wait()
-    g.begin(3)
     sort.wait()
     g.y_wait(0)
 
@@ -943,15 +1004,10 @@
         v = pieces(xf, sorts, 1, n * 4, 4).astype(F32)
         h = (v * unit(v)).astype(BF)
 
-        @pl.when(n == 1)
-        def _():
-            g.step(1, 1)
-            g.begin(4)
-
-        @pl.when(n == 3)
-        def _():
-            g.step(1, 2)
-            g.step(2, 1)
+        @pl.when(n == 2)
+        def _():
+            g.token_pass(1, 0, 3)
+            g.begin(3)
 
         raw = jnp.dot(h, wq[...].reshape(WIDTH, WIDTH), preferred_element_type=F32)
         raw_o[rows, :] = raw[:, :768]
@@ -969,16 +1025,28 @@
 
     @pl.loop(0, 4)
     def _(h):
-        for turn, (piece, dist) in enumerate(((1, 3), (2, 2), (2, 3), (3, 1))):
-
-            @pl.when(h == turn)
-            def _():
-                g.step(piece, dist)
-                if turn == 0:
-                    g.begin(5)
-                if turn == 2:
-                    g.begin(6)
-                    g.token_start(1)
+        @pl.when(h == 0)
+        def _():
+            g.step(1, 1)
+            g.token_pass(1, 3, 6)
+
+        @pl.when(h == 1)
+        def _():
+            g.step(1, 2)
+            g.token_pass(1, 6, 8)
+            g.begin(4)
+
+        @pl.when(h == 2)
+        def _():
+            g.step(1, 3)
+            g.step(2, 1)
+            g.begin(5)
+
+        @pl.when(h == 3)
+        def _():
+            g.step(2, 2)
+            g.step(2, 3)
+            g.lines_begin()
 
         kv = h // 2
         for i in range(4):
@@ -1010,25 +1078,27 @@
             s1.across(n - 1)
 
     s1.across(3)
+    g.step(3, 1)
     g.step(3, 2)
-    g.step(4, 1)
     s1.back(0)
     g.step(3, 3)
+    g.step(4, 1)
+    s1.back(1)
+    g.lines_turn()
     g.step(4, 2)
-    s1.back(1)
     g.step(4, 3)
+    s1.back(2)
     g.step(5, 1)
-    s1.back(2)
+    g.line_step(False, 1)
     g.step(5, 2)
-    g.token_pass(1, 0, 3)
+    g.line_step(True, 1)
     s1.back(3)
     g.step(5, 3)
-    g.token_pass(1, 3, 6)
-    g.step(6, 1)
-    g.step(6, 2)
-    g.step(6, 3)
-    g.token_pass(1, 6, 8)
-    g.y_wait(2, 3, 4, 5, 6)
+    g.line_step(False, 2)
+    g.line_step(True, 2)
+    g.line_step(False, 3)
+    g.line_step(True, 3)
+    g.y_wait(2, 3, 4, 5)
     s1.close(0)
 
     @pl.loop(0, 4)
@@ -1063,6 +1133,18 @@
     s2.across(3)
     s1.close(1, 2)
 
+    @pl.loop(0, 2)
+    def _(n):
+        m_all = mb[...].reshape(TOKENS, 768)
+        for t in range(2):
+
+            @pl.when(n == t)
+            def _():
+                v = dims(m_all[:, t * 384 : (t + 1) * 384], cs[...], 0, 0).astype(BF)
+                v = v.reshape(2, 2, 96, WIDTH)
+                for u in range(2):
+                    gd[u, 0, 2 * t : 2 * t + 2] = v[:, u]
+
     @pl.loop(0, 4)
     def _(n):
         rows = pl.ds(pl.multiple_of(n * 256, 256), 256)
@@ -1076,18 +1158,6 @@
     for peer in near:
         pl.semaphore_signal(free, inc=1, device_id=peer, device_id_type=MESH)
     s2.back(0)
-
-    @pl.loop(0, 2)
-    def _(n):
-        m_all = mb[...].reshape(TOKENS, 768)
-        for t in range(2):
-
-            @pl.when(n == t)
-            def _():
-                v = dims(m_all[:, t * 384 : (t + 1) * 384], cs[...], 0, 0).astype(BF)
-                v = v.reshape(2, 2, 96, WIDTH)
-                for u in range(2):
-                    gd[u, 0, 2 * t : 2 * t + 2] = v[:, u]
 
     s2.back(1)
     pl.semaphore_wait(free, len(near))
@@ -1157,14 +1227,20 @@
     def _(g):
         dkv[...] = jnp.zeros_like(dkv)
         for t in range(2):
-            for turn in range(2):
-
-                @pl.when(g == turn)
+            if t == 0:
+
+                @pl.when(g == 1)
                 def _():
-                    step(2 * turn + t)
-                    if turn == 1:
-                        h_out.finish(2 * t, result)
-                        h_out.finish(2 * t + 1, result)
+                    step(1)
+            else:
+                for turn in range(2):
+
+                    @pl.when(g == turn)
+                    def _():
+                        step(2 * turn)
+                        if turn == 1:
+                            h_out.finish(0, result)
+                            h_out.finish(1, result)
 
             h = g * 2 + t
             lanes = pl.ds(pl.multiple_of(h * 128, 128), 128)
@@ -1193,6 +1269,9 @@
             heads[1:2, :] += dgain
         cf[:, :, pl.ds(pl.multiple_of(768 + g * 128, 128), 128)] = dkv[1].astype(BF).reshape(16, BLK, 128)
 
+    step(3)
+    h_out.finish(2, result)
+    h_out.finish(3, result)
     hy_copy = remote(heads, hy, hs.at[0], hr.at[0], (q, 2 * z + 1 - y))
     hy_copy.start()
 
@@ -1351,39 +1430,69 @@
         tokens.reshape(2, 2, BLK, WIDTH), cotangent.reshape(2, 2, BLK, WIDTH), pos, pq, pg, w_out, w_down,
         table, qg, kg,
     )
-    ogu, oqkv = ogu.astype(F32), oqkv.astype(F32)
     return finish(
-        out, igrad, od, ogu, oo, oqkv, oheads, ga, gm, w_query, key_projection, value_projection, w_gate, w_up
+        out, igrad, od, ogu, oo, oqkv, oheads, attn_gain[None, :], mlp_gain[None, :], w_query, key_projection, value_projection, w_gate, w_up
     )
 
 
-def finish(out, igrad, od, ogu, oo, oqkv, oheads, ga, gm, w_query, key_projection, value_projection, w_gate, w_up):
-    def join(part):
-        return jnp.transpose(part, (1, 0, 2)).reshape(part.shape[1], -1)
-
-    hq, hk, hv = join(oqkv[:, :, :512]), join(oqkv[:, :, 512:768]), join(oqkv[:, :, 768:])
-    hg, hu = join(ogu[:, :, :768]), join(ogu[:, :, 768:])
-
-    def along(w, h):
-        return jnp.sum(w.astype(F32) * h, axis=1)
-
-    grad_attn_gain = along(w_query, hq) + along(key_projection, hk) + along(value_projection, hv)
-    grad_mlp_gain = along(w_gate, hg) + along(w_up, hu)
-    return (
-        out,
-        igrad,
-        grad_attn_gain,
-        ga * hq,
-        ga * hk,
-        ga * hv,
-        oheads[0],
-        oheads[1],
-        oo,
-        grad_mlp_gain,
-        gm * hg,
-        gm * hu,
-        od,
-    )
+def finish_kernel(
+    out_i, igrad_i, od_i, ogu, oo_i, oqkv, oheads, ga, gm, w_query, key_projection, value_projection, w_gate, w_up,
+    out, igrad, attn, query, key, value, qgain, kgain, oo, mlp, gate, up, od,
+):
+    out[...] = out_i[...]
+    igrad[...] = igrad_i[...]
+    od[...] = od_i[...]
+    oo[...] = oo_i[...]
+    qgain[...] = oheads[0:1, :]
+    kgain[...] = oheads[1:2, :]
+    eye = lax.broadcasted_iota(jnp.int32, (32, 32), 0) == lax.broadcasted_iota(jnp.int32, (32, 32), 1)
+
+    def upright(row):
+        return jnp.sum(jnp.where(eye, jnp.broadcast_to(row, (32, 32)), 0.0), axis=1, keepdims=True)
+
+    def flat(col):
+        return jnp.sum(jnp.where(eye, jnp.broadcast_to(col, (32, 32)), 0.0), axis=0, keepdims=True)
+
+    for gain, grads, total, todo in (
+        (ga, oqkv, attn, ((w_query, query, 0, 512), (key_projection, key, 512, 256), (value_projection, value, 768, 256))),
+        (gm, ogu, mlp, ((w_gate, gate, 0, 768), (w_up, up, 768, 768))),
+    ):
+        g = upright(gain[...].astype(F32))
+        dot = jnp.zeros((32, 1), F32)
+        for w, o, first, width in todo:
+            for t in range(4):
+                h = grads[t, :, first : first + width].astype(F32)
+                lanes = slice(t * width, (t + 1) * width)
+                o[:, lanes] = g * h
+                dot = dot + jnp.sum(w[:, lanes].astype(F32) * h, axis=1, keepdims=True)
+        total[...] = flat(dot)
+
+
+def finish(*args):
+    shape = jax.ShapeDtypeStruct
+    ws = args[9:]
+    res = pl.pallas_call(
+        finish_kernel,
+        out_shape=(
+            shape(args[0].shape, BF),
+            shape(args[1].shape, BF),
+            shape((1, 32), F32),
+            *[shape(w.shape, F32) for w in ws[:3]],
+            shape((1, 128), F32),
+            shape((1, 128), F32),
+            shape(args[4].shape, F32),
+            shape((1, 32), F32),
+            *[shape(w.shape, F32) for w in ws[3:]],
+            shape(args[2].shape, F32),
+        ),
+        in_specs=[VM] * 14,
+        out_specs=(VM,) * 13,
+        name="gains_and_layout",
+    )(*args)
+    res = list(res)
+    for i in (2, 6, 7, 9):
+        res[i] = res[i].reshape(-1)
+    return tuple(res)
 
 
 def layer(tokens, *rest):

time: 321 us -> 297 us (0.925)
  Pallas kernels: 300 us -> 287 us
  other arithmetic: 10.5 us -> 3.36 us
  local copies, waits for them, and re-layouts: 8.87 us -> 4.04 us
    pallas_call x1, Pallas kernels: 300 us -> 283 us  [layer_call(): pl.pallas_call(layer_kernel, out_shape=(shape((2, 128, WIDTH), BF), shape...]
    pallas_call x0 -> x1, Pallas kernels: none -> 3.62 us  [finish(): pl.pallas_call(finish_kernel, out_shape=(shape(args[0].shape, BF), shape(...]
    unnamed x39 -> x20, local copies, waits for them, and re-layouts: 7.27 us -> 3.86 us
where the time goes in v4:
time: 297 us; the launch traced here: 295 us
  Pallas kernels  287 us (97%)
  local copies, waits for them, and re-layouts  4.04 us (1%)
  other arithmetic  3.36 us (1%)
    pallas_call x1, Pallas kernels, layer_call(): pl.pallas_call(layer_kernel, out_shape=(shape((2, 128, WIDTH), BF), shape...  283 us

profile of v4, /device:TPU:27, one launch (start us, length us, event | category | flops | bytes accessed | tf_op | source)
XLA Modules:
  0.0 295.4 jit_solution(14988970011176025259)
XLA Ops:
  0.7 0.0 copy-start.8
  0.7 0.6 copy-done.8
  1.3 0.0 copy-start.9
  1.3 0.7 copy-done.9
  2.0 0.0 copy-start.5
  2.0 0.7 copy-done.5
  2.7 0.1 select_reduce_fusion
  2.8 0.0 copy-start.6
  2.8 0.0 copy-start.7
  2.8 0.6 copy-done.6
  3.4 0.0 copy-done.7
  3.5 0.5 bitcast_convert_fusion
  4.0 0.1 scatter.9.pos
  4.1 0.0 copy-start.4
  4.1 1.0 multiply_convert_fusion.2
  5.1 0.0 copy-done.4
  5.1 0.0 copy-start.2
  5.2 0.0 copy-start.3
  5.2 0.8 copy-done.2
  6.0 0.0 copy-done.3
  6.0 0.1 multiply_convert_fusion.4
  6.1 0.0 copy-start
  6.1 0.0 copy-start.1
  6.2 0.7 pad_maximum_fusion.1.pq
  6.9 0.2 copy-done
  7.1 0.1 copy-done.1
  7.2 0.1 multiply_convert_fusion.1
  7.4 0.8 pad_maximum_fusion.pg
  8.2 283.5 %layer_both_ways.1 = (bf16[2,128,1024]{2,1,0:T(8,128)(2,1)}, bf16[2,128,1024]{2,1,0:T(8,128)(2,1)}, f32[96,1024]{1,0:T(8,128)}, bf16[4,32,1536]{2,1,0:T(8,128)(2...) custom-call(bf16[2,2,64,1024]{3,2,1,0:T(8,128)(2,1)} %bitcast.48, ...), custom_call_target="tpu_custom_call" | custom-call | tf_op jit(solution)/shard_map/layer_both_ways/pallas_call | solution.py:1359
  291.7 3.6 %gains_and_layout.1 = (bf16[2,128,1024]{2,1,0:T(8,128)(2,1)}, bf16[2,128,1024]{2,1,0:T(8,128)(2,1)}, f32[1,32]{1,0:T(1,128)}, f32[32,2048]{1,0:T(8,128)}, f32[32...) custom-call(bf16[2,128,1024]{2,1,0:T(8,128)(2,1)} %get-tuple-element, ...), custom_call_target="tpu_custom_call" | custom-call | tf_op jit(solution)/shard_map/gains_and_layout/pallas_call | solution.py:1474
  (8 shorter events, 0.1 us)
Async XLA Ops:
  0.7 0.7 copy-start.8
  1.3 0.7 copy-start.9
  2.0 0.7 copy-start.5
  2.8 0.7 copy-start.6
  2.8 0.7 copy-start.7
  4.1 1.0 copy-start.4
  5.1 0.8 copy-start.2
  5.2 0.9 copy-start.3
  6.1 1.0 copy-start
  6.1 1.1 copy-start.1

commit v5 on v4

--- a/solution.py
+++ b/solution.py
@@ -882,12 +882,51 @@
         def _(t):
             ly[t] = (ly[t].astype(F32) + self.g[self.y, n, t].astype(F32)).astype(BF)
 
-        for k in (1, 2, 3):
-            self.z_copy(n, k).start()
+        lz = self.lz(n)
+        z = self.z
+
+        @pl.when(z != 3)
+        def _():
+            self.z_copy(n, 1).start()
+
+        @pl.when(z != 0)
+        def _():
+            self.z_copy(n, 3).start()
+
+        for end, unused in ((0, 0), (3, 2)):
+
+            @pl.when(z == end)
+            def _():
+                self.z_copy(n, 2).start()
+                self.relay_copy(n).start()
+                lz[unused] = jnp.zeros(lz.shape[1:], BF)
+
+    def relay_copy(self, n):
+        s, r = self.sems.at[self.base + n, 8], self.sems.at[self.base + n, 9]
+        near = 1 + self.z // 3
+        return remote(self.ly(n).at[3 - self.z], self.lz(n).at[3], s, r, (self.q, 2 * near + self.y))
+
+    def relay(self, n):
+        @pl.when(jnp.logical_and(self.z > 0, self.z < 3))
+        def _():
+            ly, lz = self.ly(n), self.lz(n)
+            t = mod(self.z + 2, 4)
+            s, r = self.sems.at[self.base + n, 8], self.sems.at[self.base + n, 9]
+            remote(ly.at[t], lz.at[3], s, r, (self.q, self.p)).wait_recv()
+            ly[t] = (ly[t].astype(F32) + lz[3].astype(F32)).astype(BF)
+            self.z_copy(n, 2).start()
 
     def z_sum(self, n):
-        for k in (1, 2, 3):
-            self.z_copy(n, k).wait_recv()
+        @pl.when(self.z != 0)
+        def _():
+            self.z_copy(n, 1).wait_recv()
+
+        self.z_copy(n, 2).wait_recv()
+
+        @pl.when(self.z != 3)
+        def _():
+            self.z_copy(n, 3).wait_recv()
+
         ly, lz = self.ly(n), self.lz(n)
         return ly[self.z].astype(F32) + lz[0].astype(F32) + lz[1].astype(F32) + lz[2].astype(F32)
 
@@ -895,8 +934,19 @@
         @pl.loop(0, count)
         def _(n):
             self.y_copy(n).wait_send()
-            for k in (1, 2, 3):
-                self.z_copy(n, k).wait_send()
+            self.z_copy(n, 2).wait_send()
+
+            @pl.when(self.z != 3)
+            def _():
+                self.z_copy(n, 1).wait_send()
+
+            @pl.when(self.z != 0)
+            def _():
+                self.z_copy(n, 3).wait_send()
+
+            @pl.when(jnp.logical_or(self.z == 0, self.z == 3))
+            def _():
+                self.relay_copy(n).wait_send()
 
 
 class Columns:
@@ -938,15 +988,15 @@
 
 
 def layer_kernel(
-    tok, cot, pos, pq, pg, po, pd, table, qg, kg,
+    tok, cot, pos, po, pd, table, qg, kg, ga, gm, w_query, key_projection, value_projection, w_gate, w_up,
     out, igrad, od, ogu, oo, oqkv, oheads, of,
     xf, cf, wq, wg, wo, wd, raw_o, qb, kb, vb, ob, lse, hidden, rest, cs, pa, pb, pc, mb, dgu, gd, ggu,
     dkv, go, gqkv, yo, yqkv, zo, zqkv, heads, hy, hz, hdp,
-    l1, own, l2, l1b, ownb, l2b, l2c, sorts, sorts_sem, free, sums, gsem, csem, hs, hr, homes, here, *sems,
+    l1, own, l2, l1b, ownb, l2b, l2c, rows_of_two, sorts, sorts_sem, free, sums, gsem, csem, hs, hr, homes, here, *sems,
 ):
     q, p, x_, c, z, y = place()
-    sd = Scatter(gd, lambda n: wd.at[pl.ds(0, 4)], lambda n: wd.at[pl.ds(4, 3)], gsem, 0)
-    sgu = Scatter(ggu, lambda n: wg.at[n, pl.ds(0, 4)], lambda n: wg.at[n, pl.ds(4, 3)], gsem, 1)
+    sd = Scatter(gd, lambda n: wd.at[pl.ds(0, 4)], lambda n: wd.at[pl.ds(4, 4)], gsem, 0)
+    sgu = Scatter(ggu, lambda n: wg.at[n, pl.ds(0, 4)], lambda n: wg.at[n, pl.ds(4, 4)], gsem, 1)
     so = Scatter(go, lambda n: yo.at[n], lambda n: zo.at[n], gsem, 5)
     sqkv = Scatter(gqkv, lambda n: yqkv.at[n], lambda n: zqkv.at[n], gsem, 6)
     cgu = Columns(sgu, ogu, csem, 0)
@@ -959,12 +1009,28 @@
         which, n = order[j]
         which.y_send(n)
 
+    def relay(j):
+        which, n = order[j]
+        which.relay(n)
+
     def step(j):
         which, n = order[j]
         which.z_step(n)
         if j + 2 < len(order):
             y_send(j + 2)
-
+        if j > 0:
+            relay(j - 1)
+
+    pq, pg = yqkv.at[0], ggu.at[0, 0]
+    for gain, dst, todo in (
+        (ga, pq, ((w_query, 0, 512), (key_projection, 512, 256), (value_projection, 768, 256))),
+        (gm, pg, ((w_gate, 0, 768), (w_up, 768, 768))),
+    ):
+        up = upright(gain[...].astype(F32))
+        for w, first, width in todo:
+            for t in range(4):
+                v = w[:, t * width : (t + 1) * width].astype(F32) * up
+                dst[t, :, first : first + width] = v.astype(BF)
     g = Gather((tok, cot, pos, pq, pg, po, pd), (xf, cf, of, wq, wg, wo, wd), sems)
     peers = [(2 * x_ + cc, mod(p + k, 8)) for k in range(1, 8) for cc in (0, 1)]
     peers += [(mod(q + k, 4), p) for k in (1, 2, 3)]
@@ -979,7 +1045,7 @@
     g.column_wait(0)
     g.begin(0)
     g.pos_finish()
-    sort = pltpu.make_async_copy(of, sorts, sorts_sem.at[0])
+    sort = pltpu.make_async_copy(of, rows_of_two, sorts_sem.at[0])
     sort.start()
     lse[...] = jnp.zeros_like(lse)
     g.step(0, 1)
@@ -993,9 +1059,16 @@
     g.begin(1)
     g.own_copy(1).wait()
     g.column_wait(1)
-    g.begin(2)
+    g.begin(2, 3)
     g.own_copy(3).wait()
     sort.wait()
+    slot = mod(z, 2)
+    for j in range(16):
+        sorts[0, j] = rows_of_two[slot, j]
+        where = jnp.int32(0)
+        for b in range(16):
+            where = jnp.where(rows_of_two[slot, b] == j, b, where)
+        sorts[1, j] = where
     g.y_wait(0)
 
     @pl.loop(0, 4)
@@ -1007,7 +1080,7 @@
         @pl.when(n == 2)
         def _():
             g.token_pass(1, 0, 3)
-            g.begin(3)
+            g.begin(4)
 
         raw = jnp.dot(h, wq[...].reshape(WIDTH, WIDTH), preferred_element_type=F32)
         raw_o[rows, :] = raw[:, :768]
@@ -1034,19 +1107,18 @@
         def _():
             g.step(1, 2)
             g.token_pass(1, 6, 8)
-            g.begin(4)
+            g.begin(5)
 
         @pl.when(h == 2)
         def _():
             g.step(1, 3)
             g.step(2, 1)
-            g.begin(5)
+            g.lines_begin()
 
         @pl.when(h == 3)
         def _():
             g.step(2, 2)
             g.step(2, 3)
-            g.lines_begin()
 
         kv = h // 2
         for i in range(4):
@@ -1321,6 +1393,7 @@
         if n < 3:
             h_in.finish(n + 1, inward)
     step(9)
+    relay(9)
     for k in (1, 2, 3):
         f = mod(z + 4 - k, 4)
         remote(hz.at[f], hz.at[f], hs.at[k], hr.at[k], (q, p)).wait_recv()
@@ -1351,7 +1424,7 @@
         dp_heads(k).wait_send()
 
 
-def layer_call(tok, cot, pos, pq, pg, po, pd, table, qg, kg):
+def layer_call(tok, cot, pos, po, pd, table, qg, kg, *rest):
     sem = pltpu.SemaphoreType.DMA
     shape = jax.ShapeDtypeStruct
     vm = pltpu.VMEM
@@ -1368,11 +1441,11 @@
             shape((8, 128), F32),
             shape((8, 128), jnp.int32),
         ),
-        in_specs=[ANY] * 7 + [VM] * 3,
+        in_specs=[ANY] * 5 + [VM] * 10,
         out_specs=(ANY, ANY) + (VM,) * 5 + (ANY,),
         scratch_shapes=[
             vm((16, BLK, WIDTH), BF), vm((16, BLK, WIDTH), BF),
-            vm((4, 8) + pq.shape[1:], BF), vm((4, 8) + pg.shape[1:], BF),
+            vm((4, 8, 32, WIDTH), BF), vm((4, 8, 32, 1536), BF),
             vm((8,) + po.shape, BF), vm((8,) + pd.shape, BF),
             vm((TOKENS, 768), F32),
             vm((4, TOKENS, 128), BF), vm((2, TOKENS, 128), BF), vm((2, TOKENS, 128), BF), vm((TOKENS, 512), BF),
@@ -1383,56 +1456,53 @@
             vm((2, TOKENS, 128), F32),
             vm((2, 1, 4, 64, WIDTH), BF), vm((2, 4, 4, 32, WIDTH), BF),
             vm((1, 4, 64, WIDTH), BF), vm((4, 4, 32, WIDTH), BF),
-            vm((1, 3, 64, WIDTH), BF), vm((4, 3, 32, WIDTH), BF),
+            vm((1, 4, 64, WIDTH), BF), vm((4, 4, 32, WIDTH), BF),
             vm((8, 128), F32), vm((8, 128), F32), vm((4, 8, 128), F32), vm((4, 8, 128), F32),
         ]
         + [vm((4, 128, WIDTH), BF)] * 7
         + [
-            pltpu.SMEM((8, 128), jnp.int32), sem((1,)), pltpu.SemaphoreType.REGULAR, sem((12, 4)),
-            sem((10, 8)), sem((4, 4)), sem((7,)), sem((7,)), sem((12, 4)), sem((2,)),
+            pltpu.SMEM((8, 128), jnp.int32), pltpu.SMEM((2, 16), jnp.int32), sem((1,)), pltpu.SemaphoreType.REGULAR, sem((12, 4)),
+            sem((10, 10)), sem((4, 4)), sem((7,)), sem((7,)), sem((12, 4)), sem((2,)),
         ]
         + [sem(n) for n in GATHER_SEMS],
         compiler_params=pltpu.CompilerParams(
             collective_id=0, has_side_effects=True, vmem_limit_bytes=VMEM_BYTES
         ),
         name="layer_both_ways",
-    )(tok, cot, pos, pq, pg, po, pd, table, qg, kg)
-
-
-def quarter_columns(w, gain):
-    rows, cols = w.shape
-    v = w if gain is None else (w.astype(F32) * gain).astype(BF)
-    return jnp.transpose(v.reshape(rows, 4, cols // 4), (1, 0, 2))
+    )(tok, cot, pos, po, pd, table, qg, kg, *rest)
 
 
 def whole_sequences(
     tokens, attn_gain, w_query, key_projection, value_projection, query_head_gain, key_gain, w_out,
     mlp_gain, w_gate, w_up, w_down, cotangent, span_order,
 ):
-    p = lax.axis_index("seq")
-    ga = attn_gain.astype(F32)[:, None]
-    gm = mlp_gain.astype(F32)[:, None]
-    pq = jnp.concatenate(
-        [quarter_columns(w, ga) for w in (w_query, key_projection, value_projection)], axis=2
-    )
-    pg = jnp.concatenate([quarter_columns(w, gm) for w in (w_gate, w_up)], axis=2)
-    row = jnp.where(lax.rem(p // 2, 2) == 0, span_order[0], span_order[1])
-    spots = lax.iota(jnp.int32, 16)
-    inverse = jnp.sum(jnp.where(row[None, :] == spots[:, None], spots[None, :], 0), axis=1)
-    pos = jnp.zeros((8, 128), jnp.int32)
-    pos = pos.at[0, :16].set(row).at[1, :16].set(inverse)
+    pos = jnp.pad(span_order, ((0, 6), (0, 112)))
+    gains = attn_gain[None, :], mlp_gain[None, :]
+    weights = w_query, key_projection, value_projection, w_gate, w_up
     freqs = BASE ** (-np.arange(HEAD_SIZE // 2) * 2.0 / HEAD_SIZE)
     angles = np.arange(TOKENS)[:, None] * freqs.astype(np.float32)[None, :].astype(np.float64)
     table = np.concatenate([np.cos(angles), np.sin(angles)], axis=1).astype(np.float32)
     qg = query_head_gain.astype(F32)[None, :]
     kg = key_gain.astype(F32)[None, :]
     out, igrad, od, ogu, oo, oqkv, oheads, _ = layer_call(
-        tokens.reshape(2, 2, BLK, WIDTH), cotangent.reshape(2, 2, BLK, WIDTH), pos, pq, pg, w_out, w_down,
-        table, qg, kg,
+        tokens.reshape(2, 2, BLK, WIDTH), cotangent.reshape(2, 2, BLK, WIDTH), pos, w_out, w_down,
+        table, qg, kg, *gains, *weights,
     )
-    return finish(
-        out, igrad, od, ogu, oo, oqkv, oheads, attn_gain[None, :], mlp_gain[None, :], w_query, key_projection, value_projection, w_gate, w_up
-    )
+    return finish(out, igrad, od, ogu, oo, oqkv, oheads, *gains, *weights)
+
+
+def diagonal(v):
+    i = lax.broadcasted_iota(jnp.int32, (32, 32), 0)
+    j = lax.broadcasted_iota(jnp.int32, (32, 32), 1)
+    return jnp.where(i == j, jnp.broadcast_to(v, (32, 32)), 0.0)
+
+
+def upright(row):
+    return jnp.sum(diagonal(row), axis=1, keepdims=True)
+
+
+def flat_row(col):
+    return jnp.sum(diagonal(col), axis=0, keepdims=True)
 
 
 def finish_kernel(
@@ -1445,14 +1515,6 @@
     oo[...] = oo_i[...]
     qgain[...] = oheads[0:1, :]
     kgain[...] = oheads[1:2, :]
-    eye = lax.broadcasted_iota(jnp.int32, (32, 32), 0) == lax.broadcasted_iota(jnp.int32, (32, 32), 1)
-
-    def upright(row):
-        return jnp.sum(jnp.where(eye, jnp.broadcast_to(row, (32, 32)), 0.0), axis=1, keepdims=True)
-
-    def flat(col):
-        return jnp.sum(jnp.where(eye, jnp.broadcast_to(col, (32, 32)), 0.0), axis=0, keepdims=True)
-
     for gain, grads, total, todo in (
         (ga, oqkv, attn, ((w_query, query, 0, 512), (key_projection, key, 512, 256), (value_projection, value, 768, 256))),
         (gm, ogu, mlp, ((w_gate, gate, 0, 768), (w_up, up, 768, 768))),
@@ -1465,7 +1527,7 @@
                 lanes = slice(t * width, (t + 1) * width)
                 o[:, lanes] = g * h
                 dot = dot + jnp.sum(w[:, lanes].astype(F32) * h, axis=1, keepdims=True)
-        total[...] = flat(dot)
+        total[...] = flat_row(dot)
 
 
 def finish(*args):

time: 297 us -> 286 us (0.963)
  Pallas kernels: 287 us -> 281 us
    pallas_call x1, Pallas kernels: 283 us -> 277 us  [layer_call(): pl.pallas_call(layer_kernel, out_shape=(shape((2, 128, WIDTH), BF), shape...]
where the time goes in v5:
time: 286 us; the launch traced here: 284 us
  Pallas kernels  281 us (98%)
    pallas_call x1, Pallas kernels, layer_call(): pl.pallas_call(layer_kernel, out_shape=(shape((2, 128, WIDTH), BF), shape...  277 us

profile of v5, /device:TPU:27, one launch (start us, length us, event | category | flops | bytes accessed | tf_op | source)
XLA Modules:
  0.0 284.3 jit_solution(12091313947129155386)
XLA Ops:
  0.6 0.0 copy-start.1
  0.7 0.0 copy-start.2
  0.7 0.6 copy-done.1
  1.3 0.0 copy-done.2
  1.3 0.5 bitcast_convert_fusion
  1.8 0.0 copy-start
  1.8 0.7 copy-done
  2.5 0.6 pad.4.pos
  3.1 277.4 %layer_both_ways.1 = (bf16[2,128,1024]{2,1,0:T(8,128)(2,1)}, bf16[2,128,1024]{2,1,0:T(8,128)(2,1)}, f32[96,1024]{1,0:T(8,128)}, bf16[4,32,1536]{2,1,0:T(8,128)(2...) custom-call(bf16[2,2,64,1024]{3,2,1,0:T(8,128)(2,1)} %bitcast.14, ...), custom_call_target="tpu_custom_call" | custom-call | tf_op jit(solution)/shard_map/layer_both_ways/pallas_call | solution.py:1432
  280.5 3.6 %gains_and_layout.1 = (bf16[2,128,1024]{2,1,0:T(8,128)(2,1)}, bf16[2,128,1024]{2,1,0:T(8,128)(2,1)}, f32[1,32]{1,0:T(1,128)}, f32[32,2048]{1,0:T(8,128)}, f32[32...) custom-call(bf16[2,128,1024]{2,1,0:T(8,128)(2,1)} %get-tuple-element, ...), custom_call_target="tpu_custom_call" | custom-call | tf_op jit(solution)/shard_map/gains_and_layout/pallas_call | solution.py:1536
Async XLA Ops:
  0.6 0.7 copy-start.1
  0.7 0.7 copy-start.2
  1.8 0.7 copy-start

commit v6 on v5

--- a/solution.py
+++ b/solution.py
@@ -950,27 +950,30 @@
 
 
 class Columns:
-    def __init__(self, scatter, land, sems, base):
-        self.scatter, self.land = scatter, land
+    def __init__(self, scatter, out, sems, base, here):
+        self.scatter, self.out, self.here = scatter, out, here
         self.sems, self.base = sems, base
         self.q, self.p = scatter.q, scatter.p
 
     def copy(self, t):
         s, r = self.sems.at[self.base, t], self.sems.at[self.base + 1, self.q]
-        return remote(self.scatter.ly(t).at[self.scatter.z], self.land.at[self.q], s, r, (t, self.p))
+        return remote(self.scatter.ly(t).at[self.scatter.z], self.out.at[self.q], s, r, (t, self.p))
+
+    def own(self, t):
+        return pltpu.make_async_copy(self.scatter.ly(t).at[self.scatter.z], self.out.at[t], self.here)
 
     def step(self, t):
         s = self.scatter.z_sum(t).astype(BF)
+        ly = self.scatter.ly(t)
+        ly[self.scatter.z] = s
 
         @pl.when(t != self.q)
         def _():
-            ly = self.scatter.ly(t)
-            ly[self.scatter.z] = s
             self.copy(t).start()
 
         @pl.when(t == self.q)
         def _():
-            self.land[t] = s
+            self.own(t).start()
 
     def close(self):
         for t in range(4):
@@ -978,8 +981,12 @@
             @pl.when(t != self.q)
             def _():
                 r = self.sems.at[self.base + 1, t]
-                remote(self.land.at[t], self.land.at[t], self.sems.at[self.base, t], r, (self.q, self.p)).wait_recv()
+                remote(self.out.at[t], self.out.at[t], self.sems.at[self.base, t], r, (self.q, self.p)).wait_recv()
                 self.copy(t).wait_send()
+
+            @pl.when(t == self.q)
+            def _():
+                self.own(t).wait()
 
 
 def column(table, h):
@@ -991,16 +998,16 @@
     tok, cot, pos, po, pd, table, qg, kg, ga, gm, w_query, key_projection, value_projection, w_gate, w_up,
     out, igrad, od, ogu, oo, oqkv, oheads, of,
     xf, cf, wq, wg, wo, wd, raw_o, qb, kb, vb, ob, lse, hidden, rest, cs, pa, pb, pc, mb, dgu, gd, ggu,
-    dkv, go, gqkv, yo, yqkv, zo, zqkv, heads, hy, hz, hdp,
-    l1, own, l2, l1b, ownb, l2b, l2c, rows_of_two, sorts, sorts_sem, free, sums, gsem, csem, hs, hr, homes, here, *sems,
+    dkv, go, gqkv, yo, yqkv, zo, zqkv, sums_d, sums_o, heads, hy, hz, hdp,
+    l1, own, l2, l1b, ownb, l2b, l2c, rows_of_two, sorts, sorts_sem, free, sums, gsem, csem, hs, hr, homes, here, kept, *sems,
 ):
     q, p, x_, c, z, y = place()
     sd = Scatter(gd, lambda n: wd.at[pl.ds(0, 4)], lambda n: wd.at[pl.ds(4, 4)], gsem, 0)
     sgu = Scatter(ggu, lambda n: wg.at[n, pl.ds(0, 4)], lambda n: wg.at[n, pl.ds(4, 4)], gsem, 1)
     so = Scatter(go, lambda n: yo.at[n], lambda n: zo.at[n], gsem, 5)
     sqkv = Scatter(gqkv, lambda n: yqkv.at[n], lambda n: zqkv.at[n], gsem, 6)
-    cgu = Columns(sgu, ogu, csem, 0)
-    cqkv = Columns(sqkv, oqkv, csem, 2)
+    cgu = Columns(sgu, ogu, csem, 0, kept.at[0])
+    cqkv = Columns(sqkv, oqkv, csem, 2, kept.at[1])
     h_out = Home(pb, out, l1, own, l2, homes, here.at[0], 0)
     h_in = Home(pc, igrad, l1b, ownb, l2c, homes, here.at[1], 6)
     order = [(sd, 0)] + [(sgu, n) for n in range(4)] + [(so, 0)] + [(sqkv, n) for n in range(4)]
@@ -1381,26 +1388,31 @@
     def dp_heads(k):
         return remote(hdp.at[q], hdp.at[q], hs.at[3 + k], hr.at[3 + k], (mod(q + k, 4), p))
 
-    hy_copy.wait_recv()
+    hy_copy.wait()
     hz[z] = heads[...] + hy[...]
     for k in (1, 2, 3):
         z_heads(k).start()
-    h_in.finish(0, inward)
-    od[...] = sd.z_sum(0)
+    sums_d[...] = sd.z_sum(0)
+    to_d = pltpu.make_async_copy(sums_d, od, kept.at[2])
+    to_d.start()
     for n in range(4):
         step(5 + n)
         cgu.step(n)
-        if n < 3:
-            h_in.finish(n + 1, inward)
+        if n == 3:
+            h_in.finish(0, inward)
     step(9)
     relay(9)
+    for n in (1, 2, 3):
+        h_in.finish(n, inward)
     for k in (1, 2, 3):
         f = mod(z + 4 - k, 4)
         remote(hz.at[f], hz.at[f], hs.at[k], hr.at[k], (q, p)).wait_recv()
     hdp[q] = hz[0] + hz[1] + hz[2] + hz[3]
     for k in (1, 2, 3):
         dp_heads(k).start()
-    oo[...] = so.z_sum(0)
+    sums_o[...] = so.z_sum(0)
+    to_o = pltpu.make_async_copy(sums_o, oo, kept.at[3])
+    to_o.start()
 
     @pl.loop(0, 4)
     def _(n):
@@ -1410,7 +1422,9 @@
     for k in (1, 2, 3):
         f = mod(q + 4 - k, 4)
         remote(hdp.at[f], hdp.at[f], hs.at[3 + k], hr.at[3 + k], (q, p)).wait_recv()
-    oheads[...] = hdp[0] + hdp[1] + hdp[2] + hdp[3]
+    heads[...] = hdp[0] + hdp[1] + hdp[2] + hdp[3]
+    to_h = pltpu.make_async_copy(heads, oheads, kept.at[4])
+    to_h.start()
     cqkv.close()
     h_out.close()
     h_in.close()
@@ -1418,7 +1432,8 @@
     sgu.close(4)
     so.close(1)
     sqkv.close(4)
-    hy_copy.wait_send()
+    for cp in (to_d, to_o, to_h):
+        cp.wait()
     for k in (1, 2, 3):
         z_heads(k).wait_send()
         dp_heads(k).wait_send()
@@ -1442,7 +1457,7 @@
             shape((8, 128), jnp.int32),
         ),
         in_specs=[ANY] * 5 + [VM] * 10,
-        out_specs=(ANY, ANY) + (VM,) * 5 + (ANY,),
+        out_specs=(ANY,) * 8,
         scratch_shapes=[
             vm((16, BLK, WIDTH), BF), vm((16, BLK, WIDTH), BF),
             vm((4, 8, 32, WIDTH), BF), vm((4, 8, 32, 1536), BF),
@@ -1457,12 +1472,12 @@
             vm((2, 1, 4, 64, WIDTH), BF), vm((2, 4, 4, 32, WIDTH), BF),
             vm((1, 4, 64, WIDTH), BF), vm((4, 4, 32, WIDTH), BF),
             vm((1, 4, 64, WIDTH), BF), vm((4, 4, 32, WIDTH), BF),
-            vm((8, 128), F32), vm((8, 128), F32), vm((4, 8, 128), F32), vm((4, 8, 128), F32),
+            vm((96, WIDTH), F32), vm((64, WIDTH), F32), vm((8, 128), F32), vm((8, 128), F32), vm((4, 8, 128), F32), vm((4, 8, 128), F32),
         ]
         + [vm((4, 128, WIDTH), BF)] * 7
         + [
             pltpu.SMEM((8, 128), jnp.int32), pltpu.SMEM((2, 16), jnp.int32), sem((1,)), pltpu.SemaphoreType.REGULAR, sem((12, 4)),
-            sem((10, 10)), sem((4, 4)), sem((7,)), sem((7,)), sem((12, 4)), sem((2,)),
+            sem((10, 10)), sem((4, 4)), sem((7,)), sem((7,)), sem((12, 4)), sem((2,)), sem((5,)),
         ]
         + [sem(n) for n in GATHER_SEMS],
         compiler_params=pltpu.CompilerParams(

time: 286 us -> 279 us (0.976)
  Pallas kernels: 281 us -> 271 us
    pallas_call x1, Pallas kernels: 277 us -> 268 us  [layer_call(): pl.pallas_call(layer_kernel, out_shape=(shape((2, 128, WIDTH), BF), shape...]
where the time goes in v6:
time: 279 us; the launch traced here: 274 us
  Pallas kernels  271 us (97%)
    pallas_call x1, Pallas kernels, layer_call(): pl.pallas_call(layer_kernel, out_shape=(shape((2, 128, WIDTH), BF), shape...  268 us

profile of v6, /device:TPU:27, one launch (start us, length us, event | category | flops | bytes accessed | tf_op | source)
XLA Modules:
  0.0 274.5 jit_solution(18052372371100460076)
XLA Ops:
  0.6 0.0 copy-start.1
  0.7 0.0 copy-start.2
  0.7 0.6 copy-done.1
  1.3 0.0 copy-done.2
  1.3 0.5 bitcast_convert_fusion
  1.8 0.0 copy-start
  1.8 0.7 copy-done
  2.5 0.6 pad.4.pos
  3.1 267.6 %layer_both_ways.1 = (bf16[2,128,1024]{2,1,0:T(8,128)(2,1)}, bf16[2,128,1024]{2,1,0:T(8,128)(2,1)}, f32[96,1024]{1,0:T(8,128)}, bf16[4,32,1536]{2,1,0:T(8,128)(2...) custom-call(bf16[2,2,64,1024]{3,2,1,0:T(8,128)(2,1)} %bitcast.14, ...), custom_call_target="tpu_custom_call" | custom-call | tf_op jit(solution)/shard_map/layer_both_ways/pallas_call | solution.py:1447
  270.8 3.6 %gains_and_layout.1 = (bf16[2,128,1024]{2,1,0:T(8,128)(2,1)}, bf16[2,128,1024]{2,1,0:T(8,128)(2,1)}, f32[1,32]{1,0:T(1,128)}, f32[32,2048]{1,0:T(8,128)}, f32[32...) custom-call(bf16[2,128,1024]{2,1,0:T(8,128)(2,1)} %get-tuple-element, ...), custom_call_target="tpu_custom_call" | custom-call | tf_op jit(solution)/shard_map/gains_and_layout/pallas_call | solution.py:1551
Async XLA Ops:
  0.6 0.7 copy-start.1
  0.7 0.7 copy-start.2
  1.8 0.7 copy-start

commit v7 on v6

--- a/solution.py
+++ b/solution.py
@@ -547,7 +547,7 @@
 
     def z_copy(self, piece, src, way):
         v = self.view(piece, 2 * src + self.y)
-        s = self.zs.at[piece, src + (4 if way < 0 else 0)]
+        s = self.zs.at[piece, src + (1 if way < 0 else 0)]
         return remote(v, v, s, self.zr.at[piece, src], (self.q, 2 * (self.z + way) + self.y))
 
     def y_copy(self, piece, src):
@@ -575,7 +575,7 @@
 
     def line_copy(self, line, src, way):
         v = self.view(LINES, 2 * src + line)
-        s = self.ls.at[line, src + (4 if way < 0 else 0)]
+        s = self.ls.at[line, src + (1 if way < 0 else 0)]
         return remote(v, v, s, self.lr.at[line, src], (self.q, 2 * (self.z + way) + self.y))
 
     def line_spread(self, line, src, up, down):
@@ -770,7 +770,7 @@
         self.token_close(1)
 
 
-GATHER_SEMS = ((7,), (2, 2), (2, 8), (2, 2, 8), (2, 8), (3,), (1,), (2, 3), (2, 3), (7, 8), (7, 4), (7, 4), (7, 4), (2, 8), (2, 4))
+GATHER_SEMS = ((7,), (2, 2), (2, 8), (2, 2, 8), (2, 8), (3,), (1,), (2, 3), (2, 3), (6, 5), (6, 4), (7, 4), (7, 4), (2, 5), (2, 4))
 
 
 class Home:
@@ -1062,11 +1062,11 @@
     g.token_start(1)
     g.step(0, 3)
     g.token_pass(0, 4, 8)
-    g.own_copy(2).wait()
-    g.begin(1)
     g.own_copy(1).wait()
     g.column_wait(1)
-    g.begin(2, 3)
+    g.begin(2)
+    g.own_copy(2).wait()
+    g.begin(1, 3)
     g.own_copy(3).wait()
     sort.wait()
     slot = mod(z, 2)
@@ -1311,6 +1311,8 @@
                 @pl.when(g == 1)
                 def _():
                     step(1)
+                    h_out.finish(0, result)
+                    h_out.finish(1, result)
             else:
                 for turn in range(2):
 
@@ -1318,8 +1320,8 @@
                     def _():
                         step(2 * turn)
                         if turn == 1:
-                            h_out.finish(0, result)
-                            h_out.finish(1, result)
+                            h_out.finish(2, result)
+                            h_out.finish(3, result)
 
             h = g * 2 + t
             lanes = pl.ds(pl.multiple_of(h * 128, 128), 128)
@@ -1349,8 +1351,6 @@
         cf[:, :, pl.ds(pl.multiple_of(768 + g * 128, 128), 128)] = dkv[1].astype(BF).reshape(16, BLK, 128)
 
     step(3)
-    h_out.finish(2, result)
-    h_out.finish(3, result)
     hy_copy = remote(heads, hy, hs.at[0], hr.at[0], (q, 2 * z + 1 - y))
     hy_copy.start()
 

time: 279 us -> 279 us (level)
  no operation moved by 1% of the time
where the time goes in v7:
time: 279 us; the launch traced here: 274 us
  Pallas kernels  271 us (97%)
    pallas_call x1, Pallas kernels, layer_call(): pl.pallas_call(layer_kernel, out_shape=(shape((2, 128, WIDTH), BF), shape...  267 us

profile of v7, /device:TPU:27, one launch (start us, length us, event | category | flops | bytes accessed | tf_op | source)
XLA Modules:
  0.0 274.2 jit_solution(13980006481602877152)
XLA Ops:
  0.6 0.0 copy-start.1
  0.7 0.0 copy-start.2
  0.7 0.6 copy-done.1
  1.3 0.0 copy-done.2
  1.3 0.5 bitcast_convert_fusion
  1.8 0.0 copy-start
  1.8 0.7 copy-done
  2.5 0.6 pad.4.pos
  3.1 267.4 %layer_both_ways.1 = (bf16[2,128,1024]{2,1,0:T(8,128)(2,1)}, bf16[2,128,1024]{2,1,0:T(8,128)(2,1)}, f32[96,1024]{1,0:T(8,128)}, bf16[4,32,1536]{2,1,0:T(8,128)(2...) custom-call(bf16[2,2,64,1024]{3,2,1,0:T(8,128)(2,1)} %bitcast.14, ...), custom_call_target="tpu_custom_call" | custom-call | tf_op jit(solution)/shard_map/layer_both_ways/pallas_call | solution.py:1447
  270.5 3.6 %gains_and_layout.1 = (bf16[2,128,1024]{2,1,0:T(8,128)(2,1)}, bf16[2,128,1024]{2,1,0:T(8,128)(2,1)}, f32[1,32]{1,0:T(1,128)}, f32[32,2048]{1,0:T(8,128)}, f32[32...) custom-call(bf16[2,128,1024]{2,1,0:T(8,128)(2,1)} %get-tuple-element, ...), custom_call_target="tpu_custom_call" | custom-call | tf_op jit(solution)/shard_map/gains_and_layout/pallas_call | solution.py:1551
Async XLA Ops:
  0.6 0.7 copy-start.1
  0.7 0.7 copy-start.2
  1.8 0.7 copy-start
